TPU v7x, 32 devices: a whole 2x2x4 slice. The times are simulated.
32 devices in a mesh: pat: 4 (over x, core), slab: 8 (over z, y).
Axes of the slice: x: 2, y: 2, z: 4, core: 2. Of those that a mesh axis runs over, the one named last changes fastest.
Arguments:
- features: bfloat16 [4, 64, 48, 384], P('pat', None, 'slab'), may hold values from -50 to 50
- cotangent: bfloat16 [4, 64, 48, 384], P('pat', None, 'slab'), may hold values from -50 to 50
- weights: float32 [2, 64, 1728], replicated, may hold values from -0.15625 to 0.15625
- prev_state: float32 [2, 64, 1728], replicated, may hold values from -6 to 6
- tree_noise: float32 [2, 64, 1728], replicated, may hold values from -6 to 6
Outputs:
- state_next: float32 [2, 64, 1728], replicated
- weights_next: float32 [2, 64, 1728], replicated
All inputs are finite; a program needn't handle non-finite values.
Results may differ from a plain program's by a relative error of at most 0.006.
Values may be sent and summed in bfloat16 or wider, within the bound.
No kernel may reach another device: no remote copies, remote signals or barrier semaphores. Data moves between devices by JAX's collectives and lax.ppermute only.
A program may use at most 64 MiB of HBM per device.

v0:
```python
import jax
import jax.numpy as jnp
from jax import lax
from jax.sharding import PartitionSpec as P

W = 24


eps_norm = 1e-05
clip_bound = 400.0
step_rate = 0.1


def padded_2(shard, sides, width):
    for axis, dim in sides:
        peers, length = (lax.axis_size(axis), shard.shape[dim])
        up = [(i, (i + 1) % peers) for i in range(peers - 1)]
        down = [(j, i) for i, j in up]
        last = lax.slice_in_dim(shard, length - width, length, axis=dim)
        initial = lax.slice_in_dim(shard, 0, width, axis=dim)
        before = lax.ppermute(last, axis, up)
        after = lax.ppermute(initial, axis, down)
        shard = jnp.concatenate([before, shard, after], axis=dim)
    return shard


def depth_rims(volume, width):
    return padded_2(volume, (("slab", 1),), width)


def slab_totals(first, second):
    return lax.psum((first, second), "slab")


def plane_taps(volume):
    plane_size = volume.shape[2]
    padded = jnp.pad(volume, ((0, 0), (0, 0), (W + 1, W + 1)))
    column = lax.broadcasted_iota(jnp.int32, (1, 1, plane_size), 2) % W
    pieces = []
    for row_step in (-1, 0, 1):
        for col_step in (-1, 0, 1):
            offset = W + 1 + row_step * W + col_step
            shifted = padded[:, :, offset : offset + plane_size]
            if col_step != 0:
                inside = (column + col_step >= 0) & (column + col_step < W)
                shifted = jnp.where(inside, shifted, jnp.zeros_like(shifted))
            pieces.append(shifted)
    return jnp.concatenate(pieces, axis=0)


def convolve(padded_field, kernel):
    channels = kernel.shape[0]
    planes = padded_field.shape[1] - 2
    summed = None
    for depth_step in range(3):
        stacked = plane_taps(padded_field[:, depth_step : depth_step + planes, :])
        block_cols = kernel[:, depth_step * 9 * channels : (depth_step + 1) * 9 * channels]
        partial_value = jnp.einsum(
            "oi,izp->ozp", block_cols, stacked, preferred_element_type=jnp.float32
        )
        summed = partial_value if summed is None else summed + partial_value
    return summed


def kernel_grad(padded_field, upstream):
    planes = upstream.shape[1]
    blocks = []
    for depth_step in range(3):
        stacked = plane_taps(padded_field[:, depth_step : depth_step + planes, :])
        blocks.append(
            jnp.einsum("ozp,izp->oi", upstream, stacked, preferred_element_type=jnp.float32)
        )
    return jnp.concatenate(blocks, axis=1)


def flipped(kernel):
    channels = kernel.shape[0]
    return jnp.flip(kernel.reshape(channels, 27, channels).transpose(2, 1, 0), axis=1).reshape(
        channels, 27 * channels
    )


def statistics(summed, cell_count):
    totals, squares = slab_totals(
        jnp.sum(summed, axis=(1, 2)), jnp.sum(summed * summed, axis=(1, 2))
    )
    centre = totals / cell_count
    spread = lax.rsqrt(squares / cell_count - centre * centre + eps_norm)
    return (centre[:, None, None], spread[:, None, None])


def norm_back(gradient, normed, spread, cell_count):
    totals, crossed = slab_totals(
        jnp.sum(gradient, axis=(1, 2)), jnp.sum(gradient * normed, axis=(1, 2))
    )
    return spread * (
        gradient
        - (totals / cell_count)[:, None, None]
        - normed * (crossed / cell_count)[:, None, None]
    )


def silu_slope(values):
    sigmoid_val = jax.nn.sigmoid(values)
    return sigmoid_val * (1.0 + values * (1.0 - sigmoid_val))


def per_device(features, cotangent, weights, prev_state, tree_noise):
    kernels = weights.astype(jnp.bfloat16)
    conv_one = kernels[0]
    conv_two = kernels[1]
    volume = features[0]
    upstream = cotangent[0]
    planes = volume.shape[1]
    cell_count = lax.axis_size("slab") * planes * volume.shape[2]
    input_rims = depth_rims(volume, 1)
    first = convolve(input_rims, conv_one)
    centre_one, spread_one = statistics(first, cell_count)
    normed_one = (first - centre_one) * spread_one
    hidden = jax.nn.silu(normed_one).astype(jnp.bfloat16)
    hidden_rims = depth_rims(hidden, 1)
    second = convolve(hidden_rims, conv_two)
    centre_two, spread_two = statistics(second, cell_count)
    normed_two = (second - centre_two) * spread_two
    gradient_two = upstream.astype(jnp.float32) * silu_slope(normed_two)
    cotan_two = norm_back(gradient_two, normed_two, spread_two, cell_count).astype(jnp.bfloat16)
    kgrad_two = kernel_grad(hidden_rims, cotan_two)
    back_hidden = convolve(depth_rims(cotan_two, 1), flipped(conv_two))
    gradient_one = back_hidden * silu_slope(normed_one)
    cotan_one = norm_back(gradient_one, normed_one, spread_one, cell_count).astype(jnp.bfloat16)
    kgrad_one = kernel_grad(input_rims, cotan_one)
    sum_one, sum_two = lax.psum((kgrad_one, kgrad_two), "slab")
    squared = jnp.sum(sum_one * sum_one) + jnp.sum(sum_two * sum_two)
    factor = clip_bound / jnp.maximum(jnp.sqrt(squared), clip_bound)
    total_one, total_two = lax.psum((factor * sum_one, factor * sum_two), "pat")
    combined = jnp.stack([total_one, total_two])
    state_next = prev_state + combined
    weights_next = weights - step_rate * (combined + tree_noise)
    return (state_next, weights_next)


def solution(mesh):
    return jax.shard_map(
        per_device,
        mesh=mesh,
        in_specs=(P("pat", None, "slab", None), P("pat", None, "slab", None), P(), P(), P()),
        out_specs=(P(), P()),
        check_vma=False,
    )
```

profile of v0, /device:TPU:0, one launch (start us, length us, event | category | flops | bytes accessed | tf_op | source)
XLA Modules:
  0.0 285.9 jit_solution(14837690863451738196)
XLA Ops:
  7.2 0.9 fusion.162
  8.1 1.3 collective-permute-start.1
  9.4 5.5 %collective-permute-start = (bf16[64,1,384]{2,0,1:T(8,128)(2,1)S(1)}, bf16[64,1,384]{2,0,1:T(8,128)(2,1)S(1)}, u32[]{:S(2)}, u32[]{:S(2)}) collective-permute-start(bf16[64,1,384]{2,0,1:T(8,128)(2,1)S(1)} %get-tuple-element.42), channel_id=1, source_target_pairs={{0,1},{1,2},{2,3},{3,4},{4,5},{5,6},{6,7},{8,9},{9,10},{10,11},{11... | collective-permute-start | bytes 147464 | tf_op jit(solution)/shard_map/ppermute | solution.py:21
  14.9 1.2 convert_element_type.34
  16.3 0.9 fusion.36
  17.1 0.9 fusion.37
  18.0 0.5 reshape_squeeze.3
  18.5 0.5 rev.4
  19.0 1.1 copy.8
  20.1 1.1 reshape.49
  21.2 0.9 pad_maximum_fusion.4
  23.1 0.3 fusion.57
  23.4 0.5 copy-done.5
  23.9 0.5 fusion.59
  24.6 0.5 fusion.62
  25.1 0.3 fusion.45
  26.1 0.5 fusion.149
  26.6 1.0 copy-done.6
  27.6 0.6 convolution_add_fusion.5
  28.2 1.5 fusion.158
  29.7 20.3 %all-reduce.12 = (f32[64]{0:T(128)S(1)}, f32[64]{0:T(128)S(1)}) all-reduce(f32[64]{0:T(128)S(1)} %get-tuple-element.9, f32[64]{0:T(128)S(1)} %get-tuple-element.8), channel_id=1, replica_groups=mesh['pat'=4,'slab'=8] {'slab'}, use_global_device_ids=true, to_apply=%region_1.2 | all-reduce | flops 128 | bytes 1024 | tf_op jit(solution)/shard_map/psum | solution.py:32
  50.3 1.3 collective-permute-start.3
  51.6 4.7 %collective-permute-start.2 = (bf16[64,1,384]{2,0,1:T(8,128)(2,1)S(1)}, bf16[64,1,384]{2,0,1:T(8,128)(2,1)S(1)}, u32[]{:S(2)}, u32[]{:S(2)}) collective-permute-start(bf16[64,1,384]{2,0,1:T(8,128)(2,1)S(1)} %get-tuple-element.37), channel_id=1, source_target_pairs={{0,1},{1,2},{2,3},{3,4},{4,5},{5,6},{6,7},{8,9},{9,10},{10,11},{11... | collective-permute-start | bytes 147464 | tf_op jit(solution)/shard_map/ppermute | solution.py:21
  56.5 1.4 collective-permute-done.2
  59.6 0.5 fusion.104
  60.7 0.3 fusion.87
  62.1 0.5 fusion.147
  62.7 0.6 convolution_add_fusion.3
  63.2 0.7 copy-done.1
  63.9 1.5 fusion.157
  65.4 19.5 %all-reduce.11 = (f32[64]{0:T(128)S(1)}, f32[64]{0:T(128)S(1)}) all-reduce(f32[64]{0:T(128)S(1)} %get-tuple-element.7, f32[64]{0:T(128)S(1)} %get-tuple-element.6), channel_id=1, replica_groups=mesh['pat'=4,'slab'=8] {'slab'}, use_global_device_ids=true, to_apply=%region_5.6 | all-reduce | flops 128 | bytes 1024 | tf_op jit(solution)/shard_map/psum | solution.py:32
  84.9 2.4 fusion.156
  87.3 17.1 %all-reduce.10 = (f32[64]{0:T(128)S(1)}, f32[64]{0:T(128)S(1)}) all-reduce(f32[64]{0:T(128)S(1)} %get-tuple-element.5, f32[64]{0:T(128)S(1)} %get-tuple-element.4), channel_id=1, replica_groups=mesh['pat'=4,'slab'=8] {'slab'}, use_global_device_ids=true, to_apply=%region_11.12 | all-reduce | flops 128 | bytes 1024 | tf_op jit(solution)/shard_map/psum | solution.py:32
  104.5 1.7 fusion.10
  106.2 3.5 %convolution_bitcast_fusion = f32[64,576]{1,0:T(8,128)} fusion(bf16[64,6,384]{2,0,1:T(8,128)(2,1)S(1)} %fusion.10, bf16[576,6,384]{2,0,1:T(8,128)(2,1)} %copy-done.9), kind=kOutput, calls=%fused_computation.8 | convolution fusion | flops 169869312 | bytes 3096576 | tf_op jit(solution)/shard_map/ozp,izp->oi/dot_general | solution.py:71
  109.7 1.6 convolution_bitcast_fusion.1
  111.3 1.6 convolution_bitcast_fusion.2
  112.9 0.6 fusion.160
  113.5 1.3 collective-permute-start.5
  114.8 5.2 %collective-permute-start.4 = (bf16[64,1,384]{2,0,1:T(8,128)(2,1)}, bf16[64,1,384]{2,0,1:T(8,128)(2,1)}, u32[]{:S(2)}, u32[]{:S(2)}) collective-permute-start(bf16[64,1,384]{2,0,1:T(8,128)(2,1)} %get-tuple-element.32), channel_id=1, source_target_pairs={{0,1},{1,2},{2,3},{3,4},{4,5},{5,6},{6,7},{8,9},{9,10},{10,11},{11... | collective-permute-start | bytes 147464 | tf_op jit(solution)/shard_map/ppermute | solution.py:21
  120.0 0.9 fusion.120
  120.9 2.0 concatenate.76
  122.8 1.7 pad_maximum_fusion
  126.1 0.4 copy-done.11
  126.5 0.5 fusion.146
  127.4 0.3 fusion.129
  128.7 0.5 fusion.148
  129.3 0.6 convolution_add_fusion.1
  129.8 1.5 fusion.155
  131.4 19.6 %all-reduce.9 = (f32[64]{0:T(128)S(1)}, f32[64]{0:T(128)S(1)}) all-reduce(f32[64]{0:T(128)S(1)} %get-tuple-element.3, f32[64]{0:T(128)S(1)} %get-tuple-element.2), channel_id=1, replica_groups=mesh['pat'=4,'slab'=8] {'slab'}, use_global_device_ids=true, to_apply=%region_15.16 | all-reduce | flops 128 | bytes 1024 | tf_op jit(solution)/shard_map/psum | solution.py:32
  151.0 1.5 fusion.20
  152.5 2.6 convolution_bitcast_fusion.3
  155.2 0.9 convolution_bitcast_fusion.4
  156.1 0.9 convolution_bitcast_fusion.5
  157.0 0.9 concatenate.75
  158.0 73.9 %all-reduce.18.cloned.1.call-done = (f32[64,1728]{1,0:T(8,128)}, f32[64,1728]{1,0:T(8,128)}) async-done(((f32[64,1728]{1,0:T(8,128)}, f32[64,1728]{1,0:T(8,128)}), (f32[64,1728]{1,0:T(8,128)}, f32[64,1728]{1,0:T(8,128)})) %all-reduce.18.cloned.1.call-update) | async-done | bytes 884752 | tf_op jit(solution)/shard_map/psum | solution.py:132
  231.9 1.9 multiply_reduce_fusion.2
  233.8 1.7 multiply_reduce_fusion.3
  236.9 1.8 multiply_bitcast_fusion
  238.7 1.8 multiply_bitcast_fusion.1
  240.6 34.8 %all-reduce.20.cloned.1.call-done = (f32[1,64,1728]{2,1,0:T(8,128)}, f32[1,64,1728]{2,1,0:T(8,128)}) async-done(((f32[1,64,1728]{2,1,0:T(8,128)}, f32[1,64,1728]{2,1,0:T(8,128)}), (f32[1,64,1728]{2,1,0:T(8,128)}, f32[1,64,1728]{2,1,0:T(8,128)})) %all-reduce.20.cloned.1.call-update) | async-done | bytes 884752 | tf_op jit(solution)/shard_map/psum | solution.py:135
  275.4 1.0 constant_dynamic-update-slice_fusion.10
  276.5 1.1 constant_dynamic-update-slice_fusion.9
  277.6 1.5 multiply_subtract_fusion
  (101 shorter events, 8.7 us)
Async XLA Ops:
  7.2 9.1 %copy-start = (bf16[1,64,6,384]{3,1,2,0:T(8,128)(2,1)S(1)}, bf16[1,64,6,384]{3,1,2,0:T(8,128)(2,1)}, u32[]{:S(2)}) copy-start(bf16[1,64,6,384]{3,1,2,0:T(8,128)(2,1)} %param.5) | copy-start | bytes 884740
  7.2 224.7 %all-reduce.18.cloned.1.call-start = ((), (), s32[]{:S(2)}) async-start(), calls=%async_computation | async-start | bytes 1835008 | tf_op jit(solution)/shard_map/psum | solution.py:132
  8.1 13.1 %collective-permute-start.1 = (bf16[64,1,384]{2,0,1:T(8,128)(2,1)S(1)}, bf16[64,1,384]{2,0,1:T(8,128)(2,1)S(1)}, u32[]{:S(2)}, u32[]{:S(2)}) collective-permute-start(bf16[64,1,384]{2,0,1:T(8,128)(2,1)S(1)} %get-tuple-element.41), channel_id=1, source_target_pairs={{1,0},{2,1},{3,2},{4,3},{5,4},{6,5},{7,6},{9,8},{10,9},{11,10},{12... | collective-permute-start | bytes 147464 | tf_op jit(solution)/shard_map/ppermute | solution.py:22
  9.4 11.8 %collective-permute-start = (bf16[64,1,384]{2,0,1:T(8,128)(2,1)S(1)}, bf16[64,1,384]{2,0,1:T(8,128)(2,1)S(1)}, u32[]{:S(2)}, u32[]{:S(2)}) collective-permute-start(bf16[64,1,384]{2,0,1:T(8,128)(2,1)S(1)} %get-tuple-element.42), channel_id=1, source_target_pairs={{0,1},{1,2},{2,3},{3,4},{4,5},{5,6},{6,7},{8,9},{9,10},{10,11},{11... | collective-permute-start | bytes 147464 | tf_op jit(solution)/shard_map/ppermute | solution.py:21
  16.2 10.4 %copy-start.12 = (bf16[64,1728]{1,0:T(8,128)(2,1)}, bf16[64,1728]{1,0:T(8,128)(2,1)S(1)}, u32[]{:S(2)}) copy-start(bf16[64,1728]{1,0:T(8,128)(2,1)S(1)} %get-tuple-element.27) | copy-start | bytes 663556
  22.1 1.7 copy-start.5
  25.1 3.1 %copy-start.8 = (bf16[576,6,384]{2,0,1:T(8,128)(2,1)}, bf16[576,6,384]{2,0,1:T(8,128)(2,1)S(1)}, u32[]{:S(2)}) copy-start(bf16[576,6,384]{2,0,1:T(8,128)(2,1)S(1)} %get-tuple-element.65) | copy-start | bytes 7962628
  26.1 1.5 copy-start.6
  50.3 6.2 %collective-permute-start.3 = (bf16[64,1,384]{2,0,1:T(8,128)(2,1)S(1)}, bf16[64,1,384]{2,0,1:T(8,128)(2,1)S(1)}, u32[]{:S(2)}, u32[]{:S(2)}) collective-permute-start(bf16[64,1,384]{2,0,1:T(8,128)(2,1)S(1)} %get-tuple-element.36), channel_id=1, source_target_pairs={{1,0},{2,1},{3,2},{4,3},{5,4},{6,5},{7,6},{9,8},{10,9},{11,10},{12... | collective-permute-start | bytes 147464 | tf_op jit(solution)/shard_map/ppermute | solution.py:22
  51.6 6.3 %collective-permute-start.2 = (bf16[64,1,384]{2,0,1:T(8,128)(2,1)S(1)}, bf16[64,1,384]{2,0,1:T(8,128)(2,1)S(1)}, u32[]{:S(2)}, u32[]{:S(2)}) collective-permute-start(bf16[64,1,384]{2,0,1:T(8,128)(2,1)S(1)} %get-tuple-element.37), channel_id=1, source_target_pairs={{0,1},{1,2},{2,3},{3,4},{4,5},{5,6},{6,7},{8,9},{9,10},{10,11},{11... | collective-permute-start | bytes 147464 | tf_op jit(solution)/shard_map/ppermute | solution.py:21
  60.1 3.9 %copy-start.9 = (bf16[576,6,384]{2,0,1:T(8,128)(2,1)}, bf16[576,6,384]{2,0,1:T(8,128)(2,1)S(1)}, u32[]{:S(2)}) copy-start(bf16[576,6,384]{2,0,1:T(8,128)(2,1)S(1)} %get-tuple-element.54) | copy-start | bytes 7962628
  61.6 1.6 copy-start.3
  62.1 1.8 copy-start.1
  84.9 19.6 %copy-start.16 = (f32[64]{0:T(128)}, f32[64]{0:T(128)S(1)}, u32[]{:S(2)}) copy-start(f32[64]{0:T(128)S(1)} %get-tuple-element.53) | copy-start | bytes 772
  84.9 19.6 %copy-start.17 = (f32[64]{0:T(128)}, f32[64]{0:T(128)S(1)}, u32[]{:S(2)}) copy-start(f32[64]{0:T(128)S(1)} %get-tuple-element.52) | copy-start | bytes 772
  104.5 5.2 %copy-start.4 = (bf16[576,6,384]{2,0,1:T(8,128)(2,1)S(1)}, bf16[576,6,384]{2,0,1:T(8,128)(2,1)}, u32[]{:S(2)}) copy-start(bf16[576,6,384]{2,0,1:T(8,128)(2,1)} %copy-done.3) | copy-start | bytes 7962628
  106.2 5.1 %copy-start.2 = (bf16[576,6,384]{2,0,1:T(8,128)(2,1)S(1)}, bf16[576,6,384]{2,0,1:T(8,128)(2,1)}, u32[]{:S(2)}) copy-start(bf16[576,6,384]{2,0,1:T(8,128)(2,1)} %copy-done.1) | copy-start | bytes 7962628
  113.5 9.3 %collective-permute-start.5 = (bf16[64,1,384]{2,0,1:T(8,128)(2,1)}, bf16[64,1,384]{2,0,1:T(8,128)(2,1)}, u32[]{:S(2)}, u32[]{:S(2)}) collective-permute-start(bf16[64,1,384]{2,0,1:T(8,128)(2,1)} %get-tuple-element.31), channel_id=1, source_target_pairs={{1,0},{2,1},{3,2},{4,3},{5,4},{6,5},{7,6},{9,8},{10,9},{11,10},{12... | collective-permute-start | bytes 147464 | tf_op jit(solution)/shard_map/ppermute | solution.py:22
  114.8 8.0 %collective-permute-start.4 = (bf16[64,1,384]{2,0,1:T(8,128)(2,1)}, bf16[64,1,384]{2,0,1:T(8,128)(2,1)}, u32[]{:S(2)}, u32[]{:S(2)}) collective-permute-start(bf16[64,1,384]{2,0,1:T(8,128)(2,1)} %get-tuple-element.32), channel_id=1, source_target_pairs={{0,1},{1,2},{2,3},{3,4},{4,5},{5,6},{6,7},{8,9},{9,10},{10,11},{11... | collective-permute-start | bytes 147464 | tf_op jit(solution)/shard_map/ppermute | solution.py:21
  124.7 1.8 copy-start.11
  127.3 1.4 copy-start.15
  151.0 4.2 %copy-start.7 = (bf16[576,6,384]{2,0,1:T(8,128)(2,1)S(1)}, bf16[576,6,384]{2,0,1:T(8,128)(2,1)}, u32[]{:S(2)}) copy-start(bf16[576,6,384]{2,0,1:T(8,128)(2,1)} %copy-done.6) | copy-start | bytes 7962628
  157.9 117.5 %all-reduce.20.cloned.1.call-start = ((), (), s32[]{:S(2)}) async-start(), calls=%async_computation.1 | async-start | bytes 1835008 | tf_op jit(solution)/shard_map/psum | solution.py:135
  231.9 45.6 %copy-start.10 = (f32[2,64,1728]{2,1,0:T(8,128)S(1)}, f32[2,64,1728]{2,1,0:T(8,128)}, u32[]{:S(2)}) copy-start(f32[2,64,1728]{2,1,0:T(8,128)} %param.7) | copy-start | bytes 2654212
  231.9 45.6 %copy-start.13 = (f32[2,64,1728]{2,1,0:T(8,128)S(1)}, f32[2,64,1728]{2,1,0:T(8,128)}, u32[]{:S(2)}) copy-start(f32[2,64,1728]{2,1,0:T(8,128)} %param.9) | copy-start | bytes 2654212
  231.9 45.6 %copy-start.14 = (f32[2,64,1728]{2,1,0:T(8,128)S(1)}, f32[2,64,1728]{2,1,0:T(8,128)}, u32[]{:S(2)}) copy-start(f32[2,64,1728]{2,1,0:T(8,128)} %param.8) | copy-start | bytes 2654212
Sparse Core Ops, SparseCore 0:
  158.1 73.8 all-reduce.17
  240.7 34.6 all-reduce.19
where the time goes:
time: 287 us; the launch traced here: 286 us
  waiting for transfers between devices  110 us (38%)
  blocking collectives  76.5 us (27%)
  other arithmetic  28.8 us (10%)
  starting transfers between devices  19.4 us (7%)
  matrix products  18.9 us (7%)
  between operations  16.2 us (6%)
  local copies, waits for them, and re-layouts  15.9 us (6%)
    psum x4, blocking collectives, slab_totals(): return lax.psum((first, second), 'slab')  76.5 us
    psum x1, waiting for transfers between devices, per_device(): sum_one, sum_two = lax.psum((kgrad_one, kgrad_two), 'slab')  73.9 us
    psum x1, waiting for transfers between devices, per_device(): total_one, total_two = lax.psum((factor * sum_one, factor * sum_two), 'pat')  34.8 us
    ppermute x3, starting transfers between devices, padded_2(): before = lax.ppermute(last, axis, up)  15.4 us
    dot_general x6, matrix products, kernel_grad(): jnp.einsum('ozp,izp->oi', upstream, stacked, preferred_element_type=jnp.f...  11.1 us
    dot_general x9, matrix products, convolve(): jnp.einsum('oi,izp->ozp', block_cols, stacked, preferred_element_type=jnp...  7.79 us
    unnamed x28, other arithmetic  7.35 us
    unnamed x60, local copies, waits for them, and re-layouts  7.31 us
  transfers between devices with their start and end apart: 8, of which 3 were waited for; matrix products, arithmetic and copies ran while one was open for 3% of the time, Pallas kernels for 0%

commit v1 on v0

v1 whole, which is shorter than its diff:
```python
import functools

import jax
import jax.numpy as jnp
from jax import lax
from jax.experimental import pallas as pl
from jax.experimental.pallas import tpu as pltpu
from jax.sharding import PartitionSpec as P

W = 24

eps_norm = 1e-05
clip_bound = 400.0
step_rate = 0.1

f32 = jnp.float32
bf16 = jnp.bfloat16

AXES = ("pat", "slab")
PAD = 128
FEATURE_HALO = 3
COTAN_HALO = 1


def call(kernel, out_shape, *args, scratch=(), flops=0):
    vmem = pl.BlockSpec(memory_space=pltpu.VMEM)
    outs = out_shape if isinstance(out_shape, (tuple, list)) else (out_shape,)
    size = sum(a.size * a.dtype.itemsize for a in args)
    return pl.pallas_call(
        kernel,
        out_shape=out_shape,
        in_specs=[vmem] * len(args),
        out_specs=jax.tree.map(lambda _: vmem, out_shape),
        scratch_shapes=list(scratch),
        cost_estimate=pl.CostEstimate(flops=flops, bytes_accessed=size, transcendentals=0),
        compiler_params=pltpu.CompilerParams(vmem_limit_bytes=40 * 2**20),
    )(*args)


def sds(shape, dtype):
    return jax.ShapeDtypeStruct(shape, dtype)


def column_masks(cells):
    column = lax.broadcasted_iota(jnp.int32, (1, cells), 1) % W
    return (column != W - 1).astype(bf16), (column != 0).astype(bf16)


def patches(planes, edge, stack):
    channels, cells = planes[0].shape
    not_last, not_first = column_masks(cells)
    edge[...] = jnp.zeros_like(edge)
    for z, plane in enumerate(planes):
        edge[0:channels, PAD + 1 : PAD + 1 + cells] = plane * not_last
        edge[channels : 2 * channels, PAD : PAD + cells] = plane
        edge[2 * channels : 3 * channels, PAD - 1 : PAD - 1 + cells] = plane * not_first
        for b in range(3):
            start = PAD + (b - 1) * W
            stack[b * 3 * channels : (b + 1) * 3 * channels, z * cells : (z + 1) * cells] = edge[
                :, start : start + cells
            ]


def tap_products(kernel, stack, product, planes, cells):
    for z in range(0, planes, 2):
        span = slice(z * cells, min(z + 2, planes) * cells)
        product[:, span] = jnp.dot(kernel[...], stack[:, span], preferred_element_type=f32)


def depth_sum(product, z, channels, cells):
    return (
        product[0:channels, z * cells : (z + 1) * cells]
        + product[channels : 2 * channels, (z + 1) * cells : (z + 2) * cells]
        + product[2 * channels : 3 * channels, (z + 2) * cells : (z + 3) * cells]
    )


def eye(size):
    return lax.broadcasted_iota(jnp.int32, (size, size), 0) == lax.broadcasted_iota(
        jnp.int32, (size, size), 1
    )


def to_row(first, second):
    both = jnp.concatenate([first, second], axis=0)
    size = both.shape[0]
    return jnp.sum(jnp.where(eye(size), both, 0.0), axis=0, keepdims=True)


def to_columns(rows):
    row = jnp.sum(rows, axis=0, keepdims=True)
    size = row.shape[1]
    both = jnp.sum(jnp.where(eye(size), row, 0.0), axis=1, keepdims=True)
    return both[: size // 2], both[size // 2 :]


def moments(rows, cell_count):
    totals, squares = to_columns(rows)
    centre = totals / cell_count
    return centre, lax.rsqrt(squares / cell_count - centre * centre + eps_norm)


def sigmoid(values):
    return 1.0 / (1.0 + jnp.exp(-values))


def slope(values):
    gate = sigmoid(values)
    return gate * (1.0 + values * (1.0 - gate))


def add_to(total, value):
    return value if total is None else total + value


def send_totals(ref, first, second):
    row = to_row(
        jnp.sum(first, axis=1, keepdims=True), jnp.sum(second, axis=1, keepdims=True)
    )
    ref[...] = jnp.broadcast_to(row, ref.shape)


def inside(z, halo, depth, slab, peers, value):
    if z < halo:
        return jnp.where(slab > 0, value, jnp.zeros_like(value))
    if z >= halo + depth:
        return jnp.where(slab < peers - 1, value, jnp.zeros_like(value))
    return value


def kernel_stacks(weights, one, two, back):
    channels = weights.shape[1]
    width = 9 * channels
    for k, target in ((0, one), (1, two)):
        rounded = weights[k].astype(bf16)
        for a in range(3):
            target[a * channels : (a + 1) * channels, :] = rounded[:, a * width : (a + 1) * width]
    turned = weights[1].T
    for a in range(3):
        for tap in range(9):
            block = (2 - a) * 9 + 8 - tap
            back[
                a * channels : (a + 1) * channels, tap * channels : (tap + 1) * channels
            ] = turned[block * channels : (block + 1) * channels, :].astype(bf16)


def field_halo(own, even_recv, odd_recv, start, count, slab, peers):
    even = slab % 2 == 0
    zero = jnp.zeros(own.shape[1:], own.dtype)
    before, after = [], []
    for z in range(start, start + count):
        x, y = even_recv[z], odd_recv[z]
        before.append(jnp.where(slab == 0, zero, jnp.where(even, y, x)))
        after.append(jnp.where(slab == peers - 1, zero, jnp.where(even, x, y)))
    return before + [own[z] for z in range(own.shape[0])] + after


def first_conv(peers, own, even_recv, odd_recv, kernel, first, totals, edge, stack, product):
    slab = lax.axis_index("slab")
    depth, channels, cells = own.shape
    planes = field_halo(own, even_recv, odd_recv, 0, FEATURE_HALO, slab, peers)
    patches(planes, edge, stack)
    tap_products(kernel, stack, product, len(planes), cells)
    s = q = None
    for z in range(depth + 4):
        value = depth_sum(product, z, channels, cells)
        first[z] = value
        if 2 <= z < depth + 2:
            s, q = add_to(s, value), add_to(q, value * value)
    send_totals(totals, s, q)


def second_conv(peers, cell_count, rows, first, kernel, hidden, second, totals, edge, stack, product):
    slab = lax.axis_index("slab")
    extended, channels, cells = first.shape
    depth = extended - 4
    centre, spread = moments(rows[...], cell_count)
    planes = []
    for z in range(extended):
        normed = (first[z] - centre) * spread
        value = inside(z, 2, depth, slab, peers, (normed * sigmoid(normed)).astype(bf16))
        planes.append(value)
        if 1 <= z < extended - 1:
            hidden[z - 1] = value
    patches(planes, edge, stack)
    tap_products(kernel, stack, product, extended, cells)
    s = q = None
    for z in range(depth + 2):
        value = depth_sum(product, z, channels, cells)
        second[z] = value
        if 1 <= z < depth + 1:
            s, q = add_to(s, value), add_to(q, value * value)
    send_totals(totals, s, q)


def second_gradient(peers, cell_count, rows, second, cotan, even_recv, odd_recv, gradient, totals):
    slab = lax.axis_index("slab")
    depth = cotan.shape[0]
    upstream = field_halo(cotan, even_recv, odd_recv, FEATURE_HALO, COTAN_HALO, slab, peers)
    centre, spread = moments(rows[...], cell_count)
    s = q = None
    for z in range(depth + 2):
        normed = (second[z] - centre) * spread
        value = upstream[z].astype(f32) * slope(normed)
        gradient[z] = value
        if 1 <= z < depth + 1:
            s, q = add_to(s, value), add_to(q, value * normed)
    send_totals(totals, s, q)


def back_conv(
    peers, cell_count, rows_one, rows_two, rows, first, second, gradient, kernel,
    cotan_two, gradient_one, totals, edge, stack, product,
):
    slab = lax.axis_index("slab")
    extended, channels, cells = second.shape
    depth = extended - 2
    centre, spread = moments(rows_two[...], cell_count)
    mean, crossed = (x / cell_count for x in to_columns(rows[...]))
    planes = []
    for z in range(extended):
        normed = (second[z] - centre) * spread
        value = (spread * (gradient[z] - mean - normed * crossed)).astype(bf16)
        value = inside(z, 1, depth, slab, peers, value)
        planes.append(value)
        if 1 <= z < depth + 1:
            cotan_two[z - 1] = value
    patches(planes, edge, stack)
    tap_products(kernel, stack, product, extended, cells)
    centre, spread = moments(rows_one[...], cell_count)
    s = q = None
    for z in range(depth):
        normed = (first[z + 2] - centre) * spread
        value = depth_sum(product, z, channels, cells) * slope(normed)
        gradient_one[z] = value
        s, q = add_to(s, value), add_to(q, value * normed)
    send_totals(totals, s, q)


def correlate(planes, cotans, edge, stack, taps):
    depth, (channels, cells) = len(cotans), cotans[0].shape
    patches(planes, edge, stack)
    zero = jnp.zeros((channels, cells), bf16)
    for a in range(3):
        for z in range(depth + 2):
            inner = 0 <= z - a < depth
            taps[a * channels : (a + 1) * channels, z * cells : (z + 1) * cells] = (
                cotans[z - a] if inner else zero
            )
    return lax.dot_general(
        stack[...], taps[...], (((1,), (1,)), ((), ())), preferred_element_type=f32
    )


def kernel_grads(
    peers, cell_count, rows_one, rows, first, gradient_one, cotan_two, hidden, own, even_recv, odd_recv,
    pieces, edge, stack, taps, gathered,
):
    slab = lax.axis_index("slab")
    depth, channels, cells = own.shape
    count, length, _ = pieces.shape
    centre, spread = moments(rows_one[...], cell_count)
    mean, crossed = (x / cell_count for x in to_columns(rows[...]))
    cotans = []
    for z in range(depth):
        normed = (first[z + 2] - centre) * spread
        cotans.append((spread * (gradient_one[z] - mean - normed * crossed)).astype(bf16))
    planes = field_halo(own, even_recv, odd_recv, 0, FEATURE_HALO, slab, peers)
    width = 9 * channels
    grads = (
        correlate(planes[FEATURE_HALO - 1 : depth + FEATURE_HALO + 1], cotans, edge, stack, taps),
        None,
    )
    for k in range(2):
        if k == 0:
            grad = grads[0]
        else:
            grad = correlate(
                [hidden[z] for z in range(depth + 2)],
                [cotan_two[z] for z in range(depth)],
                edge,
                stack,
                taps,
            )
        for a in range(3):
            gathered[a * width : (a + 1) * width, k * channels : (k + 1) * channels] = grad[
                :, a * channels : (a + 1) * channels
            ]
    if count * length > 3 * width:
        gathered[3 * width :, :] = jnp.zeros((count * length - 3 * width, 2 * channels), f32)
    for j in range(count):
        pieces[j] = gathered[j * length : (j + 1) * length, :].astype(bf16)


def piece_sums(patients, pieces, sums, squares):
    count, length, lanes = pieces.shape
    peers = count // patients
    lane = lax.broadcasted_iota(jnp.int32, (1, squares.shape[1]), 1)
    row = jnp.zeros((1, squares.shape[1]), f32)
    for p in range(patients):
        total = None
        for j in range(peers):
            total = add_to(total, pieces[p * peers + j].astype(f32))
        sums[p] = total
        part = jnp.sum(jnp.sum(total * total, axis=0, keepdims=True), axis=1, keepdims=True)
        row = jnp.where(lane == p, part, row)
    squares[...] = jnp.broadcast_to(row, squares.shape)


def clipped(patients, squares, sums, pieces):
    row = jnp.sum(squares[...], axis=0, keepdims=True)
    factor = clip_bound / jnp.maximum(jnp.sqrt(row), clip_bound)
    total = None
    for p in range(patients):
        total = add_to(total, sums[p] * factor[:, p : p + 1])
    rounded = total.astype(bf16)
    for j in range(pieces.shape[0]):
        pieces[j] = rounded


def update(pieces, weights, prev_state, tree_noise, state_next, weights_next, gathered):
    count, length, lanes = pieces.shape
    columns = state_next.shape[1]
    for j in range(count):
        gathered[j * length : (j + 1) * length, :] = pieces[j].astype(f32)
    for start in range(0, columns, 128):
        span = slice(start, min(start + 128, columns))
        combined = gathered[span, :].T
        state_next[:, span] = prev_state[:, span] + combined
        weights_next[:, span] = weights[:, span] - step_rate * (combined + tree_noise[:, span])


def exchange(rows):
    return lax.all_to_all(rows, "slab", 0, 0)


def per_device(features, cotangent, weights, prev_state, tree_noise):
    peers, patients = lax.axis_size("slab"), lax.axis_size("pat")
    devices = peers * patients
    slab = lax.axis_index("slab")
    own = features[0].transpose(1, 0, 2)
    cotan = cotangent[0].transpose(1, 0, 2)
    depth, channels, cells = own.shape
    cell_count = peers * depth * cells
    columns = weights.shape[2]

    def edge_planes(last):
        return jnp.concatenate(
            [
                lax.dynamic_slice_in_dim(own, jnp.where(last, depth - FEATURE_HALO, 0), FEATURE_HALO, 0),
                lax.dynamic_slice_in_dim(cotan, jnp.where(last, depth - COTAN_HALO, 0), COTAN_HALO, 0),
            ],
            axis=0,
        )

    even = slab % 2 == 0
    even_pairs = [(i, i ^ 1) for i in range(peers)]
    odd_pairs = [(i, (i + 1) % peers if i % 2 else (i - 1) % peers) for i in range(peers)]
    even_recv = lax.ppermute(edge_planes(even), "slab", even_pairs)
    odd_recv = lax.ppermute(edge_planes(~even), "slab", odd_pairs)

    stack_shape = sds((3 * channels, 9 * channels), bf16)
    kernel_one, kernel_two, kernel_back = call(kernel_stacks, (stack_shape,) * 3, weights)

    rows_shape = sds((peers, 2 * channels), f32)

    def scratch(planes):
        return [
            pltpu.VMEM((3 * channels, cells + 2 * PAD), bf16),
            pltpu.VMEM((9 * channels, planes * cells), bf16),
            pltpu.VMEM((3 * channels, planes * cells), f32),
        ]

    def field(planes, dtype):
        return sds((planes, channels, cells), dtype)

    conv_flops = 2 * 27 * channels * channels * cells * depth
    first, totals = call(
        functools.partial(first_conv, peers),
        (field(depth + 4, f32), rows_shape),
        own, even_recv, odd_recv, kernel_one,
        scratch=scratch(depth + 6), flops=conv_flops,
    )
    rows_one = exchange(totals)
    hidden, second, totals = call(
        functools.partial(second_conv, peers, cell_count),
        (field(depth + 2, bf16), field(depth + 2, f32), rows_shape),
        rows_one, first, kernel_two,
        scratch=scratch(depth + 4), flops=conv_flops,
    )
    rows_two = exchange(totals)
    gradient_two, totals = call(
        functools.partial(second_gradient, peers, cell_count),
        (field(depth + 2, f32), rows_shape),
        rows_two, second, cotan, even_recv, odd_recv,
    )
    rows_three = exchange(totals)
    cotan_two, gradient_one, totals = call(
        functools.partial(back_conv, peers, cell_count),
        (field(depth, bf16), field(depth, f32), rows_shape),
        rows_one, rows_two, rows_three, first, second, gradient_two, kernel_back,
        scratch=scratch(depth + 2), flops=conv_flops,
    )
    rows_four = exchange(totals)

    length = 8 * pl.cdiv(columns, 8 * devices)
    pieces_shape = sds((devices, length, 2 * channels), bf16)
    pieces = call(
        functools.partial(kernel_grads, peers, cell_count),
        pieces_shape,
        rows_one, rows_four, first, gradient_one, cotan_two, hidden, own, even_recv, odd_recv,
        scratch=[
            pltpu.VMEM((3 * channels, cells + 2 * PAD), bf16),
            pltpu.VMEM((9 * channels, (depth + 2) * cells), bf16),
            pltpu.VMEM((3 * channels, (depth + 2) * cells), bf16),
            pltpu.VMEM((devices * length, 2 * channels), f32),
        ],
        flops=2 * conv_flops,
    )
    pieces = lax.all_to_all(pieces, AXES, 0, 0)
    sums, squares = call(
        functools.partial(piece_sums, patients),
        (sds((patients, length, 2 * channels), f32), sds((devices, 128), f32)),
        pieces,
    )
    squares = lax.all_to_all(squares, AXES, 0, 0)
    pieces = call(functools.partial(clipped, patients), pieces_shape, squares, sums)
    pieces = lax.all_to_all(pieces, AXES, 0, 0)
    flat = (2 * channels, columns)
    state_next, weights_next = call(
        update,
        (sds(flat, f32), sds(flat, f32)),
        pieces, weights.reshape(flat), prev_state.reshape(flat), tree_noise.reshape(flat),
        scratch=[pltpu.VMEM((devices * length, 2 * channels), f32)],
    )
    return (state_next.reshape(weights.shape), weights_next.reshape(weights.shape))


def solution(mesh):
    return jax.shard_map(
        per_device,
        mesh=mesh,
        in_specs=(P("pat", None, "slab", None), P("pat", None, "slab", None), P(), P(), P()),
        out_specs=(P(), P()),
        check_vma=False,
    )
```

time: 287 us -> 111 us (0.39)
  waiting for transfers between devices: 110 us -> 5.14 us
  other arithmetic: 28.8 us -> 0.05 us
  matrix products: 18.9 us -> 0 us
  between operations: 16.2 us -> 0.73 us
  Pallas kernels: 0 us -> 14.4 us
  local copies, waits for them, and re-layouts: 15.9 us -> 1.96 us
  starting transfers between devices: 19.4 us -> 6.67 us
  blocking collectives: 76.5 us -> 81.2 us
    psum x2 -> x0, waiting for transfers between devices: 109 us -> none  [the longest x1 73.9 us: per_device(): sum_one, sum_two = lax.psum((kgrad_one, kgrad_two), 'slab')]
    all_to_all x0 -> x7, blocking collectives: none -> 81.2 us  [the longest x4 38.9 us: exchange(): return lax.all_to_all(rows, 'slab', 0, 0)]
    psum x4 -> x0, blocking collectives: 76.5 us -> none  [slab_totals(): return lax.psum((first, second), 'slab')]
    dot_general x15 -> x0, matrix products: 18.9 us -> none  [the longest x6 11.1 us: kernel_grad(): jnp.einsum('ozp,izp->oi', upstream, stacked, preferred_element_type=jnp.f...]
    pallas_call x0 -> x9, Pallas kernels: none -> 14.4 us  [call(): pl.pallas_call(kernel, out_shape=out_shape, in_specs=[vmem] * len(args),...]
    ppermute x6 -> x2, starting transfers between devices: 19.3 us -> 6.67 us  [the longest x1 3.61 us: per_device(): odd_recv = lax.ppermute(edge_planes(~even), 'slab', odd_pairs)]
    unnamed x28 -> x0, other arithmetic: 7.35 us -> none
    unnamed x60 -> x10, local copies, waits for them, and re-layouts: 7.31 us -> 0.02 us
  transfers between devices with their start and end apart: 8 -> 2, of which waited for: 3 -> 2; matrix products, arithmetic and copies ran while one was open for 3% -> 0% of each run, Pallas kernels for 0% -> 0%
where the time goes in v1:
time: 111 us; the launch traced here: 110 us
  blocking collectives  81.2 us (73%)
  Pallas kernels  14.4 us (13%)
  starting transfers between devices  6.67 us (6%)
  waiting for transfers between devices  5.14 us (5%)
  local copies, waits for them, and re-layouts  1.96 us (2%)
    all_to_all x4, blocking collectives, exchange(): return lax.all_to_all(rows, 'slab', 0, 0)  38.9 us
    all_to_all x2, blocking collectives, per_device(): pieces = lax.all_to_all(pieces, AXES, 0, 0)  33.1 us
    pallas_call x9, Pallas kernels, call(): pl.pallas_call(kernel, out_shape=out_shape, in_specs=[vmem] * len(args),...  14.4 us
    all_to_all x1, blocking collectives, per_device(): squares = lax.all_to_all(squares, AXES, 0, 0)  9.27 us
    ppermute x1, waiting for transfers between devices, per_device(): even_recv = lax.ppermute(edge_planes(even), 'slab', even_pairs)  4.35 us
    ppermute x1, starting transfers between devices, per_device(): odd_recv = lax.ppermute(edge_planes(~even), 'slab', odd_pairs)  3.61 us
    ppermute x1, starting transfers between devices, per_device(): even_recv = lax.ppermute(edge_planes(even), 'slab', even_pairs)  3.06 us
  transfers between devices with their start and end apart: 2, of which 2 were waited for; matrix products, arithmetic and copies ran while one was open for 0% of the time, Pallas kernels for 0%

profile of v1, /device:TPU:0, one launch (start us, length us, event | category | flops | bytes accessed | tf_op | source)
XLA Modules:
  0.0 110.2 jit_solution(12818865024291753246)
XLA Ops:
  0.6 0.0 copy-start
  0.7 0.9 dynamic-slice_bitcast_fusion.2
  1.6 1.0 dynamic-slice_bitcast_fusion
  2.6 3.1 %collective-permute-start = (bf16[4,64,384]{2,1,0:T(8,128)(2,1)S(1)}, bf16[4,64,384]{2,1,0:T(8,128)(2,1)S(1)}, u32[]{:S(2)}, u32[]{:S(2)}) collective-permute-start(bf16[4,64,384]{2,1,0:T(8,128)(2,1)S(1)} %pad_maximum_fusion), channel_id=1, source_target_pairs={{0,1},{1,0},{2,3},{3,2},{4,5},{5,4},{6,7},{7,6},{8,9},{9,8},{10,11... | collective-permute-start | bytes 589832 | tf_op jit(solution)/shard_map/ppermute | solution.py:359
  5.7 0.0 copy-start.4
  5.7 3.6 %collective-permute-start.1 = (bf16[4,64,384]{2,1,0:T(8,128)(2,1)S(1)}, bf16[4,64,384]{2,1,0:T(8,128)(2,1)S(1)}, u32[]{:S(2)}, u32[]{:S(2)}) collective-permute-start(bf16[4,64,384]{2,1,0:T(8,128)(2,1)S(1)} %pad_maximum_fusion.1), channel_id=1, source_target_pairs={{0,7},{1,2},{2,1},{3,4},{4,3},{5,6},{6,5},{7,0},{8,15},{9,10},{10,... | collective-permute-start | bytes 589832 | tf_op jit(solution)/shard_map/ppermute | solution.py:360
  9.3 0.0 copy-done
  9.3 0.4 shard_map.68
  9.7 4.3 %collective-permute-done.even_recv = bf16[4,64,384]{2,1,0:T(8,128)(2,1)S(1)} collective-permute-done((bf16[4,64,384]{2,1,0:T(8,128)(2,1)S(1)}, bf16[4,64,384]{2,1,0:T(8,128)(2,1)S(1)}, u32[]{:S(2)}, u32[]{:S(2)}) %collective-permute-start) | collective-permute-done | bytes 196640 | tf_op jit(solution)/shard_map/ppermute | solution.py:359
  14.1 0.8 collective-permute-done.1.odd_recv
  14.9 0.0 copy-done.4
  14.9 2.7 %shard_map.69 = (f32[10,64,384]{2,1,0:T(8,128)S(1)}, f32[8,128]{1,0:T(8,128)S(1)}) custom-call(bf16[6,64,384]{2,1,0:T(8,128)(2,1)S(1)} %bitcast.47, bf16[4,64,384]{2,1,0:T(8,128)(2,1)S(1)} %collective-permute-done.even_recv, bf16[4,64,384]{2,1,0:T(8,128)(2,1)S(1)} %collective-permute-done.1.odd_recv, bf16[192,576]{1,0:T(8,128)(2,1)S(1)} %get-tuple-element.19.kernel), custom_call_target="tpu_custom_call" | custom-call | flops 509607936 | bytes 909312 | tf_op jit(solution)/shard_map/pallas_call | solution.py:29
  17.6 12.3 %all_to_all.65 = f32[8,1,128]{2,1,0:T(1,128)S(1)} all-to-all(f32[8,1,128]{2,1,0:T(1,128)S(1)} %bitcast.60), channel_id=1, replica_groups=mesh['pat'=4,'slab'=8] {'slab'}, dimensions={0} | all-to-all | bytes 8192 | tf_op jit(solution)/shard_map/all_to_all | solution.py:334
  29.9 0.0 copy-start.3
  29.9 2.6 %shard_map.70 = (bf16[8,64,384]{2,1,0:T(8,128)(2,1)S(1)}, f32[8,64,384]{2,1,0:T(8,128)S(1)}, f32[8,128]{1,0:T(8,128)S(1)}) custom-call(f32[8,128]{1,0:T(8,128)S(1)} %bitcast.52, f32[10,64,384]{2,1,0:T(8,128)S(1)} %get-tuple-element.21.first, bf16[192,576]{1,0:T(8,128)(2,1)S(1)} %get-tuple-element.22.kernel), custom_call_target="tpu_custom_call" | custom-call | flops 509607936 | bytes 1208320 | tf_op jit(solution)/shard_map/pallas_call | solution.py:29
  32.5 8.9 %all_to_all.66 = f32[8,1,128]{2,1,0:T(1,128)S(1)} all-to-all(f32[8,1,128]{2,1,0:T(1,128)S(1)} %bitcast.59), channel_id=1, replica_groups=mesh['pat'=4,'slab'=8] {'slab'}, dimensions={0} | all-to-all | bytes 8192 | tf_op jit(solution)/shard_map/all_to_all | solution.py:334
  41.4 0.0 copy-done.3
  41.4 0.7 shard_map.71
  42.0 8.9 %all_to_all.67 = f32[8,1,128]{2,1,0:T(1,128)S(1)} all-to-all(f32[8,1,128]{2,1,0:T(1,128)S(1)} %bitcast.61), channel_id=1, replica_groups=mesh['pat'=4,'slab'=8] {'slab'}, dimensions={0} | all-to-all | bytes 8192 | tf_op jit(solution)/shard_map/all_to_all | solution.py:334
  50.9 2.4 %shard_map.72 = (bf16[6,64,384]{2,1,0:T(8,128)(2,1)S(1)}, f32[6,64,384]{2,1,0:T(8,128)S(1)}, f32[8,128]{1,0:T(8,128)S(1)}) custom-call(f32[8,128]{1,0:T(8,128)S(1)} %bitcast.53, f32[8,128]{1,0:T(8,128)S(1)} %bitcast.51, f32[8,128]{1,0:T(8,128)S(1)} %bitcast.55, f32[10,64,384]{2,1,0:T(8,128)S(1)} %get-tuple-element.21.first, ...), custom_call_target="tpu_custom_call" | custom-call | flops 509607936 | bytes 2789376 | tf_op jit(solution)/shard_map/pallas_call | solution.py:29
  53.3 8.9 %all_to_all.68 = f32[8,1,128]{2,1,0:T(1,128)S(1)} all-to-all(f32[8,1,128]{2,1,0:T(1,128)S(1)} %bitcast.58), channel_id=1, replica_groups=mesh['pat'=4,'slab'=8] {'slab'}, dimensions={0} | all-to-all | bytes 8192 | tf_op jit(solution)/shard_map/all_to_all | solution.py:334
  62.1 4.0 %shard_map.73 = bf16[32,56,128]{2,1,0:T(8,128)(2,1)S(1)} custom-call(f32[8,128]{1,0:T(8,128)S(1)} %bitcast.54, f32[8,128]{1,0:T(8,128)S(1)} %bitcast.57, f32[10,64,384]{2,1,0:T(8,128)S(1)} %get-tuple-element.21.first, f32[6,64,384]{2,1,0:T(8,128)S(1)} %get-tuple-element.29.gradient_one, bf16[6,64,384]{2,1,0:T(8,128)(2,1)S(1)} %get-tuple-element.30.cotan_two, ...), custom_call_target="tpu_custom_call" | custom-call | flops 1019215872 | bytes 2957312 | tf_op jit(solution)/shard_map/pallas_call | solution.py:29
  66.1 16.5 %all_to_all.69.pieces = bf16[32,56,128]{2,1,0:T(8,128)(2,1)S(1)} all-to-all(bf16[32,56,128]{2,1,0:T(8,128)(2,1)S(1)} %shard_map.73), channel_id=1, replica_groups=mesh['pat'=4,'slab'=8] {'pat','slab'}, dimensions={0} | all-to-all | bytes 917504 | tf_op jit(solution)/shard_map/all_to_all | solution.py:420
  82.7 0.0 copy-start.1
  82.7 0.0 copy-start.2
  82.7 0.1 shard_map.74
  82.8 9.3 %all_to_all.70 = f32[32,1,128]{2,1,0:T(1,128)S(1)} all-to-all(f32[32,1,128]{2,1,0:T(1,128)S(1)} %bitcast.56), channel_id=1, replica_groups=mesh['pat'=4,'slab'=8] {'pat','slab'}, dimensions={0} | all-to-all | bytes 32768 | tf_op jit(solution)/shard_map/all_to_all | solution.py:426
  92.1 0.1 shard_map.75
  92.2 16.5 %all_to_all.71.pieces = bf16[32,56,128]{2,1,0:T(8,128)(2,1)S(1)} all-to-all(bf16[32,56,128]{2,1,0:T(8,128)(2,1)S(1)} %shard_map.75), channel_id=1, replica_groups=mesh['pat'=4,'slab'=8] {'pat','slab'}, dimensions={0} | all-to-all | bytes 917504 | tf_op jit(solution)/shard_map/all_to_all | solution.py:428
  108.8 0.0 copy-done.1
  108.8 0.0 copy-done.2
  108.8 1.5 %shard_map.76 = (f32[128,1728]{1,0:T(8,128)}, f32[128,1728]{1,0:T(8,128)}) custom-call(bf16[32,56,128]{2,1,0:T(8,128)(2,1)S(1)} %all_to_all.71.pieces, f32[128,1728]{1,0:T(8,128)S(1)} %bitcast.43, f32[128,1728]{1,0:T(8,128)S(1)} %bitcast.44, f32[128,1728]{1,0:T(8,128)S(1)} %bitcast.45), custom_call_target="tpu_custom_call" | custom-call | bytes 3112960 | tf_op jit(solution)/shard_map/pallas_call | solution.py:29
  (2 shorter events, 0.1 us)
Async XLA Ops:
  0.6 8.7 %copy-start = (f32[2,64,1728]{2,1,0:T(8,128)S(1)}, f32[2,64,1728]{2,1,0:T(8,128)}, u32[]{:S(2)}) copy-start(f32[2,64,1728]{2,1,0:T(8,128)} %weights.1) | copy-start | bytes 2654212
  2.6 11.4 %collective-permute-start = (bf16[4,64,384]{2,1,0:T(8,128)(2,1)S(1)}, bf16[4,64,384]{2,1,0:T(8,128)(2,1)S(1)}, u32[]{:S(2)}, u32[]{:S(2)}) collective-permute-start(bf16[4,64,384]{2,1,0:T(8,128)(2,1)S(1)} %pad_maximum_fusion), channel_id=1, source_target_pairs={{0,1},{1,0},{2,3},{3,2},{4,5},{5,4},{6,7},{7,6},{8,9},{9,8},{10,11... | collective-permute-start | bytes 589832 | tf_op jit(solution)/shard_map/ppermute | solution.py:359
  5.7 9.1 %copy-start.4 = (bf16[1,64,6,384]{3,1,2,0:T(8,128)(2,1)S(1)}, bf16[1,64,6,384]{3,1,2,0:T(8,128)(2,1)}, u32[]{:S(2)}) copy-start(bf16[1,64,6,384]{3,1,2,0:T(8,128)(2,1)} %param.5) | copy-start | bytes 884740
  5.7 9.1 %collective-permute-start.1 = (bf16[4,64,384]{2,1,0:T(8,128)(2,1)S(1)}, bf16[4,64,384]{2,1,0:T(8,128)(2,1)S(1)}, u32[]{:S(2)}, u32[]{:S(2)}) collective-permute-start(bf16[4,64,384]{2,1,0:T(8,128)(2,1)S(1)} %pad_maximum_fusion.1), channel_id=1, source_target_pairs={{0,7},{1,2},{2,1},{3,4},{4,3},{5,6},{6,5},{7,0},{8,15},{9,10},{10,... | collective-permute-start | bytes 589832 | tf_op jit(solution)/shard_map/ppermute | solution.py:360
  29.9 11.4 %copy-start.3 = (bf16[1,64,6,384]{3,1,2,0:T(8,128)(2,1)S(1)}, bf16[1,64,6,384]{3,1,2,0:T(8,128)(2,1)}, u32[]{:S(2)}) copy-start(bf16[1,64,6,384]{3,1,2,0:T(8,128)(2,1)} %param.6) | copy-start | bytes 884740
  82.7 26.1 %copy-start.1 = (f32[2,64,1728]{2,1,0:T(8,128)S(1)}, f32[2,64,1728]{2,1,0:T(8,128)}, u32[]{:S(2)}) copy-start(f32[2,64,1728]{2,1,0:T(8,128)} %param.8) | copy-start | bytes 2654212
  82.7 26.1 %copy-start.2 = (f32[2,64,1728]{2,1,0:T(8,128)S(1)}, f32[2,64,1728]{2,1,0:T(8,128)}, u32[]{:S(2)}) copy-start(f32[2,64,1728]{2,1,0:T(8,128)} %param.9) | copy-start | bytes 2654212

commit v2 on v1

v2 whole, which is shorter than its diff:
```python
import functools

import jax
import jax.numpy as jnp
from jax import lax
from jax.experimental import pallas as pl
from jax.experimental.pallas import tpu as pltpu
from jax.sharding import PartitionSpec as P


W = 24

eps_norm = 1e-05
clip_bound = 400.0
step_rate = 0.1

f32 = jnp.float32
bf16 = jnp.bfloat16

AXES = ("pat", "slab")
PAD = 128
FEATURE_HALO = 3
COTAN_HALO = 1


def call(kernel, out_shape, *args, scratch=(), flops=0):
    vmem = pl.BlockSpec(memory_space=pltpu.VMEM)
    size = sum(a.size * a.dtype.itemsize for a in args)
    return pl.pallas_call(
        kernel,
        out_shape=out_shape,
        in_specs=[vmem] * len(args),
        out_specs=jax.tree.map(lambda _: vmem, out_shape),
        scratch_shapes=list(scratch),
        cost_estimate=pl.CostEstimate(flops=flops, bytes_accessed=size, transcendentals=0),
        compiler_params=pltpu.CompilerParams(vmem_limit_bytes=14 * 2**20),
    )(*args)


def sds(shape, dtype):
    return jax.ShapeDtypeStruct(shape, dtype)


def column_masks(cells):
    column = lax.broadcasted_iota(jnp.int32, (1, cells), 1) % W
    return (column != W - 1).astype(bf16), (column != 0).astype(bf16)


def patches(plane, edge, stack, z):
    channels, cells = plane.shape
    not_last, not_first = column_masks(cells)
    edge[0:channels, PAD + 1 : PAD + 1 + cells] = plane * not_last
    edge[channels : 2 * channels, PAD : PAD + cells] = plane
    edge[2 * channels : 3 * channels, PAD - 1 : PAD - 1 + cells] = plane * not_first
    for b in range(3):
        start = PAD + (b - 1) * W
        stack[b * 3 * channels : (b + 1) * 3 * channels, z * cells : (z + 1) * cells] = edge[
            :, start : start + cells
        ]


def products(planes, kernel, edges, stack, product):
    edges[...] = jnp.zeros_like(edges)
    count = len(planes)

    def fill(z):
        plane = planes[z]() if callable(planes[z]) else planes[z]
        patches(plane, edges.at[z % 2], stack, z)
        return plane.shape[1]

    cells = fill(0)
    if count > 1:
        fill(1)
    for z in range(0, count, 2):
        for ahead in range(z + 2, min(z + 4, count)):
            fill(ahead)
        span = slice(z * cells, min(z + 2, count) * cells)
        product[:, span] = jnp.dot(kernel[...], stack[:, span], preferred_element_type=f32)


def tap(product, a, z, channels, cells):
    return product[a * channels : (a + 1) * channels, z * cells : (z + 1) * cells]


def depth_sum(product, z, channels, cells):
    return (
        tap(product, 0, z, channels, cells)
        + tap(product, 1, z + 1, channels, cells)
        + tap(product, 2, z + 2, channels, cells)
    )


def eye(size):
    return lax.broadcasted_iota(jnp.int32, (size, size), 0) == lax.broadcasted_iota(
        jnp.int32, (size, size), 1
    )


def to_row(first, second):
    both = jnp.concatenate([first, second], axis=0)
    size = both.shape[0]
    return jnp.sum(jnp.where(eye(size), both, 0.0), axis=0, keepdims=True)


def to_columns(rows):
    row = jnp.sum(rows, axis=0, keepdims=True)
    size = row.shape[1]
    both = jnp.sum(jnp.where(eye(size), row, 0.0), axis=1, keepdims=True)
    return both[: size // 2], both[size // 2 :]


def moments(rows, cell_count):
    totals, squares = to_columns(rows)
    centre = totals / cell_count
    return centre, lax.rsqrt(squares / cell_count - centre * centre + eps_norm)


def sigmoid(values):
    return 1.0 / (1.0 + jnp.exp(-values))


def slope(values):
    gate = sigmoid(values)
    return gate * (1.0 + values * (1.0 - gate))


def add_to(total, value):
    return value if total is None else total + value


def send_totals(ref, first, second):
    row = to_row(
        jnp.sum(first, axis=1, keepdims=True), jnp.sum(second, axis=1, keepdims=True)
    )
    ref[...] = jnp.broadcast_to(row, ref.shape)


def inside(z, halo, depth, slab, peers, value):
    if z < halo:
        return jnp.where(slab > 0, value, jnp.zeros_like(value))
    if z >= halo + depth:
        return jnp.where(slab < peers - 1, value, jnp.zeros_like(value))
    return value


def cut_edges(own, cotan, near_even, near_odd, far_even, far_odd, sems):
    depth = own.shape[0]
    even = lax.axis_index("slab") % 2 == 0
    copies = []

    def copy(source, start, count, target, at):
        copies.append(
            pltpu.make_async_copy(
                source.at[pl.ds(start, count)], target.at[pl.ds(at, count)], sems.at[len(copies)]
            )
        )

    for near, far, last in ((near_even, far_even, even), (near_odd, far_odd, ~even)):
        copy(own, jnp.where(last, depth - 1, 0), 1, near, 0)
        copy(own, jnp.where(last, depth - FEATURE_HALO, 1), FEATURE_HALO - 1, far, 0)
        copy(cotan, jnp.where(last, depth - 1, 0), 1, far, FEATURE_HALO - 1)
    for c in copies:
        c.start()
    for c in copies:
        c.wait()


def halo_plane(even_recv, odd_recv, z, before, slab, peers):
    even = slab % 2 == 0
    picked = jnp.where(even == before, odd_recv[z], even_recv[z])
    return jnp.where(slab == (0 if before else peers - 1), jnp.zeros_like(picked), picked)


def kernel_stack(rounded, target):
    channels = rounded.shape[0]
    width = 9 * channels
    for a in range(3):
        target[a * channels : (a + 1) * channels, :] = rounded[:, a * width : (a + 1) * width]


def own_products(weights, own, kernel, kernel_two, back, stack, product, edge):
    channels = weights.shape[1]
    kernel_stack(weights[0].astype(bf16), kernel)
    products([own[z] for z in range(own.shape[0])], kernel, edge, stack, product)
    kernel_stack(weights[1].astype(bf16), kernel_two)
    turned = weights[1].T
    for a in range(3):
        for tap_at in range(9):
            block = (2 - a) * 9 + 8 - tap_at
            back[
                a * channels : (a + 1) * channels, tap_at * channels : (tap_at + 1) * channels
            ] = turned[block * channels : (block + 1) * channels, :].astype(bf16)


def first_conv(peers, near_even, near_odd, kernel, own_product, first, totals, stack, product, edge):
    slab = lax.axis_index("slab")
    depth, channels, cells = first.shape
    planes = [halo_plane(near_even, near_odd, 0, before, slab, peers) for before in (True, False)]
    products(planes, kernel, edge, stack, product)

    def part(a, z):
        if 0 <= z < depth:
            return tap(own_product, a, z, channels, cells)
        return tap(product, a, 0 if z < 0 else 1, channels, cells)

    s = q = None
    for z in range(depth):
        value = part(0, z - 1) + part(1, z) + part(2, z + 1)
        first[z] = value
        s, q = add_to(s, value), add_to(q, value * value)
    send_totals(totals, s, q)


def first_conv_edges(peers, far_even, far_odd, kernel, own_product, near_product, stack, product, edge):
    slab = lax.axis_index("slab")
    cells = stack.shape[1] // 4
    channels = own_product.shape[0] // 3
    depth = own_product.shape[1] // cells
    planes = [
        halo_plane(far_even, far_odd, z, before, slab, peers) for before in (True, False) for z in (0, 1)
    ]
    products(planes, kernel, edge, stack, product)
    where = {-3: 0, -2: 1, depth + 1: 2, depth + 2: 3}

    def part(a, z):
        if 0 <= z < depth:
            return tap(own_product, a, z, channels, cells)
        if z in (-1, depth):
            return tap(near_product, a, 0 if z < 0 else 1, channels, cells)
        return tap(product, a, where[z], channels, cells)

    return [part(0, z - 1) + part(1, z) + part(2, z + 1) for z in (-2, -1, depth, depth + 1)]


def second_conv(
    peers, cell_count, rows, first, far_even, far_odd, kernel_one, own_product, near_product, kernel,
    second, totals, stack, product, far_stack, far_product, edge,
):
    edges = first_conv_edges(
        peers, far_even, far_odd, kernel_one, own_product, near_product, far_stack, far_product, edge
    )
    slab = lax.axis_index("slab")
    depth, channels, cells = first.shape
    centre, spread = moments(rows[...], cell_count)

    def plane(z):
        at = z - 2
        source = first[at] if 0 <= at < depth else edges[z if z < 2 else z - depth]
        normed = (source - centre) * spread
        return inside(z, 2, depth, slab, peers, (normed * sigmoid(normed)).astype(bf16))

    products([functools.partial(plane, z) for z in range(depth + 4)], kernel, edge, stack, product)
    s = q = None
    for z in range(depth + 2):
        value = depth_sum(product, z, channels, cells)
        second[z] = value
        if 1 <= z < depth + 1:
            s, q = add_to(s, value), add_to(q, value * value)
    send_totals(totals, s, q)


def second_gradient(peers, cell_count, rows, second, cotan, far_even, far_odd, gradient, totals):
    slab = lax.axis_index("slab")
    depth = cotan.shape[0]
    centre, spread = moments(rows[...], cell_count)
    s = q = None
    for z in range(depth + 2):
        if 1 <= z < depth + 1:
            upstream = cotan[z - 1]
        else:
            upstream = halo_plane(far_even, far_odd, FEATURE_HALO - 1, z == 0, slab, peers)
        normed = (second[z] - centre) * spread
        value = upstream.astype(f32) * slope(normed)
        gradient[z] = value
        if 1 <= z < depth + 1:
            s, q = add_to(s, value), add_to(q, value * normed)
    send_totals(totals, s, q)


def back_conv(
    peers, cell_count, rows_one, rows_two, rows, first, second, gradient, kernel,
    cotan_two, gradient_one, normed_one, totals, edge, stack, product,
):
    slab = lax.axis_index("slab")
    extended, channels, cells = second.shape
    depth = extended - 2
    centre, spread = moments(rows_two[...], cell_count)
    mean, crossed = (x / cell_count for x in to_columns(rows[...]))

    def plane(z):
        normed = (second[z] - centre) * spread
        value = (spread * (gradient[z] - mean - normed * crossed)).astype(bf16)
        value = inside(z, 1, depth, slab, peers, value)
        if 1 <= z < depth + 1:
            cotan_two[z - 1] = value
        return value

    products([functools.partial(plane, z) for z in range(extended)], kernel, edge, stack, product)
    centre, spread = moments(rows_one[...], cell_count)
    s = q = None
    for z in range(depth):
        normed = (first[z] - centre) * spread
        normed_one[z] = normed
        value = depth_sum(product, z, channels, cells) * slope(normed)
        gradient_one[z] = value
        s, q = add_to(s, value), add_to(q, value * normed)
    send_totals(totals, s, q)


def fill_taps(cotans, taps, first, count):
    depth, (channels, cells) = len(cotans), cotans[0].shape
    zero = jnp.zeros((channels, cells), bf16)
    for a in range(3):
        for z in range(first, first + count):
            taps[a * channels : (a + 1) * channels, z * cells : (z + 1) * cells] = (
                cotans[z - a] if 0 <= z - a < depth else zero
            )


def contract(stack, taps):
    return lax.dot_general(stack, taps, (((1,), (1,)), ((), ())), preferred_element_type=f32)


def kernel_grads(
    cell_count, rows_one, rows, normed_one, gradient_one, own_stack, near_stack, cotan_two, hidden_stack,
    pieces, taps, taps_two, gathered,
):
    depth, channels, cells = normed_one.shape
    count, length, _ = pieces.shape
    _, spread = moments(rows_one[...], cell_count)
    mean, crossed = (x / cell_count for x in to_columns(rows[...]))
    cotans = [
        (spread * (gradient_one[z] - mean - normed_one[z] * crossed)).astype(bf16) for z in range(depth)
    ]
    fill_taps(cotans, taps, 0, depth + 2)
    width = 9 * channels
    own_taps = taps[:, cells : (depth + 1) * cells]
    near_taps = jnp.concatenate([taps[:, :cells], taps[:, (depth + 1) * cells :]], axis=1)
    grad_one = contract(own_stack[...], own_taps) + contract(near_stack[...], near_taps)
    fill_taps([cotan_two[z] for z in range(depth)], taps_two, 0, depth + 2)
    grad_two = contract(hidden_stack[:, cells : (depth + 3) * cells], taps_two[...])
    for a in range(3):
        span = slice(a * channels, (a + 1) * channels)
        rows_of = slice(a * width, (a + 1) * width)
        gathered[rows_of, :channels] = grad_one[:, span]
        gathered[rows_of, channels:] = grad_two[:, span]
    if count * length > 3 * width:
        gathered[3 * width :, :] = jnp.zeros((count * length - 3 * width, 2 * channels), f32)
    for j in range(count):
        pieces[j] = gathered[j * length : (j + 1) * length, :].astype(bf16)


def piece_sums(patients, pieces, sums, squares):
    count, _, _ = pieces.shape
    peers = count // patients
    lane = lax.broadcasted_iota(jnp.int32, (1, squares.shape[1]), 1)
    row = jnp.zeros((1, squares.shape[1]), f32)
    for p in range(patients):
        total = None
        for j in range(peers):
            total = add_to(total, pieces[p * peers + j].astype(f32))
        sums[p] = total
        part = jnp.sum(jnp.sum(total * total, axis=0, keepdims=True), axis=1, keepdims=True)
        row = jnp.where(lane == p, part, row)
    squares[...] = jnp.broadcast_to(row, squares.shape)


def clipped(patients, squares, sums, pieces):
    row = jnp.sum(squares[...], axis=0, keepdims=True)
    factor = clip_bound / jnp.maximum(jnp.sqrt(row), clip_bound)
    total = None
    for p in range(patients):
        total = add_to(total, sums[p] * factor[:, p : p + 1])
    rounded = total.astype(bf16)
    for j in range(pieces.shape[0]):
        pieces[j] = rounded


def update(pieces, weights, prev_state, tree_noise, state_next, weights_next, gathered):
    count, length, _ = pieces.shape
    columns = state_next.shape[1]
    for j in range(count):
        gathered[j * length : (j + 1) * length, :] = pieces[j].astype(f32)
    for start in range(0, columns, 128):
        span = slice(start, min(start + 128, columns))
        combined = gathered[span, :].T
        state_next[:, span] = prev_state[:, span] + combined
        weights_next[:, span] = weights[:, span] - step_rate * (combined + tree_noise[:, span])


def trade(planes, pairs):
    return lax.ppermute(planes, "slab", pairs)


def exchange(rows):
    return lax.all_to_all(rows, "slab", 0, 0)


def per_device(features, cotangent, weights, prev_state, tree_noise):
    peers, patients = lax.axis_size("slab"), lax.axis_size("pat")
    devices = peers * patients
    own = features[0].transpose(1, 0, 2)
    cotan = cotangent[0].transpose(1, 0, 2)
    depth, channels, cells = own.shape
    cell_count = peers * depth * cells
    columns = weights.shape[2]
    rows_shape = sds((peers, 2 * channels), f32)
    edge = pltpu.VMEM((2, 3 * channels, cells + 2 * PAD), bf16)

    def field(planes, dtype):
        return sds((planes, channels, cells), dtype)

    def stack_of(planes):
        return sds((9 * channels, planes * cells), bf16)

    def product_of(planes):
        return sds((3 * channels, planes * cells), f32)

    def scratch_of(shape):
        return pltpu.VMEM(shape.shape, shape.dtype)

    def flops(planes):
        return 2 * 27 * channels * channels * cells * planes

    far = field(FEATURE_HALO - 1 + COTAN_HALO, bf16)
    near_even, near_odd, far_even, far_odd = pl.pallas_call(
        cut_edges,
        out_shape=(field(1, bf16), field(1, bf16), far, far),
        in_specs=[pl.BlockSpec(memory_space=pltpu.HBM)] * 2,
        out_specs=(pl.BlockSpec(memory_space=pltpu.VMEM),) * 4,
        scratch_shapes=[pltpu.SemaphoreType.DMA((6,))],
        compiler_params=pltpu.CompilerParams(vmem_limit_bytes=2 * 2**20),
    )(own, cotan)
    even_pairs = [(i, i ^ 1) for i in range(peers)]
    odd_pairs = [(i, (i + 1) % peers if i % 2 else (i - 1) % peers) for i in range(peers)]
    near_even = trade(near_even, even_pairs)
    near_odd = trade(near_odd, odd_pairs)
    far_even = trade(far_even, even_pairs)
    far_odd = trade(far_odd, odd_pairs)

    kernel_shape = sds((3 * channels, 9 * channels), bf16)
    kernel_one, kernel_two, kernel_back, own_stack, own_product = call(
        own_products,
        (kernel_shape, kernel_shape, kernel_shape, stack_of(depth), product_of(depth)),
        weights, own,
        scratch=[edge], flops=flops(depth),
    )
    first, totals, near_stack, near_product = call(
        functools.partial(first_conv, peers),
        (field(depth, f32), rows_shape, stack_of(2), product_of(2)),
        near_even, near_odd, kernel_one, own_product,
        scratch=[edge], flops=flops(2),
    )
    rows_one = exchange(totals)
    second, totals, hidden_stack = call(
        functools.partial(second_conv, peers, cell_count),
        (field(depth + 2, f32), rows_shape, stack_of(depth + 4)),
        rows_one, first, far_even, far_odd, kernel_one, own_product, near_product, kernel_two,
        scratch=[scratch_of(product_of(depth + 4)), scratch_of(stack_of(4)), scratch_of(product_of(4)), edge],
        flops=flops(depth + 4),
    )
    rows_two = exchange(totals)
    gradient_two, totals = call(
        functools.partial(second_gradient, peers, cell_count),
        (field(depth + 2, f32), rows_shape),
        rows_two, second, cotan, far_even, far_odd,
    )
    rows_three = exchange(totals)
    cotan_two, gradient_one, normed_one, totals = call(
        functools.partial(back_conv, peers, cell_count),
        (field(depth, bf16), field(depth, f32), field(depth, f32), rows_shape),
        rows_one, rows_two, rows_three, first, second, gradient_two, kernel_back,
        scratch=[edge, scratch_of(stack_of(depth + 2)), scratch_of(product_of(depth + 2))],
        flops=flops(depth + 2),
    )
    rows_four = exchange(totals)
    taps = pltpu.VMEM((3 * channels, (depth + 2) * cells), bf16)

    length = 8 * pl.cdiv(columns, 8 * devices)
    pieces_shape = sds((devices, length, 2 * channels), bf16)
    pieces = call(
        functools.partial(kernel_grads, cell_count),
        pieces_shape,
        rows_one, rows_four, normed_one, gradient_one, own_stack, near_stack, cotan_two, hidden_stack,
        scratch=[taps, taps, pltpu.VMEM((devices * length, 2 * channels), f32)],
        flops=flops(depth + 2),
    )
    pieces = lax.all_to_all(pieces, AXES, 0, 0)
    sums, squares = call(
        functools.partial(piece_sums, patients),
        (sds((patients, length, 2 * channels), f32), sds((devices, 128), f32)),
        pieces,
    )
    squares = lax.all_to_all(squares, AXES, 0, 0)
    pieces = call(functools.partial(clipped, patients), pieces_shape, squares, sums)
    pieces = lax.all_to_all(pieces, AXES, 0, 0)
    flat = (2 * channels, columns)
    state_next, weights_next = call(
        update,
        (sds(flat, f32), sds(flat, f32)),
        pieces, weights.reshape(flat), prev_state.reshape(flat), tree_noise.reshape(flat),
        scratch=[pltpu.VMEM((devices * length, 2 * channels), f32)],
    )
    return (state_next.reshape(weights.shape), weights_next.reshape(weights.shape))


def solution(mesh):
    return jax.shard_map(
        per_device,
        mesh=mesh,
        in_specs=(P("pat", None, "slab", None), P("pat", None, "slab", None), P(), P(), P()),
        out_specs=(P(), P()),
        check_vma=False,
    )
```

time: 111 us -> 109 us (0.982)
  waiting for transfers between devices: 5.14 us -> 1.02 us
  local copies, waits for them, and re-layouts: 1.96 us -> 4.08 us
  starting transfers between devices: 6.67 us -> 8.52 us
    ppermute x2 -> x4, waiting for transfers between devices: 5.14 us -> 1.02 us  [trade(): return lax.ppermute(planes, 'slab', pairs)]
    unnamed x10 -> x16, local copies, waits for them, and re-layouts: 0.02 us -> 4.08 us
    dynamic_slice x2 -> x0, local copies, waits for them, and re-layouts: 1.93 us -> none  [the longest x1 1.02 us: edge_planes(): lax.dynamic_slice_in_dim(own, jnp.where(last, depth - FEATURE_HALO, 0), F...]
    ppermute x2 -> x4, starting transfers between devices: 6.67 us -> 8.52 us  [trade(): return lax.ppermute(planes, 'slab', pairs)]
    pallas_call x9, Pallas kernels: 14.4 us -> 13.3 us  [call(): pl.pallas_call(kernel, out_shape=out_shape, in_specs=[vmem] * len(args),...]
    all_to_all x4, blocking collectives: 38.9 us -> 37.7 us  [exchange(): return lax.all_to_all(rows, 'slab', 0, 0)]
  transfers between devices with their start and end apart: 2 -> 4, of which waited for: 2 -> 2; matrix products, arithmetic and copies ran while one was open for 0% -> 0% of each run, Pallas kernels for 0% -> 2%
where the time goes in v2:
time: 109 us; the launch traced here: 108 us
  blocking collectives  80.1 us (73%)
  Pallas kernels  13.8 us (13%)
  starting transfers between devices  8.52 us (8%)
  local copies, waits for them, and re-layouts  4.08 us (4%)
    all_to_all x4, blocking collectives, exchange(): return lax.all_to_all(rows, 'slab', 0, 0)  37.7 us
    all_to_all x2, blocking collectives, per_device(): pieces = lax.all_to_all(pieces, AXES, 0, 0)  33.2 us
    pallas_call x9, Pallas kernels, call(): pl.pallas_call(kernel, out_shape=out_shape, in_specs=[vmem] * len(args),...  13.3 us
    all_to_all x1, blocking collectives, per_device(): squares = lax.all_to_all(squares, AXES, 0, 0)  9.22 us
    ppermute x4, starting transfers between devices, trade(): return lax.ppermute(planes, 'slab', pairs)  8.52 us
    unnamed x16, local copies, waits for them, and re-layouts  4.08 us
  transfers between devices with their start and end apart: 4, of which 2 were waited for; matrix products, arithmetic and copies ran while one was open for 0% of the time, Pallas kernels for 2%

profile of v2, /device:TPU:0, one launch (start us, length us, event | category | flops | bytes accessed | tf_op | source)
XLA Modules:
  0.0 108.3 jit_solution(17534719743896911041)
XLA Ops:
  0.6 0.0 copy-start
  0.6 1.0 copy-done
  1.6 0.0 copy-start.6
  1.6 1.0 copy-done.6
  2.6 0.5 shard_map.68
  3.1 3.1 %collective-permute-start.2 = (bf16[3,64,384]{2,1,0:T(8,128)(2,1)S(1)}, bf16[3,64,384]{2,1,0:T(8,128)(2,1)S(1)}, u32[]{:S(2)}, u32[]{:S(2)}) collective-permute-start(bf16[3,64,384]{2,1,0:T(8,128)(2,1)S(1)} %get-tuple-element.34), channel_id=1, source_target_pairs={{0,1},{1,0},{2,3},{3,2},{4,5},{5,4},{6,7},{7,6},{8,9},{9,8},{10,11... | collective-permute-start | bytes 442376 | tf_op jit(solution)/shard_map/ppermute | solution.py:392
  6.2 3.5 %collective-permute-start.3 = (bf16[3,64,384]{2,1,0:T(8,128)(2,1)S(1)}, bf16[3,64,384]{2,1,0:T(8,128)(2,1)S(1)}, u32[]{:S(2)}, u32[]{:S(2)}) collective-permute-start(bf16[3,64,384]{2,1,0:T(8,128)(2,1)S(1)} %get-tuple-element.35), channel_id=1, source_target_pairs={{0,7},{1,2},{2,1},{3,4},{4,3},{5,6},{6,5},{7,0},{8,15},{9,10},{10,... | collective-permute-start | bytes 442376 | tf_op jit(solution)/shard_map/ppermute | solution.py:392
  9.7 0.0 collective-permute-start
  9.7 1.9 %collective-permute-start.1 = (bf16[1,64,384]{2,1,0:T(8,128)(2,1)S(1)}, bf16[1,64,384]{2,1,0:T(8,128)(2,1)S(1)}, u32[]{:S(2)}, u32[]{:S(2)}) collective-permute-start(bf16[1,64,384]{2,1,0:T(8,128)(2,1)S(1)} %get-tuple-element.29), channel_id=1, source_target_pairs={{0,7},{1,2},{2,1},{3,4},{4,3},{5,6},{6,5},{7,0},{8,15},{9,10},{10,... | collective-permute-start | bytes 147464 | tf_op jit(solution)/shard_map/ppermute | solution.py:392
  11.6 0.0 copy-start.2
  11.6 1.2 %copy-done.2 = f32[2,64,1728]{2,1,0:T(8,128)S(1)} copy-done((f32[2,64,1728]{2,1,0:T(8,128)S(1)}, f32[2,64,1728]{2,1,0:T(8,128)}, u32[]{:S(2)}) %copy-start.2) | copy-done | bytes 884760
  12.8 0.0 copy-start.7
  12.8 1.0 copy-done.7
  13.8 1.7 %shard_map.69 = (bf16[192,576]{1,0:T(8,128)(2,1)S(1)}, bf16[192,576]{1,0:T(8,128)(2,1)S(1)}, bf16[192,576]{1,0:T(8,128)(2,1)S(1)}, bf16[576,2304]{1,0:T(8,128)(2,1)S(1)}, f32[192,2304]{1,0:T(8,128)S(1)}) custom-call(f32[2,64,1728]{2,1,0:T(8,128)S(1)} %copy-done.2, bf16[6,64,384]{2,1,0:T(8,128)(2,1)S(1)} %bitcast.37), custom_call_target="tpu_custom_call" | custom-call | flops 509607936 | bytes 1179648 | tf_op jit(solution)/shard_map/pallas_call | solution.py:29
  15.5 0.3 collective-permute-done.near_even
  15.7 0.7 collective-permute-done.1.near_odd
  16.5 0.0 copy-start.1
  16.5 0.9 shard_map.70
  17.4 11.1 %all_to_all.65 = f32[8,1,128]{2,1,0:T(1,128)S(1)} all-to-all(f32[8,1,128]{2,1,0:T(1,128)S(1)} %bitcast.49), channel_id=1, replica_groups=mesh['pat'=4,'slab'=8] {'slab'}, dimensions={0} | all-to-all | bytes 8192 | tf_op jit(solution)/shard_map/all_to_all | solution.py:396
  28.6 0.0 collective-permute-done.2.far_even
  28.6 0.0 collective-permute-done.3.far_odd
  28.6 3.5 %shard_map.71 = (f32[8,64,384]{2,1,0:T(8,128)S(1)}, f32[8,128]{1,0:T(8,128)S(1)}, bf16[576,3840]{1,0:T(8,128)(2,1)S(1)}) custom-call(f32[8,128]{1,0:T(8,128)S(1)} %bitcast.39, f32[6,64,384]{2,1,0:T(8,128)S(1)} %get-tuple-element.33.first, bf16[3,64,384]{2,1,0:T(8,128)(2,1)S(1)} %collective-permute-done.2.far_even, ...), custom_call_target="tpu_custom_call" | custom-call | flops 849346560 | bytes 3690496 | tf_op jit(solution)/shard_map/pallas_call | solution.py:29
  32.1 8.9 %all_to_all.66 = f32[8,1,128]{2,1,0:T(1,128)S(1)} all-to-all(f32[8,1,128]{2,1,0:T(1,128)S(1)} %bitcast.48), channel_id=1, replica_groups=mesh['pat'=4,'slab'=8] {'slab'}, dimensions={0} | all-to-all | bytes 8192 | tf_op jit(solution)/shard_map/all_to_all | solution.py:396
  40.9 0.0 copy-done.1
  40.9 0.7 shard_map.72
  41.7 8.9 %all_to_all.67 = f32[8,1,128]{2,1,0:T(1,128)S(1)} all-to-all(f32[8,1,128]{2,1,0:T(1,128)S(1)} %bitcast.50), channel_id=1, replica_groups=mesh['pat'=4,'slab'=8] {'slab'}, dimensions={0} | all-to-all | bytes 8192 | tf_op jit(solution)/shard_map/all_to_all | solution.py:396
  50.5 2.3 %shard_map.73 = (bf16[6,64,384]{2,1,0:T(8,128)(2,1)S(1)}, f32[6,64,384]{2,1,0:T(8,128)S(1)}, f32[6,64,384]{2,1,0:T(8,128)S(1)}, f32[8,128]{1,0:T(8,128)S(1)}) custom-call(f32[8,128]{1,0:T(8,128)S(1)} %bitcast.40, f32[8,128]{1,0:T(8,128)S(1)} %bitcast.43, f32[8,128]{1,0:T(8,128)S(1)} %bitcast.46, f32[6,64,384]{2,1,0:T(8,128)S(1)} %get-tuple-element.33.first, ...), custom_call_target="tpu_custom_call" | custom-call | flops 679477248 | bytes 2396160 | tf_op jit(solution)/shard_map/pallas_call | solution.py:29
  52.8 8.9 %all_to_all.68 = f32[8,1,128]{2,1,0:T(1,128)S(1)} all-to-all(f32[8,1,128]{2,1,0:T(1,128)S(1)} %bitcast.47), channel_id=1, replica_groups=mesh['pat'=4,'slab'=8] {'slab'}, dimensions={0} | all-to-all | bytes 8192 | tf_op jit(solution)/shard_map/all_to_all | solution.py:396
  61.7 2.3 %shard_map.74 = bf16[32,56,128]{2,1,0:T(8,128)(2,1)S(1)} custom-call(f32[8,128]{1,0:T(8,128)S(1)} %bitcast.41, f32[8,128]{1,0:T(8,128)S(1)} %bitcast.44, f32[6,64,384]{2,1,0:T(8,128)S(1)} %get-tuple-element.44.normed_one, f32[6,64,384]{2,1,0:T(8,128)S(1)} %get-tuple-element.45.gradient_one, bf16[576,2304]{1,0:T(8,128)(2,1)S(1)} %get-tuple-element.46.own_stack, ...), custom_call_target="tpu_custom_call" | custom-call | flops 679477248 | bytes 9445376 | tf_op jit(solution)/shard_map/pallas_call | solution.py:29
  64.1 0.0 copy-start.3
  64.1 0.0 copy-start.4
  64.1 0.0 copy-start.5
  64.1 16.7 %all_to_all.69.pieces = bf16[32,56,128]{2,1,0:T(8,128)(2,1)S(1)} all-to-all(bf16[32,56,128]{2,1,0:T(8,128)(2,1)S(1)} %shard_map.74), channel_id=1, replica_groups=mesh['pat'=4,'slab'=8] {'pat','slab'}, dimensions={0} | all-to-all | bytes 917504 | tf_op jit(solution)/shard_map/all_to_all | solution.py:488
  80.8 0.1 shard_map.75
  80.9 9.2 %all_to_all.70 = f32[32,1,128]{2,1,0:T(1,128)S(1)} all-to-all(f32[32,1,128]{2,1,0:T(1,128)S(1)} %bitcast.45), channel_id=1, replica_groups=mesh['pat'=4,'slab'=8] {'pat','slab'}, dimensions={0} | all-to-all | bytes 32768 | tf_op jit(solution)/shard_map/all_to_all | solution.py:494
  90.1 0.1 shard_map.76
  90.3 16.5 %all_to_all.71.pieces = bf16[32,56,128]{2,1,0:T(8,128)(2,1)S(1)} all-to-all(bf16[32,56,128]{2,1,0:T(8,128)(2,1)S(1)} %shard_map.76), channel_id=1, replica_groups=mesh['pat'=4,'slab'=8] {'pat','slab'}, dimensions={0} | all-to-all | bytes 917504 | tf_op jit(solution)/shard_map/all_to_all | solution.py:496
  106.8 0.0 copy-done.3
  106.8 0.0 copy-done.4
  106.8 0.0 copy-done.5
  106.8 1.5 %shard_map.77 = (f32[128,1728]{1,0:T(8,128)}, f32[128,1728]{1,0:T(8,128)}) custom-call(bf16[32,56,128]{2,1,0:T(8,128)(2,1)S(1)} %all_to_all.71.pieces, f32[128,1728]{1,0:T(8,128)S(1)} %bitcast.33, f32[128,1728]{1,0:T(8,128)S(1)} %bitcast.34, f32[128,1728]{1,0:T(8,128)S(1)} %bitcast.35), custom_call_target="tpu_custom_call" | custom-call | bytes 3112960 | tf_op jit(solution)/shard_map/pallas_call | solution.py:29
Async XLA Ops:
  0.6 1.0 copy-start
  1.6 1.0 copy-start.6
  3.1 25.5 %collective-permute-start.2 = (bf16[3,64,384]{2,1,0:T(8,128)(2,1)S(1)}, bf16[3,64,384]{2,1,0:T(8,128)(2,1)S(1)}, u32[]{:S(2)}, u32[]{:S(2)}) collective-permute-start(bf16[3,64,384]{2,1,0:T(8,128)(2,1)S(1)} %get-tuple-element.34), channel_id=1, source_target_pairs={{0,1},{1,0},{2,3},{3,2},{4,5},{5,4},{6,7},{7,6},{8,9},{9,8},{10,11... | collective-permute-start | bytes 442376 | tf_op jit(solution)/shard_map/ppermute | solution.py:392
  6.2 22.4 %collective-permute-start.3 = (bf16[3,64,384]{2,1,0:T(8,128)(2,1)S(1)}, bf16[3,64,384]{2,1,0:T(8,128)(2,1)S(1)}, u32[]{:S(2)}, u32[]{:S(2)}) collective-permute-start(bf16[3,64,384]{2,1,0:T(8,128)(2,1)S(1)} %get-tuple-element.35), channel_id=1, source_target_pairs={{0,7},{1,2},{2,1},{3,4},{4,3},{5,6},{6,5},{7,0},{8,15},{9,10},{10,... | collective-permute-start | bytes 442376 | tf_op jit(solution)/shard_map/ppermute | solution.py:392
  9.7 6.0 %collective-permute-start = (bf16[1,64,384]{2,1,0:T(8,128)(2,1)S(1)}, bf16[1,64,384]{2,1,0:T(8,128)(2,1)S(1)}, u32[]{:S(2)}, u32[]{:S(2)}) collective-permute-start(bf16[1,64,384]{2,1,0:T(8,128)(2,1)S(1)} %get-tuple-element.28), channel_id=1, source_target_pairs={{0,1},{1,0},{2,3},{3,2},{4,5},{5,4},{6,7},{7,6},{8,9},{9,8},{10,11... | collective-permute-start | bytes 147464 | tf_op jit(solution)/shard_map/ppermute | solution.py:392
  9.7 6.8 %collective-permute-start.1 = (bf16[1,64,384]{2,1,0:T(8,128)(2,1)S(1)}, bf16[1,64,384]{2,1,0:T(8,128)(2,1)S(1)}, u32[]{:S(2)}, u32[]{:S(2)}) collective-permute-start(bf16[1,64,384]{2,1,0:T(8,128)(2,1)S(1)} %get-tuple-element.29), channel_id=1, source_target_pairs={{0,7},{1,2},{2,1},{3,4},{4,3},{5,6},{6,5},{7,0},{8,15},{9,10},{10,... | collective-permute-start | bytes 147464 | tf_op jit(solution)/shard_map/ppermute | solution.py:392
  11.6 1.2 %copy-start.2 = (f32[2,64,1728]{2,1,0:T(8,128)S(1)}, f32[2,64,1728]{2,1,0:T(8,128)}, u32[]{:S(2)}) copy-start(f32[2,64,1728]{2,1,0:T(8,128)} %weights.1) | copy-start | bytes 2654212
  12.8 1.0 copy-start.7
  16.5 24.4 %copy-start.1 = (bf16[1,64,6,384]{3,1,2,0:T(8,128)(2,1)S(1)}, bf16[1,64,6,384]{3,1,2,0:T(8,128)(2,1)}, u32[]{:S(2)}) copy-start(bf16[1,64,6,384]{3,1,2,0:T(8,128)(2,1)} %param.6) | copy-start | bytes 884740
  64.1 42.8 %copy-start.3 = (f32[2,64,1728]{2,1,0:T(8,128)S(1)}, f32[2,64,1728]{2,1,0:T(8,128)}, u32[]{:S(2)}) copy-start(f32[2,64,1728]{2,1,0:T(8,128)} %weights.1) | copy-start | bytes 2654212
  64.1 42.8 %copy-start.4 = (f32[2,64,1728]{2,1,0:T(8,128)S(1)}, f32[2,64,1728]{2,1,0:T(8,128)}, u32[]{:S(2)}) copy-start(f32[2,64,1728]{2,1,0:T(8,128)} %param.8) | copy-start | bytes 2654212
  64.1 42.7 %copy-start.5 = (f32[2,64,1728]{2,1,0:T(8,128)S(1)}, f32[2,64,1728]{2,1,0:T(8,128)}, u32[]{:S(2)}) copy-start(f32[2,64,1728]{2,1,0:T(8,128)} %param.9) | copy-start | bytes 2654212

commit v3 on v2

--- a/solution.py
+++ b/solution.py
@@ -18,9 +18,9 @@
 bf16 = jnp.bfloat16
 
 AXES = ("pat", "slab")
-PAD = 128
 FEATURE_HALO = 3
 COTAN_HALO = 1
+EARLY = 10**10
 
 
 def call(kernel, out_shape, *args, scratch=(), flops=0):
@@ -33,7 +33,7 @@
         out_specs=jax.tree.map(lambda _: vmem, out_shape),
         scratch_shapes=list(scratch),
         cost_estimate=pl.CostEstimate(flops=flops, bytes_accessed=size, transcendentals=0),
-        compiler_params=pltpu.CompilerParams(vmem_limit_bytes=14 * 2**20),
+        compiler_params=pltpu.CompilerParams(vmem_limit_bytes=18 * 2**20),
     )(*args)
 
 
@@ -41,31 +41,23 @@
     return jax.ShapeDtypeStruct(shape, dtype)
 
 
-def column_masks(cells):
+def patches(plane, stack, z):
+    channels, cells = plane.shape
     column = lax.broadcasted_iota(jnp.int32, (1, cells), 1) % W
-    return (column != W - 1).astype(bf16), (column != 0).astype(bf16)
-
-
-def patches(plane, edge, stack, z):
-    channels, cells = plane.shape
-    not_last, not_first = column_masks(cells)
-    edge[0:channels, PAD + 1 : PAD + 1 + cells] = plane * not_last
-    edge[channels : 2 * channels, PAD : PAD + cells] = plane
-    edge[2 * channels : 3 * channels, PAD - 1 : PAD - 1 + cells] = plane * not_first
-    for b in range(3):
-        start = PAD + (b - 1) * W
-        stack[b * 3 * channels : (b + 1) * 3 * channels, z * cells : (z + 1) * cells] = edge[
-            :, start : start + cells
-        ]
-
-
-def products(planes, kernel, edges, stack, product):
-    edges[...] = jnp.zeros_like(edges)
+    span = slice(z * cells, (z + 1) * cells)
+    stack[0:channels, span] = pltpu.roll(plane, 1, 1) * (column != 0).astype(bf16)
+    stack[channels : 2 * channels, span] = plane
+    stack[2 * channels : 3 * channels, span] = pltpu.roll(plane, cells - 1, 1) * (
+        column != W - 1
+    ).astype(bf16)
+
+
+def products(planes, kernel, stack, product):
     count = len(planes)
 
     def fill(z):
         plane = planes[z]() if callable(planes[z]) else planes[z]
-        patches(plane, edges.at[z % 2], stack, z)
+        patches(plane, stack, z)
         return plane.shape[1]
 
     cells = fill(0)
@@ -78,16 +70,33 @@
         product[:, span] = jnp.dot(kernel[...], stack[:, span], preferred_element_type=f32)
 
 
-def tap(product, a, z, channels, cells):
-    return product[a * channels : (a + 1) * channels, z * cells : (z + 1) * cells]
+def tap(product, a, b, z, channels, cells):
+    at = 3 * a + b
+    return product[at * channels : (at + 1) * channels, z * cells : (z + 1) * cells]
+
+
+def row_shift(value, rows):
+    if rows == 0:
+        return value
+    cells = value.shape[1]
+    cell = lax.broadcasted_iota(jnp.int32, (1, cells), 1)
+    kept = cell < cells - W if rows > 0 else cell >= W
+    moved = pltpu.roll(value, (-rows * W) % cells, 1)
+    if value.dtype == bf16:
+        return moved * kept.astype(bf16)
+    return jnp.where(kept, moved, 0.0)
+
+
+def tap_sum(part, z):
+    total = None
+    for b in range(3):
+        rows = part(0, b, z - 1) + part(1, b, z) + part(2, b, z + 1)
+        total = add_to(total, row_shift(rows, b - 1))
+    return total
 
 
 def depth_sum(product, z, channels, cells):
-    return (
-        tap(product, 0, z, channels, cells)
-        + tap(product, 1, z + 1, channels, cells)
-        + tap(product, 2, z + 2, channels, cells)
-    )
+    return tap_sum(lambda a, b, at: tap(product, a, b, at + 1, channels, cells), z)
 
 
 def eye(size):
@@ -143,26 +152,20 @@
     return value
 
 
-def cut_edges(own, cotan, near_even, near_odd, far_even, far_odd, sems):
+def cut_near(own, near_even, near_odd):
     depth = own.shape[0]
     even = lax.axis_index("slab") % 2 == 0
-    copies = []
-
-    def copy(source, start, count, target, at):
-        copies.append(
-            pltpu.make_async_copy(
-                source.at[pl.ds(start, count)], target.at[pl.ds(at, count)], sems.at[len(copies)]
-            )
-        )
-
-    for near, far, last in ((near_even, far_even, even), (near_odd, far_odd, ~even)):
-        copy(own, jnp.where(last, depth - 1, 0), 1, near, 0)
-        copy(own, jnp.where(last, depth - FEATURE_HALO, 1), FEATURE_HALO - 1, far, 0)
-        copy(cotan, jnp.where(last, depth - 1, 0), 1, far, FEATURE_HALO - 1)
-    for c in copies:
-        c.start()
-    for c in copies:
-        c.wait()
+    for near, last in ((near_even, even), (near_odd, ~even)):
+        near[0] = own[jnp.where(last, depth - 1, 0)]
+
+
+def cut_far(own, cotan, far_even, far_odd):
+    depth = own.shape[0]
+    even = lax.axis_index("slab") % 2 == 0
+    for far, last in ((far_even, even), (far_odd, ~even)):
+        for z in range(FEATURE_HALO - 1):
+            far[z] = own[jnp.where(last, depth - FEATURE_HALO, 1) + z]
+        far[FEATURE_HALO - 1] = cotan[jnp.where(last, depth - 1, 0)]
 
 
 def halo_plane(even_recv, odd_recv, z, before, slab, peers):
@@ -173,71 +176,71 @@
 
 def kernel_stack(rounded, target):
     channels = rounded.shape[0]
-    width = 9 * channels
-    for a in range(3):
-        target[a * channels : (a + 1) * channels, :] = rounded[:, a * width : (a + 1) * width]
-
-
-def own_products(weights, own, kernel, kernel_two, back, stack, product, edge):
+    width = 3 * channels
+    for at in range(9):
+        target[at * channels : (at + 1) * channels, :] = rounded[:, at * width : (at + 1) * width]
+
+
+def own_products(weights, own, kernel, kernel_two, back, stack, product):
     channels = weights.shape[1]
     kernel_stack(weights[0].astype(bf16), kernel)
-    products([own[z] for z in range(own.shape[0])], kernel, edge, stack, product)
+    products([own[z] for z in range(own.shape[0])], kernel, stack, product)
     kernel_stack(weights[1].astype(bf16), kernel_two)
     turned = weights[1].T
-    for a in range(3):
-        for tap_at in range(9):
-            block = (2 - a) * 9 + 8 - tap_at
-            back[
-                a * channels : (a + 1) * channels, tap_at * channels : (tap_at + 1) * channels
-            ] = turned[block * channels : (block + 1) * channels, :].astype(bf16)
-
-
-def first_conv(peers, near_even, near_odd, kernel, own_product, first, totals, stack, product, edge):
+    for at in range(9):
+        for e in range(3):
+            block = (8 - at) * 3 + 2 - e
+            back[at * channels : (at + 1) * channels, e * channels : (e + 1) * channels] = turned[
+                block * channels : (block + 1) * channels, :
+            ].astype(bf16)
+
+
+def first_conv(peers, near_even, near_odd, kernel, own_product, first, totals, stack, product):
     slab = lax.axis_index("slab")
     depth, channels, cells = first.shape
     planes = [halo_plane(near_even, near_odd, 0, before, slab, peers) for before in (True, False)]
-    products(planes, kernel, edge, stack, product)
-
-    def part(a, z):
+    products(planes, kernel, stack, product)
+
+    def part(a, b, z):
         if 0 <= z < depth:
-            return tap(own_product, a, z, channels, cells)
-        return tap(product, a, 0 if z < 0 else 1, channels, cells)
+            return tap(own_product, a, b, z, channels, cells)
+        return tap(product, a, b, 0 if z < 0 else 1, channels, cells)
 
     s = q = None
     for z in range(depth):
-        value = part(0, z - 1) + part(1, z) + part(2, z + 1)
+        value = tap_sum(part, z)
         first[z] = value
         s, q = add_to(s, value), add_to(q, value * value)
     send_totals(totals, s, q)
 
 
-def first_conv_edges(peers, far_even, far_odd, kernel, own_product, near_product, stack, product, edge):
+def first_conv_edges(peers, far_even, far_odd, kernel, own_product, near_product, stack, product):
     slab = lax.axis_index("slab")
     cells = stack.shape[1] // 4
-    channels = own_product.shape[0] // 3
+    channels = own_product.shape[0] // 9
     depth = own_product.shape[1] // cells
     planes = [
         halo_plane(far_even, far_odd, z, before, slab, peers) for before in (True, False) for z in (0, 1)
     ]
-    products(planes, kernel, edge, stack, product)
+    products(planes, kernel, stack, product)
     where = {-3: 0, -2: 1, depth + 1: 2, depth + 2: 3}
 
-    def part(a, z):
+    def part(a, b, z):
         if 0 <= z < depth:
-            return tap(own_product, a, z, channels, cells)
+            return tap(own_product, a, b, z, channels, cells)
         if z in (-1, depth):
-            return tap(near_product, a, 0 if z < 0 else 1, channels, cells)
-        return tap(product, a, where[z], channels, cells)
-
-    return [part(0, z - 1) + part(1, z) + part(2, z + 1) for z in (-2, -1, depth, depth + 1)]
+            return tap(near_product, a, b, 0 if z < 0 else 1, channels, cells)
+        return tap(product, a, b, where[z], channels, cells)
+
+    return [tap_sum(part, z) for z in (-2, -1, depth, depth + 1)]
 
 
 def second_conv(
     peers, cell_count, rows, first, far_even, far_odd, kernel_one, own_product, near_product, kernel,
-    second, totals, stack, product, far_stack, far_product, edge,
+    second, totals, stack, product, far_stack, far_product,
 ):
     edges = first_conv_edges(
-        peers, far_even, far_odd, kernel_one, own_product, near_product, far_stack, far_product, edge
+        peers, far_even, far_odd, kernel_one, own_product, near_product, far_stack, far_product
     )
     slab = lax.axis_index("slab")
     depth, channels, cells = first.shape
@@ -249,7 +252,7 @@
         normed = (source - centre) * spread
         return inside(z, 2, depth, slab, peers, (normed * sigmoid(normed)).astype(bf16))
 
-    products([functools.partial(plane, z) for z in range(depth + 4)], kernel, edge, stack, product)
+    products([functools.partial(plane, z) for z in range(depth + 4)], kernel, stack, product)
     s = q = None
     for z in range(depth + 2):
         value = depth_sum(product, z, channels, cells)
@@ -279,7 +282,7 @@
 
 def back_conv(
     peers, cell_count, rows_one, rows_two, rows, first, second, gradient, kernel,
-    cotan_two, gradient_one, normed_one, totals, edge, stack, product,
+    cotan_two, gradient_one, normed_one, totals, stack, product,
 ):
     slab = lax.axis_index("slab")
     extended, channels, cells = second.shape
@@ -295,7 +298,7 @@
             cotan_two[z - 1] = value
         return value
 
-    products([functools.partial(plane, z) for z in range(extended)], kernel, edge, stack, product)
+    products([functools.partial(plane, z) for z in range(extended)], kernel, stack, product)
     centre, spread = moments(rows_one[...], cell_count)
     s = q = None
     for z in range(depth):
@@ -307,18 +310,23 @@
     send_totals(totals, s, q)
 
 
-def fill_taps(cotans, taps, first, count):
+def fill_taps(cotans, taps):
     depth, (channels, cells) = len(cotans), cotans[0].shape
-    zero = jnp.zeros((channels, cells), bf16)
+    zero = jnp.zeros((3 * channels, cells), bf16)
     for a in range(3):
-        for z in range(first, first + count):
-            taps[a * channels : (a + 1) * channels, z * cells : (z + 1) * cells] = (
-                cotans[z - a] if 0 <= z - a < depth else zero
-            )
-
-
-def contract(stack, taps):
-    return lax.dot_general(stack, taps, (((1,), (1,)), ((), ())), preferred_element_type=f32)
+        for z in range(depth + 2):
+            if not 0 <= z - a < depth:
+                taps[3 * a * channels : 3 * (a + 1) * channels, z * cells : (z + 1) * cells] = zero
+    for z, plane in enumerate(cotans):
+        for b in range(3):
+            value = row_shift(plane, 1 - b)
+            for a in range(3):
+                at = 3 * a + b
+                taps[at * channels : (at + 1) * channels, (z + a) * cells : (z + a + 1) * cells] = value
+
+
+def contract(taps, stack):
+    return lax.dot_general(taps, stack, (((1,), (1,)), ((), ())), preferred_element_type=f32)
 
 
 def kernel_grads(
@@ -332,16 +340,16 @@
     cotans = [
         (spread * (gradient_one[z] - mean - normed_one[z] * crossed)).astype(bf16) for z in range(depth)
     ]
-    fill_taps(cotans, taps, 0, depth + 2)
+    fill_taps(cotans, taps)
     width = 9 * channels
     own_taps = taps[:, cells : (depth + 1) * cells]
     near_taps = jnp.concatenate([taps[:, :cells], taps[:, (depth + 1) * cells :]], axis=1)
-    grad_one = contract(own_stack[...], own_taps) + contract(near_stack[...], near_taps)
-    fill_taps([cotan_two[z] for z in range(depth)], taps_two, 0, depth + 2)
-    grad_two = contract(hidden_stack[:, cells : (depth + 3) * cells], taps_two[...])
-    for a in range(3):
-        span = slice(a * channels, (a + 1) * channels)
-        rows_of = slice(a * width, (a + 1) * width)
+    grad_one = contract(own_taps, own_stack[...]) + contract(near_taps, near_stack[...])
+    fill_taps([cotan_two[z] for z in range(depth)], taps_two)
+    grad_two = contract(taps_two[...], hidden_stack[:, cells : (depth + 3) * cells])
+    for e in range(3):
+        span = slice(e * channels, (e + 1) * channels)
+        rows_of = slice(e * width, (e + 1) * width)
         gathered[rows_of, :channels] = grad_one[:, span]
         gathered[rows_of, channels:] = grad_two[:, span]
     if count * length > 3 * width:
@@ -377,15 +385,23 @@
 
 
 def update(pieces, weights, prev_state, tree_noise, state_next, weights_next, gathered):
-    count, length, _ = pieces.shape
-    columns = state_next.shape[1]
+    count, length, lanes = pieces.shape
+    channels, blocks = lanes // 2, 27
     for j in range(count):
         gathered[j * length : (j + 1) * length, :] = pieces[j].astype(f32)
-    for start in range(0, columns, 128):
-        span = slice(start, min(start + 128, columns))
-        combined = gathered[span, :].T
-        state_next[:, span] = prev_state[:, span] + combined
-        weights_next[:, span] = weights[:, span] - step_rate * (combined + tree_noise[:, span])
+
+    def block(at, k):
+        row = (at % 3 * 9 + at // 3) * channels
+        return gathered[row : row + channels, k * channels : (k + 1) * channels]
+
+    for at in range(0, blocks, 2):
+        group = range(at, min(at + 2, blocks))
+        span = slice(at * channels, (group[-1] + 1) * channels)
+        for k in range(2):
+            rows = slice(k * channels, (k + 1) * channels)
+            combined = jnp.concatenate([block(i, k) for i in group], axis=1)
+            state_next[rows, span] = prev_state[rows, span] + combined
+            weights_next[rows, span] = weights[rows, span] - step_rate * (combined + tree_noise[rows, span])
 
 
 def trade(planes, pairs):
@@ -405,16 +421,15 @@
     cell_count = peers * depth * cells
     columns = weights.shape[2]
     rows_shape = sds((peers, 2 * channels), f32)
-    edge = pltpu.VMEM((2, 3 * channels, cells + 2 * PAD), bf16)
 
     def field(planes, dtype):
         return sds((planes, channels, cells), dtype)
 
     def stack_of(planes):
-        return sds((9 * channels, planes * cells), bf16)
+        return sds((3 * channels, planes * cells), bf16)
 
     def product_of(planes):
-        return sds((3 * channels, planes * cells), f32)
+        return sds((9 * channels, planes * cells), f32)
 
     def scratch_of(shape):
         return pltpu.VMEM(shape.shape, shape.dtype)
@@ -423,14 +438,8 @@
         return 2 * 27 * channels * channels * cells * planes
 
     far = field(FEATURE_HALO - 1 + COTAN_HALO, bf16)
-    near_even, near_odd, far_even, far_odd = pl.pallas_call(
-        cut_edges,
-        out_shape=(field(1, bf16), field(1, bf16), far, far),
-        in_specs=[pl.BlockSpec(memory_space=pltpu.HBM)] * 2,
-        out_specs=(pl.BlockSpec(memory_space=pltpu.VMEM),) * 4,
-        scratch_shapes=[pltpu.SemaphoreType.DMA((6,))],
-        compiler_params=pltpu.CompilerParams(vmem_limit_bytes=2 * 2**20),
-    )(own, cotan)
+    near_even, near_odd = call(cut_near, (field(1, bf16),) * 2, own, flops=EARLY)
+    far_even, far_odd = call(cut_far, (far,) * 2, own, cotan)
     even_pairs = [(i, i ^ 1) for i in range(peers)]
     odd_pairs = [(i, (i + 1) % peers if i % 2 else (i - 1) % peers) for i in range(peers)]
     near_even = trade(near_even, even_pairs)
@@ -438,25 +447,25 @@
     far_even = trade(far_even, even_pairs)
     far_odd = trade(far_odd, odd_pairs)
 
-    kernel_shape = sds((3 * channels, 9 * channels), bf16)
+    kernel_shape = sds((9 * channels, 3 * channels), bf16)
     kernel_one, kernel_two, kernel_back, own_stack, own_product = call(
         own_products,
         (kernel_shape, kernel_shape, kernel_shape, stack_of(depth), product_of(depth)),
         weights, own,
-        scratch=[edge], flops=flops(depth),
+        flops=flops(depth),
     )
     first, totals, near_stack, near_product = call(
         functools.partial(first_conv, peers),
         (field(depth, f32), rows_shape, stack_of(2), product_of(2)),
         near_even, near_odd, kernel_one, own_product,
-        scratch=[edge], flops=flops(2),
+        flops=flops(2),
     )
     rows_one = exchange(totals)
     second, totals, hidden_stack = call(
         functools.partial(second_conv, peers, cell_count),
         (field(depth + 2, f32), rows_shape, stack_of(depth + 4)),
         rows_one, first, far_even, far_odd, kernel_one, own_product, near_product, kernel_two,
-        scratch=[scratch_of(product_of(depth + 4)), scratch_of(stack_of(4)), scratch_of(product_of(4)), edge],
+        scratch=[scratch_of(product_of(depth + 4)), scratch_of(stack_of(4)), scratch_of(product_of(4))],
         flops=flops(depth + 4),
     )
     rows_two = exchange(totals)
@@ -470,11 +479,11 @@
         functools.partial(back_conv, peers, cell_count),
         (field(depth, bf16), field(depth, f32), field(depth, f32), rows_shape),
         rows_one, rows_two, rows_three, first, second, gradient_two, kernel_back,
-        scratch=[edge, scratch_of(stack_of(depth + 2)), scratch_of(product_of(depth + 2))],
+        scratch=[scratch_of(stack_of(depth + 2)), scratch_of(product_of(depth + 2))],
         flops=flops(depth + 2),
     )
     rows_four = exchange(totals)
-    taps = pltpu.VMEM((3 * channels, (depth + 2) * cells), bf16)
+    taps = pltpu.VMEM((9 * channels, (depth + 2) * cells), bf16)
 
     length = 8 * pl.cdiv(columns, 8 * devices)
     pieces_shape = sds((devices, length, 2 * channels), bf16)

time: 109 us -> 107 us (0.982)
  waiting for transfers between devices: 1.02 us -> 3.99 us
  Pallas kernels: 13.8 us -> 11.3 us
  local copies, waits for them, and re-layouts: 4.08 us -> 1.94 us
    ppermute x4, waiting for transfers between devices: 1.02 us -> 3.99 us  [trade(): return lax.ppermute(planes, 'slab', pairs)]
    unnamed x16 -> x12, local copies, waits for them, and re-layouts: 4.08 us -> 1.94 us
    pallas_call x9 -> x11, Pallas kernels: 13.3 us -> 11.3 us  [call(): pl.pallas_call(kernel, out_shape=out_shape, in_specs=[vmem] * len(args),...]
where the time goes in v3:
time: 107 us; the launch traced here: 106 us
  blocking collectives  80 us (75%)
  Pallas kernels  11.3 us (11%)
  starting transfers between devices  8.57 us (8%)
  waiting for transfers between devices  3.99 us (4%)
  local copies, waits for them, and re-layouts  1.94 us (2%)
    all_to_all x4, blocking collectives, exchange(): return lax.all_to_all(rows, 'slab', 0, 0)  37.5 us
    all_to_all x2, blocking collectives, per_device(): pieces = lax.all_to_all(pieces, AXES, 0, 0)  33.2 us
    pallas_call x11, Pallas kernels, call(): pl.pallas_call(kernel, out_shape=out_shape, in_specs=[vmem] * len(args),...  11.3 us
    all_to_all x1, blocking collectives, per_device(): squares = lax.all_to_all(squares, AXES, 0, 0)  9.22 us
    ppermute x4, starting transfers between devices, trade(): return lax.ppermute(planes, 'slab', pairs)  8.57 us
    ppermute x4, waiting for transfers between devices, trade(): return lax.ppermute(planes, 'slab', pairs)  3.99 us
  transfers between devices with their start and end apart: 4, of which 2 were waited for; matrix products, arithmetic and copies ran while one was open for 0% of the time, Pallas kernels for 2%

profile of v3, /device:TPU:0, one launch (start us, length us, event | category | flops | bytes accessed | tf_op | source)
XLA Modules:
  0.0 106.5 jit_solution(2857868889437601909)
XLA Ops:
  0.6 0.0 copy-start
  0.6 1.0 copy-done
  1.6 0.0 copy-start.5
  1.6 1.0 copy-done.5
  2.6 3.1 %collective-permute-start.2 = (bf16[3,64,384]{2,1,0:T(8,128)(2,1)S(1)}, bf16[3,64,384]{2,1,0:T(8,128)(2,1)S(1)}, u32[]{:S(2)}, u32[]{:S(2)}) collective-permute-start(bf16[3,64,384]{2,1,0:T(8,128)(2,1)S(1)} %get-tuple-element.34), channel_id=1, source_target_pairs={{0,1},{1,0},{2,3},{3,2},{4,5},{5,4},{6,7},{7,6},{8,9},{9,8},{10,11... | collective-permute-start | bytes 442376 | tf_op jit(solution)/shard_map/ppermute | solution.py:408
  5.6 0.0 copy-start.2
  5.6 3.5 %collective-permute-start.3 = (bf16[3,64,384]{2,1,0:T(8,128)(2,1)S(1)}, bf16[3,64,384]{2,1,0:T(8,128)(2,1)S(1)}, u32[]{:S(2)}, u32[]{:S(2)}) collective-permute-start(bf16[3,64,384]{2,1,0:T(8,128)(2,1)S(1)} %get-tuple-element.35), channel_id=1, source_target_pairs={{0,7},{1,2},{2,1},{3,4},{4,3},{5,6},{6,5},{7,0},{8,15},{9,10},{10,... | collective-permute-start | bytes 442376 | tf_op jit(solution)/shard_map/ppermute | solution.py:408
  9.2 0.1 collective-permute-start
  9.3 1.9 %collective-permute-start.1 = (bf16[1,64,384]{2,1,0:T(8,128)(2,1)S(1)}, bf16[1,64,384]{2,1,0:T(8,128)(2,1)S(1)}, u32[]{:S(2)}, u32[]{:S(2)}) collective-permute-start(bf16[1,64,384]{2,1,0:T(8,128)(2,1)S(1)} %get-tuple-element.29), channel_id=1, source_target_pairs={{0,7},{1,2},{2,1},{3,4},{4,3},{5,6},{6,5},{7,0},{8,15},{9,10},{10,... | collective-permute-start | bytes 147464 | tf_op jit(solution)/shard_map/ppermute | solution.py:408
  11.2 0.0 copy-done.2
  11.2 1.0 shard_map.69
  12.2 3.1 %collective-permute-done.near_even = bf16[1,64,384]{2,1,0:T(8,128)(2,1)S(1)} collective-permute-done((bf16[1,64,384]{2,1,0:T(8,128)(2,1)S(1)}, bf16[1,64,384]{2,1,0:T(8,128)(2,1)S(1)}, u32[]{:S(2)}, u32[]{:S(2)}) %collective-permute-start) | collective-permute-done | bytes 49184 | tf_op jit(solution)/shard_map/ppermute | solution.py:408
  15.2 0.9 collective-permute-done.1.near_odd
  16.1 0.8 shard_map.70
  17.0 11.0 %all_to_all.65 = f32[8,1,128]{2,1,0:T(1,128)S(1)} all-to-all(f32[8,1,128]{2,1,0:T(1,128)S(1)} %bitcast.50), channel_id=1, replica_groups=mesh['pat'=4,'slab'=8] {'slab'}, dimensions={0} | all-to-all | bytes 8192 | tf_op jit(solution)/shard_map/all_to_all | solution.py:412
  27.9 0.0 collective-permute-done.2.far_even
  27.9 0.0 collective-permute-done.3.far_odd
  27.9 0.0 copy-start.1
  28.0 2.5 %shard_map.72 = (f32[8,64,384]{2,1,0:T(8,128)S(1)}, f32[8,128]{1,0:T(8,128)S(1)}, bf16[192,3840]{1,0:T(8,128)(2,1)S(1)}) custom-call(f32[8,128]{1,0:T(8,128)S(1)} %bitcast.40, f32[6,64,384]{2,1,0:T(8,128)S(1)} %get-tuple-element.33.first, bf16[3,64,384]{2,1,0:T(8,128)(2,1)S(1)} %collective-permute-done.2.far_even, ...), custom_call_target="tpu_custom_call" | custom-call | flops 849346560 | bytes 8409088 | tf_op jit(solution)/shard_map/pallas_call | solution.py:29
  30.4 8.9 %all_to_all.66 = f32[8,1,128]{2,1,0:T(1,128)S(1)} all-to-all(f32[8,1,128]{2,1,0:T(1,128)S(1)} %bitcast.49), channel_id=1, replica_groups=mesh['pat'=4,'slab'=8] {'slab'}, dimensions={0} | all-to-all | bytes 8192 | tf_op jit(solution)/shard_map/all_to_all | solution.py:412
  39.3 0.0 copy-done.1
  39.3 0.7 shard_map.73
  40.0 8.9 %all_to_all.67 = f32[8,1,128]{2,1,0:T(1,128)S(1)} all-to-all(f32[8,1,128]{2,1,0:T(1,128)S(1)} %bitcast.51), channel_id=1, replica_groups=mesh['pat'=4,'slab'=8] {'slab'}, dimensions={0} | all-to-all | bytes 8192 | tf_op jit(solution)/shard_map/all_to_all | solution.py:412
  48.8 1.8 %shard_map.74 = (bf16[6,64,384]{2,1,0:T(8,128)(2,1)S(1)}, f32[6,64,384]{2,1,0:T(8,128)S(1)}, f32[6,64,384]{2,1,0:T(8,128)S(1)}, f32[8,128]{1,0:T(8,128)S(1)}) custom-call(f32[8,128]{1,0:T(8,128)S(1)} %bitcast.41, f32[8,128]{1,0:T(8,128)S(1)} %bitcast.44, f32[8,128]{1,0:T(8,128)S(1)} %bitcast.47, f32[6,64,384]{2,1,0:T(8,128)S(1)} %get-tuple-element.33.first, ...), custom_call_target="tpu_custom_call" | custom-call | flops 679477248 | bytes 2396160 | tf_op jit(solution)/shard_map/pallas_call | solution.py:29
  50.6 8.9 %all_to_all.68 = f32[8,1,128]{2,1,0:T(1,128)S(1)} all-to-all(f32[8,1,128]{2,1,0:T(1,128)S(1)} %bitcast.48), channel_id=1, replica_groups=mesh['pat'=4,'slab'=8] {'slab'}, dimensions={0} | all-to-all | bytes 8192 | tf_op jit(solution)/shard_map/all_to_all | solution.py:412
  59.5 2.6 %shard_map.75 = bf16[32,56,128]{2,1,0:T(8,128)(2,1)S(1)} custom-call(f32[8,128]{1,0:T(8,128)S(1)} %bitcast.42, f32[8,128]{1,0:T(8,128)S(1)} %bitcast.45, f32[6,64,384]{2,1,0:T(8,128)S(1)} %get-tuple-element.44.normed_one, f32[6,64,384]{2,1,0:T(8,128)S(1)} %get-tuple-element.45.gradient_one, bf16[192,2304]{1,0:T(8,128)(2,1)S(1)} %get-tuple-element.46.own_stack, ...), custom_call_target="tpu_custom_call" | custom-call | flops 679477248 | bytes 4136960 | tf_op jit(solution)/shard_map/pallas_call | solution.py:29
  62.1 0.0 copy-start.3
  62.1 0.0 copy-start.4
  62.1 16.7 %all_to_all.69.pieces = bf16[32,56,128]{2,1,0:T(8,128)(2,1)S(1)} all-to-all(bf16[32,56,128]{2,1,0:T(8,128)(2,1)S(1)} %shard_map.75), channel_id=1, replica_groups=mesh['pat'=4,'slab'=8] {'pat','slab'}, dimensions={0} | all-to-all | bytes 917504 | tf_op jit(solution)/shard_map/all_to_all | solution.py:497
  78.8 0.1 shard_map.76
  79.0 9.2 %all_to_all.70 = f32[32,1,128]{2,1,0:T(1,128)S(1)} all-to-all(f32[32,1,128]{2,1,0:T(1,128)S(1)} %bitcast.46), channel_id=1, replica_groups=mesh['pat'=4,'slab'=8] {'pat','slab'}, dimensions={0} | all-to-all | bytes 32768 | tf_op jit(solution)/shard_map/all_to_all | solution.py:503
  88.2 0.1 shard_map.77
  88.3 16.5 %all_to_all.71.pieces = bf16[32,56,128]{2,1,0:T(8,128)(2,1)S(1)} all-to-all(bf16[32,56,128]{2,1,0:T(8,128)(2,1)S(1)} %shard_map.77), channel_id=1, replica_groups=mesh['pat'=4,'slab'=8] {'pat','slab'}, dimensions={0} | all-to-all | bytes 917504 | tf_op jit(solution)/shard_map/all_to_all | solution.py:505
  104.9 0.0 copy-done.3
  104.9 0.0 copy-done.4
  104.9 1.6 %shard_map.78 = (f32[128,1728]{1,0:T(8,128)}, f32[128,1728]{1,0:T(8,128)}) custom-call(bf16[32,56,128]{2,1,0:T(8,128)(2,1)S(1)} %all_to_all.71.pieces, f32[128,1728]{1,0:T(8,128)S(1)} %bitcast.33, f32[128,1728]{1,0:T(8,128)S(1)} %bitcast.34, f32[128,1728]{1,0:T(8,128)S(1)} %bitcast.35), custom_call_target="tpu_custom_call" | custom-call | bytes 3112960 | tf_op jit(solution)/shard_map/pallas_call | solution.py:29
  (2 shorter events, 0.0 us)
Async XLA Ops:
  0.6 1.0 copy-start
  1.6 1.0 copy-start.5
  2.6 25.4 %collective-permute-start.2 = (bf16[3,64,384]{2,1,0:T(8,128)(2,1)S(1)}, bf16[3,64,384]{2,1,0:T(8,128)(2,1)S(1)}, u32[]{:S(2)}, u32[]{:S(2)}) collective-permute-start(bf16[3,64,384]{2,1,0:T(8,128)(2,1)S(1)} %get-tuple-element.34), channel_id=1, source_target_pairs={{0,1},{1,0},{2,3},{3,2},{4,5},{5,4},{6,7},{7,6},{8,9},{9,8},{10,11... | collective-permute-start | bytes 442376 | tf_op jit(solution)/shard_map/ppermute | solution.py:408
  5.6 5.5 %copy-start.2 = (f32[2,64,1728]{2,1,0:T(8,128)S(1)}, f32[2,64,1728]{2,1,0:T(8,128)}, u32[]{:S(2)}) copy-start(f32[2,64,1728]{2,1,0:T(8,128)} %weights.1) | copy-start | bytes 2654212
  5.6 22.3 %collective-permute-start.3 = (bf16[3,64,384]{2,1,0:T(8,128)(2,1)S(1)}, bf16[3,64,384]{2,1,0:T(8,128)(2,1)S(1)}, u32[]{:S(2)}, u32[]{:S(2)}) collective-permute-start(bf16[3,64,384]{2,1,0:T(8,128)(2,1)S(1)} %get-tuple-element.35), channel_id=1, source_target_pairs={{0,7},{1,2},{2,1},{3,4},{4,3},{5,6},{6,5},{7,0},{8,15},{9,10},{10,... | collective-permute-start | bytes 442376 | tf_op jit(solution)/shard_map/ppermute | solution.py:408
  9.2 6.0 %collective-permute-start = (bf16[1,64,384]{2,1,0:T(8,128)(2,1)S(1)}, bf16[1,64,384]{2,1,0:T(8,128)(2,1)S(1)}, u32[]{:S(2)}, u32[]{:S(2)}) collective-permute-start(bf16[1,64,384]{2,1,0:T(8,128)(2,1)S(1)} %get-tuple-element.28), channel_id=1, source_target_pairs={{0,1},{1,0},{2,3},{3,2},{4,5},{5,4},{6,7},{7,6},{8,9},{9,8},{10,11... | collective-permute-start | bytes 147464 | tf_op jit(solution)/shard_map/ppermute | solution.py:408
  9.3 6.9 %collective-permute-start.1 = (bf16[1,64,384]{2,1,0:T(8,128)(2,1)S(1)}, bf16[1,64,384]{2,1,0:T(8,128)(2,1)S(1)}, u32[]{:S(2)}, u32[]{:S(2)}) collective-permute-start(bf16[1,64,384]{2,1,0:T(8,128)(2,1)S(1)} %get-tuple-element.29), channel_id=1, source_target_pairs={{0,7},{1,2},{2,1},{3,4},{4,3},{5,6},{6,5},{7,0},{8,15},{9,10},{10,... | collective-permute-start | bytes 147464 | tf_op jit(solution)/shard_map/ppermute | solution.py:408
  27.9 11.3 %copy-start.1 = (bf16[1,64,6,384]{3,1,2,0:T(8,128)(2,1)S(1)}, bf16[1,64,6,384]{3,1,2,0:T(8,128)(2,1)}, u32[]{:S(2)}) copy-start(bf16[1,64,6,384]{3,1,2,0:T(8,128)(2,1)} %param.6) | copy-start | bytes 884740
  62.1 42.7 %copy-start.3 = (f32[2,64,1728]{2,1,0:T(8,128)S(1)}, f32[2,64,1728]{2,1,0:T(8,128)}, u32[]{:S(2)}) copy-start(f32[2,64,1728]{2,1,0:T(8,128)} %param.8) | copy-start | bytes 2654212
  62.1 42.7 %copy-start.4 = (f32[2,64,1728]{2,1,0:T(8,128)S(1)}, f32[2,64,1728]{2,1,0:T(8,128)}, u32[]{:S(2)}) copy-start(f32[2,64,1728]{2,1,0:T(8,128)} %param.9) | copy-start | bytes 2654212

commit v4 on v3

--- a/solution.py
+++ b/solution.py
@@ -282,7 +282,7 @@
 
 def back_conv(
     peers, cell_count, rows_one, rows_two, rows, first, second, gradient, kernel,
-    cotan_two, gradient_one, normed_one, totals, stack, product,
+    cotan_two, gradient_one, normed_one, stack, product,
 ):
     slab = lax.axis_index("slab")
     extended, channels, cells = second.shape
@@ -300,76 +300,148 @@
 
     products([functools.partial(plane, z) for z in range(extended)], kernel, stack, product)
     centre, spread = moments(rows_one[...], cell_count)
-    s = q = None
     for z in range(depth):
         normed = (first[z] - centre) * spread
         normed_one[z] = normed
-        value = depth_sum(product, z, channels, cells) * slope(normed)
-        gradient_one[z] = value
-        s, q = add_to(s, value), add_to(q, value * normed)
-    send_totals(totals, s, q)
-
-
-def fill_taps(cotans, taps):
-    depth, (channels, cells) = len(cotans), cotans[0].shape
-    zero = jnp.zeros((3 * channels, cells), bf16)
-    for a in range(3):
-        for z in range(depth + 2):
-            if not 0 <= z - a < depth:
-                taps[3 * a * channels : 3 * (a + 1) * channels, z * cells : (z + 1) * cells] = zero
+        gradient_one[z] = depth_sum(product, z, channels, cells) * slope(normed)
+
+
+def fill_taps(cotans, taps, at):
+    rows, cells = cotans[0].shape
     for z, plane in enumerate(cotans):
         for b in range(3):
-            value = row_shift(plane, 1 - b)
-            for a in range(3):
-                at = 3 * a + b
-                taps[at * channels : (at + 1) * channels, (z + a) * cells : (z + a + 1) * cells] = value
-
-
-def contract(taps, stack):
-    return lax.dot_general(taps, stack, (((1,), (1,)), ((), ())), preferred_element_type=f32)
+            taps[at + b * rows : at + (b + 1) * rows, z * cells : (z + 1) * cells] = row_shift(plane, 1 - b)
+
+
+def contract(stack, taps, depth, cells):
+    windows = [stack[:, a * cells : (a + depth) * cells] for a in range(3)]
+    return lax.dot_general(
+        jnp.concatenate(windows, axis=0), taps, (((1,), (1,)), ((), ())), preferred_element_type=f32
+    )
+
+
+def extra_rows(length):
+    return 8 * pl.cdiv(length + 7, 16)
+
+
+def three_parts(row):
+    parts = []
+    for _ in range(3):
+        part = row.astype(bf16).astype(f32)
+        parts.append(part)
+        row = row - part
+    return parts
 
 
 def kernel_grads(
-    cell_count, rows_one, rows, normed_one, gradient_one, own_stack, near_stack, cotan_two, hidden_stack,
-    pieces, taps, taps_two, gathered,
+    cell_count, rows_one, normed_one, gradient_one, own_stack, near_stack, cotan_two, hidden_stack,
+    pieces, stack, taps_one, taps_two, gathered, side, ones_rows,
 ):
     depth, channels, cells = normed_one.shape
-    count, length, _ = pieces.shape
+    count, rows, lanes = pieces.shape
+    length = gathered.shape[0] // count
+    half = rows - length
     _, spread = moments(rows_one[...], cell_count)
-    mean, crossed = (x / cell_count for x in to_columns(rows[...]))
-    cotans = [
-        (spread * (gradient_one[z] - mean - normed_one[z] * crossed)).astype(bf16) for z in range(depth)
-    ]
-    fill_taps(cotans, taps)
-    width = 9 * channels
-    own_taps = taps[:, cells : (depth + 1) * cells]
-    near_taps = jnp.concatenate([taps[:, :cells], taps[:, (depth + 1) * cells :]], axis=1)
-    grad_one = contract(own_taps, own_stack[...]) + contract(near_taps, near_stack[...])
-    fill_taps([cotan_two[z] for z in range(depth)], taps_two)
-    grad_two = contract(taps_two[...], hidden_stack[:, cells : (depth + 3) * cells])
-    for e in range(3):
-        span = slice(e * channels, (e + 1) * channels)
-        rows_of = slice(e * width, (e + 1) * width)
-        gathered[rows_of, :channels] = grad_one[:, span]
-        gathered[rows_of, channels:] = grad_two[:, span]
-    if count * length > 3 * width:
-        gathered[3 * width :, :] = jnp.zeros((count * length - 3 * width, 2 * channels), f32)
+    s = q = None
+    for z in range(depth):
+        s, q = add_to(s, gradient_one[z]), add_to(q, gradient_one[z] * normed_one[z])
+    s = jnp.sum(s, axis=1, keepdims=True)
+    q = jnp.sum(q, axis=1, keepdims=True)
+    mean, crossed = s / (depth * cells), q / (depth * cells)
+    centred, normed = [], []
+    for z in range(depth):
+        value = spread * (gradient_one[z] - mean - normed_one[z] * crossed)
+        centred.append(value.astype(bf16))
+        normed.append((spread * normed_one[z]).astype(bf16))
+    stack[:, :cells] = near_stack[:, :cells]
+    stack[:, cells : (depth + 1) * cells] = own_stack[...]
+    stack[:, (depth + 1) * cells :] = near_stack[:, cells:]
+    width = 3 * channels
+    fill_taps(centred, taps_one, 0)
+    fill_taps(normed, taps_one, width)
+    cell = lax.broadcasted_iota(jnp.int32, (16, cells), 1)
+    tap_row = lax.broadcasted_iota(jnp.int32, (16, cells), 0)
+    ones = jnp.where(
+        ((tap_row == 0) & (cell < cells - W)) | (tap_row == 1) | ((tap_row == 2) & (cell >= W)), 1.0, 0.0
+    ).astype(bf16)
+    for z in range(depth):
+        taps_one[2 * width :, z * cells : (z + 1) * cells] = ones
+    fill_taps([cotan_two[z] for z in range(depth)], taps_two, 0)
+    grad_one = contract(stack, taps_one[...], depth, cells)
+    grad_two = contract(hidden_stack.at[:, cells : (depth + 3) * cells], taps_two[...], depth, cells)
+    for b in range(3):
+        at = slice(b * 3 * width, (b + 1) * 3 * width)
+        span = slice(b * channels, (b + 1) * channels)
+        gathered[at, :channels] = grad_one[:, span]
+        gathered[at, channels:] = grad_two[:, span]
+        side[at, :channels] = grad_one[:, width + b * channels : width + (b + 1) * channels]
+    total = 9 * width
+    if count * length > total:
+        gathered[total:, :] = jnp.zeros((count * length - total, lanes), f32)
+        side[total:, :] = jnp.zeros((count * length - total, lanes), f32)
+    turned = grad_one[:, 2 * width :].T
+    ones_rows[:, :channels] = jnp.zeros((1, channels), f32)
+    for b in range(3):
+        start = channels + b * 3 * width
+        ones_rows[:, start : start + 3 * width] = turned[b : b + 1, :]
+    ones_rows[:, channels + total :] = jnp.zeros((1, ones_rows.shape[1] - channels - total), f32)
+    row = to_row(spread * s, q)
+    sums = three_parts(row)
+    tail = jnp.concatenate(
+        [pltpu.roll(part, channels, 1) for part in sums] + sums + [jnp.zeros((1, lanes), f32)], axis=0
+    )
+    left = lax.broadcasted_iota(jnp.int32, (half, lanes), 1) < channels
     for j in range(count):
-        pieces[j] = gathered[j * length : (j + 1) * length, :].astype(bf16)
-
-
-def piece_sums(patients, pieces, sums, squares):
-    count, _, _ = pieces.shape
+        pieces[j, :length] = gathered[j * length : (j + 1) * length, :].astype(bf16)
+        first = side[j * length : j * length + half, :]
+        further = jnp.concatenate([tail, ones_rows[:, j * length : j * length + lanes]], axis=0)
+        if length > half:
+            second = pltpu.roll(side[j * length + half : (j + 1) * length, :], channels, 1)
+            further = jnp.concatenate([second, further], axis=0)
+        if further.shape[0] < half:
+            pad = jnp.zeros((half - further.shape[0], lanes), f32)
+            further = jnp.concatenate([further, pad], axis=0)
+        pieces[j, length:] = jnp.where(left, first, further).astype(bf16)
+
+
+def piece_sums(patients, cells, pieces, sums, squares):
+    count, rows, lanes = pieces.shape
+    length = sums.shape[1]
+    half, channels = rows - length, lanes // 2
     peers = count // patients
+    start = length + max(length - half, 0)
+    further = jnp.concatenate([pieces[c, start : start + 8] for c in range(count)], axis=0)
+    target = lax.broadcasted_iota(jnp.int32, (3 * count, 8 * count), 0)
+    source = lax.broadcasted_iota(jnp.int32, (3 * count, 8 * count), 1)
+    offset = source - 8 * (target % count)
+    part = target // count
+    picked = (offset >= 3 * part) & (offset < 3 * part + 3) & (part < 2) | (part == 2) & (offset == 7)
+    picks = jnp.dot(jnp.where(picked, 1.0, 0.0).astype(bf16), further, preferred_element_type=f32)
+    lower = lax.broadcasted_iota(jnp.int32, (3 * count, lanes), 1) < channels
+    picks = jnp.where(lower, pltpu.roll(picks, channels, 1), 0.0)
+
     lane = lax.broadcasted_iota(jnp.int32, (1, squares.shape[1]), 1)
     row = jnp.zeros((1, squares.shape[1]), f32)
     for p in range(patients):
-        total = None
+        means, crosses, ones = (
+            picks[at * count + p * peers : at * count + (p + 1) * peers] for at in range(3)
+        )
+        means, crosses = (
+            jnp.sum(x, axis=0, keepdims=True) / (cells * peers) - x / cells for x in (means, crosses)
+        )
+        total = -lax.dot_general(
+            ones, means, (((0,), (0,)), ((), ())), precision=lax.Precision.HIGHEST, preferred_element_type=f32
+        )[:length]
         for j in range(peers):
-            total = add_to(total, pieces[p * peers + j].astype(f32))
+            piece = pieces.at[p * peers + j]
+            normed = piece[length : length + min(length, half)].astype(f32)
+            if length > half:
+                second = pltpu.roll(piece[length : 2 * length - half].astype(f32), channels, 1)
+                normed = jnp.concatenate([normed, second], axis=0)
+            total = total + piece[:length].astype(f32) - crosses[j : j + 1] * normed
         sums[p] = total
-        part = jnp.sum(jnp.sum(total * total, axis=0, keepdims=True), axis=1, keepdims=True)
-        row = jnp.where(lane == p, part, row)
+        part_of = jnp.sum(jnp.sum(total * total, axis=0, keepdims=True), axis=1, keepdims=True)
+        row = jnp.where(lane == p, part_of, row)
     squares[...] = jnp.broadcast_to(row, squares.shape)
 
 
@@ -386,22 +458,20 @@
 
 def update(pieces, weights, prev_state, tree_noise, state_next, weights_next, gathered):
     count, length, lanes = pieces.shape
-    channels, blocks = lanes // 2, 27
+    width = 3 * (lanes // 2)
     for j in range(count):
         gathered[j * length : (j + 1) * length, :] = pieces[j].astype(f32)
 
-    def block(at, k):
-        row = (at % 3 * 9 + at // 3) * channels
-        return gathered[row : row + channels, k * channels : (k + 1) * channels]
-
-    for at in range(0, blocks, 2):
-        group = range(at, min(at + 2, blocks))
-        span = slice(at * channels, (group[-1] + 1) * channels)
-        for k in range(2):
-            rows = slice(k * channels, (k + 1) * channels)
-            combined = jnp.concatenate([block(i, k) for i in group], axis=1)
-            state_next[rows, span] = prev_state[rows, span] + combined
-            weights_next[rows, span] = weights[rows, span] - step_rate * (combined + tree_noise[rows, span])
+    def block(at):
+        row = (at % 3 * 3 + at // 3) * width
+        return gathered[row : row + width, :]
+
+    for at in range(0, 9, 2):
+        group = range(at, min(at + 2, 9))
+        span = slice(at * width, (group[-1] + 1) * width)
+        combined = jnp.concatenate([block(i) for i in group], axis=0).T
+        state_next[:, span] = prev_state[:, span] + combined
+        weights_next[:, span] = weights[:, span] - step_rate * (combined + tree_noise[:, span])
 
 
 def trade(planes, pairs):
@@ -475,34 +545,40 @@
         rows_two, second, cotan, far_even, far_odd,
     )
     rows_three = exchange(totals)
-    cotan_two, gradient_one, normed_one, totals = call(
+    cotan_two, gradient_one, normed_one = call(
         functools.partial(back_conv, peers, cell_count),
-        (field(depth, bf16), field(depth, f32), field(depth, f32), rows_shape),
+        (field(depth, bf16), field(depth, f32), field(depth, f32)),
         rows_one, rows_two, rows_three, first, second, gradient_two, kernel_back,
         scratch=[scratch_of(stack_of(depth + 2)), scratch_of(product_of(depth + 2))],
         flops=flops(depth + 2),
     )
-    rows_four = exchange(totals)
-    taps = pltpu.VMEM((9 * channels, (depth + 2) * cells), bf16)
 
     length = 8 * pl.cdiv(columns, 8 * devices)
-    pieces_shape = sds((devices, length, 2 * channels), bf16)
+    taps = pltpu.VMEM((3 * channels, depth * cells), bf16)
     pieces = call(
         functools.partial(kernel_grads, cell_count),
-        pieces_shape,
-        rows_one, rows_four, normed_one, gradient_one, own_stack, near_stack, cotan_two, hidden_stack,
-        scratch=[taps, taps, pltpu.VMEM((devices * length, 2 * channels), f32)],
-        flops=flops(depth + 2),
+        sds((devices, length + extra_rows(length), 2 * channels), bf16),
+        rows_one, normed_one, gradient_one, own_stack, near_stack, cotan_two, hidden_stack,
+        scratch=[
+            scratch_of(stack_of(depth + 2)),
+            pltpu.VMEM((6 * channels + 16, depth * cells), bf16),
+            taps,
+            pltpu.VMEM((devices * length, 2 * channels), f32),
+            pltpu.VMEM((devices * length, 2 * channels), f32),
+            pltpu.VMEM((1, devices * length + 4 * channels), f32),
+        ],
+        flops=3 * flops(depth),
     )
     pieces = lax.all_to_all(pieces, AXES, 0, 0)
     sums, squares = call(
-        functools.partial(piece_sums, patients),
+        functools.partial(piece_sums, patients, depth * cells),
         (sds((patients, length, 2 * channels), f32), sds((devices, 128), f32)),
         pieces,
     )
+    pieces_shape = sds((peers, length, 2 * channels), bf16)
     squares = lax.all_to_all(squares, AXES, 0, 0)
     pieces = call(functools.partial(clipped, patients), pieces_shape, squares, sums)
-    pieces = lax.all_to_all(pieces, AXES, 0, 0)
+    pieces = lax.all_gather(lax.all_to_all(pieces, "slab", 0, 0), "pat", tiled=True)
     flat = (2 * channels, columns)
     state_next, weights_next = call(
         update,

time: 107 us -> 104 us (0.972)
  blocking collectives: 80 us -> 76.1 us
    all_to_all x2 -> x1, blocking collectives: 33.2 us -> 22.3 us  [per_device(): pieces = lax.all_to_all(pieces, AXES, 0, 0)]
    all_to_all x0 -> x1, blocking collectives: none -> 9.62 us  [per_device(): lax.all_to_all(pieces, 'slab', 0, 0)]
    all_to_all x4 -> x3, blocking collectives: 37.5 us -> 28.7 us  [exchange(): return lax.all_to_all(rows, 'slab', 0, 0)]
    all_gather x0 -> x1, blocking collectives: none -> 6.31 us  [per_device(): lax.all_gather(lax.all_to_all(pieces, 'slab', 0, 0), 'pat', tiled=True)]
where the time goes in v4:
time: 104 us
  blocking collectives  76.1 us (73%)
  Pallas kernels  12.3 us (12%)
  starting transfers between devices  8.57 us (8%)
  waiting for transfers between devices  4 us (4%)
  local copies, waits for them, and re-layouts  1.94 us (2%)
    all_to_all x3, blocking collectives, exchange(): return lax.all_to_all(rows, 'slab', 0, 0)  28.7 us
    all_to_all x1, blocking collectives, per_device(): pieces = lax.all_to_all(pieces, AXES, 0, 0)  22.3 us
    pallas_call x11, Pallas kernels, call(): pl.pallas_call(kernel, out_shape=out_shape, in_specs=[vmem] * len(args),...  12.3 us
    all_to_all x1, blocking collectives, per_device(): lax.all_to_all(pieces, 'slab', 0, 0)  9.62 us
    all_to_all x1, blocking collectives, per_device(): squares = lax.all_to_all(squares, AXES, 0, 0)  9.22 us
    ppermute x4, starting transfers between devices, trade(): return lax.ppermute(planes, 'slab', pairs)  8.57 us
    all_gather x1, blocking collectives, per_device(): lax.all_gather(lax.all_to_all(pieces, 'slab', 0, 0), 'pat', tiled=True)  6.31 us
    ppermute x4, waiting for transfers between devices, trade(): return lax.ppermute(planes, 'slab', pairs)  4 us
  transfers between devices with their start and end apart: 4, of which 2 were waited for; matrix products, arithmetic and copies ran while one was open for 0% of the time, Pallas kernels for 2%

profile of v4, /device:TPU:0, one launch (start us, length us, event | category | flops | bytes accessed | tf_op | source)
XLA Modules:
  0.0 103.6 jit_solution(16793686759256709869)
XLA Ops:
  0.6 0.0 copy-start
  0.6 1.0 copy-done
  1.6 0.0 copy-start.5
  1.6 1.0 copy-done.5
  2.6 3.1 %collective-permute-start.2 = (bf16[3,64,384]{2,1,0:T(8,128)(2,1)S(1)}, bf16[3,64,384]{2,1,0:T(8,128)(2,1)S(1)}, u32[]{:S(2)}, u32[]{:S(2)}) collective-permute-start(bf16[3,64,384]{2,1,0:T(8,128)(2,1)S(1)} %get-tuple-element.33), channel_id=1, source_target_pairs={{0,1},{1,0},{2,3},{3,2},{4,5},{5,4},{6,7},{7,6},{8,9},{9,8},{10,11... | collective-permute-start | bytes 442376 | tf_op jit(solution)/shard_map/ppermute | solution.py:478
  5.6 0.0 copy-start.2
  5.6 3.5 %collective-permute-start.3 = (bf16[3,64,384]{2,1,0:T(8,128)(2,1)S(1)}, bf16[3,64,384]{2,1,0:T(8,128)(2,1)S(1)}, u32[]{:S(2)}, u32[]{:S(2)}) collective-permute-start(bf16[3,64,384]{2,1,0:T(8,128)(2,1)S(1)} %get-tuple-element.34), channel_id=1, source_target_pairs={{0,7},{1,2},{2,1},{3,4},{4,3},{5,6},{6,5},{7,0},{8,15},{9,10},{10,... | collective-permute-start | bytes 442376 | tf_op jit(solution)/shard_map/ppermute | solution.py:478
  9.2 0.1 collective-permute-start
  9.3 1.9 %collective-permute-start.1 = (bf16[1,64,384]{2,1,0:T(8,128)(2,1)S(1)}, bf16[1,64,384]{2,1,0:T(8,128)(2,1)S(1)}, u32[]{:S(2)}, u32[]{:S(2)}) collective-permute-start(bf16[1,64,384]{2,1,0:T(8,128)(2,1)S(1)} %get-tuple-element.28), channel_id=1, source_target_pairs={{0,7},{1,2},{2,1},{3,4},{4,3},{5,6},{6,5},{7,0},{8,15},{9,10},{10,... | collective-permute-start | bytes 147464 | tf_op jit(solution)/shard_map/ppermute | solution.py:478
  11.2 0.0 copy-done.2
  11.2 0.9 shard_map.69
  12.1 3.1 %collective-permute-done.near_even = bf16[1,64,384]{2,1,0:T(8,128)(2,1)S(1)} collective-permute-done((bf16[1,64,384]{2,1,0:T(8,128)(2,1)S(1)}, bf16[1,64,384]{2,1,0:T(8,128)(2,1)S(1)}, u32[]{:S(2)}, u32[]{:S(2)}) %collective-permute-start) | collective-permute-done | bytes 49184 | tf_op jit(solution)/shard_map/ppermute | solution.py:478
  15.2 0.9 collective-permute-done.1.near_odd
  16.1 0.8 shard_map.70
  17.0 11.0 %all_to_all.54 = f32[8,1,128]{2,1,0:T(1,128)S(1)} all-to-all(f32[8,1,128]{2,1,0:T(1,128)S(1)} %bitcast.44), channel_id=1, replica_groups=mesh['pat'=4,'slab'=8] {'slab'}, dimensions={0} | all-to-all | bytes 8192 | tf_op jit(solution)/shard_map/all_to_all | solution.py:482
  27.9 0.0 collective-permute-done.2.far_even
  27.9 0.0 collective-permute-done.3.far_odd
  27.9 0.0 copy-start.1
  28.0 2.5 %shard_map.72 = (f32[8,64,384]{2,1,0:T(8,128)S(1)}, f32[8,128]{1,0:T(8,128)S(1)}, bf16[192,3840]{1,0:T(8,128)(2,1)S(1)}) custom-call(f32[8,128]{1,0:T(8,128)S(1)} %bitcast.36, f32[6,64,384]{2,1,0:T(8,128)S(1)} %get-tuple-element.32.first, bf16[3,64,384]{2,1,0:T(8,128)(2,1)S(1)} %collective-permute-done.2.far_even, ...), custom_call_target="tpu_custom_call" | custom-call | flops 849346560 | bytes 8409088 | tf_op jit(solution)/shard_map/pallas_call | solution.py:29
  30.4 8.9 %all_to_all.55 = f32[8,1,128]{2,1,0:T(1,128)S(1)} all-to-all(f32[8,1,128]{2,1,0:T(1,128)S(1)} %bitcast.43), channel_id=1, replica_groups=mesh['pat'=4,'slab'=8] {'slab'}, dimensions={0} | all-to-all | bytes 8192 | tf_op jit(solution)/shard_map/all_to_all | solution.py:482
  39.3 0.0 copy-done.1
  39.3 0.7 shard_map.73
  40.0 8.9 %all_to_all.56 = f32[8,1,128]{2,1,0:T(1,128)S(1)} all-to-all(f32[8,1,128]{2,1,0:T(1,128)S(1)} %bitcast.45), channel_id=1, replica_groups=mesh['pat'=4,'slab'=8] {'slab'}, dimensions={0} | all-to-all | bytes 8192 | tf_op jit(solution)/shard_map/all_to_all | solution.py:482
  48.8 1.6 %shard_map.74 = (bf16[6,64,384]{2,1,0:T(8,128)(2,1)S(1)}, f32[6,64,384]{2,1,0:T(8,128)S(1)}, f32[6,64,384]{2,1,0:T(8,128)S(1)}) custom-call(f32[8,128]{1,0:T(8,128)S(1)} %bitcast.37, f32[8,128]{1,0:T(8,128)S(1)} %bitcast.40, f32[8,128]{1,0:T(8,128)S(1)} %bitcast.42, f32[6,64,384]{2,1,0:T(8,128)S(1)} %get-tuple-element.32.first, ...), custom_call_target="tpu_custom_call" | custom-call | flops 679477248 | bytes 2396160 | tf_op jit(solution)/shard_map/pallas_call | solution.py:29
  50.4 3.3 %shard_map.75 = bf16[32,88,128]{2,1,0:T(8,128)(2,1)S(1)} custom-call(f32[8,128]{1,0:T(8,128)S(1)} %bitcast.38, f32[6,64,384]{2,1,0:T(8,128)S(1)} %get-tuple-element.42.normed_one, f32[6,64,384]{2,1,0:T(8,128)S(1)} %get-tuple-element.43.gradient_one, bf16[192,2304]{1,0:T(8,128)(2,1)S(1)} %get-tuple-element.44.own_stack, ...), custom_call_target="tpu_custom_call" | custom-call | flops 1528823808 | bytes 4132864 | tf_op jit(solution)/shard_map/pallas_call | solution.py:29
  53.7 0.0 copy-start.3
  53.7 0.0 copy-start.4
  53.7 22.3 %all_to_all.57.pieces = bf16[32,88,128]{2,1,0:T(8,128)(2,1)S(1)} all-to-all(bf16[32,88,128]{2,1,0:T(8,128)(2,1)S(1)} %shard_map.75), channel_id=1, replica_groups=mesh['pat'=4,'slab'=8] {'pat','slab'}, dimensions={0} | all-to-all | bytes 1441792 | tf_op jit(solution)/shard_map/all_to_all | solution.py:572
  76.0 0.9 shard_map.76
  76.9 9.2 %all_to_all.58 = f32[32,1,128]{2,1,0:T(1,128)S(1)} all-to-all(f32[32,1,128]{2,1,0:T(1,128)S(1)} %bitcast.41), channel_id=1, replica_groups=mesh['pat'=4,'slab'=8] {'pat','slab'}, dimensions={0} | all-to-all | bytes 32768 | tf_op jit(solution)/shard_map/all_to_all | solution.py:579
  86.1 0.1 shard_map.77
  86.2 9.6 %all_to_all.59 = bf16[8,56,128]{2,1,0:T(8,128)(2,1)S(1)} all-to-all(bf16[8,56,128]{2,1,0:T(8,128)(2,1)S(1)} %shard_map.77), channel_id=1, replica_groups=mesh['pat'=4,'slab'=8] {'slab'}, dimensions={0} | all-to-all | bytes 229376 | tf_op jit(solution)/shard_map/all_to_all | solution.py:581
  95.9 6.3 %all_gather.3.pieces = bf16[32,56,128]{2,1,0:T(8,128)(2,1)S(1)} all-gather(bf16[8,56,128]{2,1,0:T(8,128)(2,1)S(1)} %all_to_all.59), channel_id=1, replica_groups=mesh['pat'=4,'slab'=8] {'pat'}, dimensions={0}, use_global_device_ids=true | all-gather | bytes 573440 | tf_op jit(solution)/shard_map/all_gather | solution.py:581
  102.2 0.0 copy-done.3
  102.2 0.0 copy-done.4
  102.2 1.5 %shard_map.78 = (f32[128,1728]{1,0:T(8,128)}, f32[128,1728]{1,0:T(8,128)}) custom-call(bf16[32,56,128]{2,1,0:T(8,128)(2,1)S(1)} %all_gather.3.pieces, f32[128,1728]{1,0:T(8,128)S(1)} %bitcast.29, f32[128,1728]{1,0:T(8,128)S(1)} %bitcast.30, f32[128,1728]{1,0:T(8,128)S(1)} %bitcast.31), custom_call_target="tpu_custom_call" | custom-call | bytes 3112960 | tf_op jit(solution)/shard_map/pallas_call | solution.py:29
  (2 shorter events, 0.0 us)
Async XLA Ops:
  0.6 1.0 copy-start
  1.6 1.0 copy-start.5
  2.6 25.4 %collective-permute-start.2 = (bf16[3,64,384]{2,1,0:T(8,128)(2,1)S(1)}, bf16[3,64,384]{2,1,0:T(8,128)(2,1)S(1)}, u32[]{:S(2)}, u32[]{:S(2)}) collective-permute-start(bf16[3,64,384]{2,1,0:T(8,128)(2,1)S(1)} %get-tuple-element.33), channel_id=1, source_target_pairs={{0,1},{1,0},{2,3},{3,2},{4,5},{5,4},{6,7},{7,6},{8,9},{9,8},{10,11... | collective-permute-start | bytes 442376 | tf_op jit(solution)/shard_map/ppermute | solution.py:478
  5.6 5.5 %copy-start.2 = (f32[2,64,1728]{2,1,0:T(8,128)S(1)}, f32[2,64,1728]{2,1,0:T(8,128)}, u32[]{:S(2)}) copy-start(f32[2,64,1728]{2,1,0:T(8,128)} %weights.1) | copy-start | bytes 2654212
  5.6 22.3 %collective-permute-start.3 = (bf16[3,64,384]{2,1,0:T(8,128)(2,1)S(1)}, bf16[3,64,384]{2,1,0:T(8,128)(2,1)S(1)}, u32[]{:S(2)}, u32[]{:S(2)}) collective-permute-start(bf16[3,64,384]{2,1,0:T(8,128)(2,1)S(1)} %get-tuple-element.34), channel_id=1, source_target_pairs={{0,7},{1,2},{2,1},{3,4},{4,3},{5,6},{6,5},{7,0},{8,15},{9,10},{10,... | collective-permute-start | bytes 442376 | tf_op jit(solution)/shard_map/ppermute | solution.py:478
  9.2 6.0 %collective-permute-start = (bf16[1,64,384]{2,1,0:T(8,128)(2,1)S(1)}, bf16[1,64,384]{2,1,0:T(8,128)(2,1)S(1)}, u32[]{:S(2)}, u32[]{:S(2)}) collective-permute-start(bf16[1,64,384]{2,1,0:T(8,128)(2,1)S(1)} %get-tuple-element.27), channel_id=1, source_target_pairs={{0,1},{1,0},{2,3},{3,2},{4,5},{5,4},{6,7},{7,6},{8,9},{9,8},{10,11... | collective-permute-start | bytes 147464 | tf_op jit(solution)/shard_map/ppermute | solution.py:478
  9.3 6.9 %collective-permute-start.1 = (bf16[1,64,384]{2,1,0:T(8,128)(2,1)S(1)}, bf16[1,64,384]{2,1,0:T(8,128)(2,1)S(1)}, u32[]{:S(2)}, u32[]{:S(2)}) collective-permute-start(bf16[1,64,384]{2,1,0:T(8,128)(2,1)S(1)} %get-tuple-element.28), channel_id=1, source_target_pairs={{0,7},{1,2},{2,1},{3,4},{4,3},{5,6},{6,5},{7,0},{8,15},{9,10},{10,... | collective-permute-start | bytes 147464 | tf_op jit(solution)/shard_map/ppermute | solution.py:478
  27.9 11.3 %copy-start.1 = (bf16[1,64,6,384]{3,1,2,0:T(8,128)(2,1)S(1)}, bf16[1,64,6,384]{3,1,2,0:T(8,128)(2,1)}, u32[]{:S(2)}) copy-start(bf16[1,64,6,384]{3,1,2,0:T(8,128)(2,1)} %param.6) | copy-start | bytes 884740
  53.7 48.5 %copy-start.3 = (f32[2,64,1728]{2,1,0:T(8,128)S(1)}, f32[2,64,1728]{2,1,0:T(8,128)}, u32[]{:S(2)}) copy-start(f32[2,64,1728]{2,1,0:T(8,128)} %param.8) | copy-start | bytes 2654212
  53.7 48.5 %copy-start.4 = (f32[2,64,1728]{2,1,0:T(8,128)S(1)}, f32[2,64,1728]{2,1,0:T(8,128)}, u32[]{:S(2)}) copy-start(f32[2,64,1728]{2,1,0:T(8,128)} %param.9) | copy-start | bytes 2654212

commit v5 on v4

--- a/solution.py
+++ b/solution.py
@@ -52,8 +52,10 @@
     ).astype(bf16)
 
 
-def products(planes, kernel, stack, product):
+def products(planes, kernel, stack, product, trimmed=False):
     count = len(planes)
+    trimmed = trimmed and count % 2 == 0
+    third = kernel.shape[0] // 3
 
     def fill(z):
         plane = planes[z]() if callable(planes[z]) else planes[z]
@@ -67,7 +69,13 @@
         for ahead in range(z + 2, min(z + 4, count)):
             fill(ahead)
         span = slice(z * cells, min(z + 2, count) * cells)
-        product[:, span] = jnp.dot(kernel[...], stack[:, span], preferred_element_type=f32)
+        work = [(slice(None), span)]
+        if trimmed and z == 0:
+            work = [(slice(third), span), (slice(third, 2 * third), slice(cells, 2 * cells))]
+        elif trimmed and z == count - 2:
+            work = [(slice(2 * third, None), span), (slice(third, 2 * third), slice(z * cells, (z + 1) * cells))]
+        for rows, columns in work:
+            product[rows, columns] = jnp.dot(kernel[rows, :], stack[:, columns], preferred_element_type=f32)
 
 
 def tap(product, a, b, z, channels, cells):
@@ -222,7 +230,7 @@
     planes = [
         halo_plane(far_even, far_odd, z, before, slab, peers) for before in (True, False) for z in (0, 1)
     ]
-    products(planes, kernel, stack, product)
+    products(planes, kernel, stack, product, trimmed=True)
     where = {-3: 0, -2: 1, depth + 1: 2, depth + 2: 3}
 
     def part(a, b, z):
@@ -252,7 +260,7 @@
         normed = (source - centre) * spread
         return inside(z, 2, depth, slab, peers, (normed * sigmoid(normed)).astype(bf16))
 
-    products([functools.partial(plane, z) for z in range(depth + 4)], kernel, stack, product)
+    products([functools.partial(plane, z) for z in range(depth + 4)], kernel, stack, product, True)
     s = q = None
     for z in range(depth + 2):
         value = depth_sum(product, z, channels, cells)
@@ -298,7 +306,7 @@
             cotan_two[z - 1] = value
         return value
 
-    products([functools.partial(plane, z) for z in range(extended)], kernel, stack, product)
+    products([functools.partial(plane, z) for z in range(extended)], kernel, stack, product, True)
     centre, spread = moments(rows_one[...], cell_count)
     for z in range(depth):
         normed = (first[z] - centre) * spread
@@ -324,9 +332,9 @@
     return 8 * pl.cdiv(length + 7, 16)
 
 
-def three_parts(row):
+def parts_of(row, count):
     parts = []
-    for _ in range(3):
+    for _ in range(count):
         part = row.astype(bf16).astype(f32)
         parts.append(part)
         row = row - part
@@ -342,15 +350,19 @@
     length = gathered.shape[0] // count
     half = rows - length
     _, spread = moments(rows_one[...], cell_count)
-    s = q = None
+    s = q = m = v = None
     for z in range(depth):
-        s, q = add_to(s, gradient_one[z]), add_to(q, gradient_one[z] * normed_one[z])
-    s = jnp.sum(s, axis=1, keepdims=True)
-    q = jnp.sum(q, axis=1, keepdims=True)
-    mean, crossed = s / (depth * cells), q / (depth * cells)
+        grad, norm = gradient_one[z], normed_one[z]
+        s, q = add_to(s, grad), add_to(q, grad * norm)
+        m, v = add_to(m, norm), add_to(v, norm * norm)
+    s, q, m, v = (jnp.sum(x, axis=1, keepdims=True) for x in (s, q, m, v))
+    size = depth * cells
+    tilt = (q / size - s / size * (m / size)) / (v / size - m / size * (m / size) + 1.0)
+    tilt = tilt.astype(bf16).astype(f32)
+    level = (spread * (s / size - tilt * (m / size))).astype(bf16).astype(f32)
     centred, normed = [], []
     for z in range(depth):
-        value = spread * (gradient_one[z] - mean - normed_one[z] * crossed)
+        value = spread * (gradient_one[z] - normed_one[z] * tilt) - level
         centred.append(value.astype(bf16))
         normed.append((spread * normed_one[z]).astype(bf16))
     stack[:, :cells] = near_stack[:, :cells]
@@ -385,10 +397,12 @@
         start = channels + b * 3 * width
         ones_rows[:, start : start + 3 * width] = turned[b : b + 1, :]
     ones_rows[:, channels + total :] = jnp.zeros((1, ones_rows.shape[1] - channels - total), f32)
-    row = to_row(spread * s, q)
-    sums = three_parts(row)
+    totals, fit = to_row(spread * s, q), to_row(level, tilt)
     tail = jnp.concatenate(
-        [pltpu.roll(part, channels, 1) for part in sums] + sums + [jnp.zeros((1, lanes), f32)], axis=0
+        [pltpu.roll(part, channels, 1) for part in parts_of(totals, 3)]
+        + parts_of(totals, 2)
+        + [pltpu.roll(fit, channels, 1), fit],
+        axis=0,
     )
     left = lax.broadcasted_iota(jnp.int32, (half, lanes), 1) < channels
     for j in range(count):
@@ -411,24 +425,26 @@
     peers = count // patients
     start = length + max(length - half, 0)
     further = jnp.concatenate([pieces[c, start : start + 8] for c in range(count)], axis=0)
-    target = lax.broadcasted_iota(jnp.int32, (3 * count, 8 * count), 0)
-    source = lax.broadcasted_iota(jnp.int32, (3 * count, 8 * count), 1)
-    offset = source - 8 * (target % count)
-    part = target // count
-    picked = (offset >= 3 * part) & (offset < 3 * part + 3) & (part < 2) | (part == 2) & (offset == 7)
+    starts = (0, 3, 5, 6, 7, 8)
+    kinds = len(starts) - 1
+    target = lax.broadcasted_iota(jnp.int32, (kinds * count, 8 * count), 0)
+    offset = lax.broadcasted_iota(jnp.int32, (kinds * count, 8 * count), 1) - 8 * (target % count)
+    picked = offset < 0
+    for at in range(kinds):
+        picked |= (target // count == at) & (offset >= starts[at]) & (offset < starts[at + 1])
+    picked &= offset >= 0
     picks = jnp.dot(jnp.where(picked, 1.0, 0.0).astype(bf16), further, preferred_element_type=f32)
-    lower = lax.broadcasted_iota(jnp.int32, (3 * count, lanes), 1) < channels
+    lower = lax.broadcasted_iota(jnp.int32, (kinds * count, lanes), 1) < channels
     picks = jnp.where(lower, pltpu.roll(picks, channels, 1), 0.0)
 
     lane = lax.broadcasted_iota(jnp.int32, (1, squares.shape[1]), 1)
     row = jnp.zeros((1, squares.shape[1]), f32)
     for p in range(patients):
-        means, crosses, ones = (
-            picks[at * count + p * peers : at * count + (p + 1) * peers] for at in range(3)
+        means, crosses, levels, tilts, ones = (
+            picks[at * count + p * peers : at * count + (p + 1) * peers] for at in range(kinds)
         )
-        means, crosses = (
-            jnp.sum(x, axis=0, keepdims=True) / (cells * peers) - x / cells for x in (means, crosses)
-        )
+        means = jnp.sum(means, axis=0, keepdims=True) / (cells * peers) - levels
+        crosses = jnp.sum(crosses, axis=0, keepdims=True) / (cells * peers) - tilts
         total = -lax.dot_general(
             ones, means, (((0,), (0,)), ((), ())), precision=lax.Precision.HIGHEST, preferred_element_type=f32
         )[:length]

time: 104 us -> 104 us (level)
  no operation moved by 1% of the time
where the time goes in v5:
time: 104 us; the launch traced here: 103 us
  blocking collectives  76.1 us (73%)
  Pallas kernels  11.8 us (11%)
  starting transfers between devices  8.57 us (8%)
  waiting for transfers between devices  4 us (4%)
  local copies, waits for them, and re-layouts  1.94 us (2%)
    all_to_all x3, blocking collectives, exchange(): return lax.all_to_all(rows, 'slab', 0, 0)  28.7 us
    all_to_all x1, blocking collectives, per_device(): pieces = lax.all_to_all(pieces, AXES, 0, 0)  22.3 us
    pallas_call x11, Pallas kernels, call(): pl.pallas_call(kernel, out_shape=out_shape, in_specs=[vmem] * len(args),...  11.8 us
    all_to_all x1, blocking collectives, per_device(): lax.all_to_all(pieces, 'slab', 0, 0)  9.62 us
    all_to_all x1, blocking collectives, per_device(): squares = lax.all_to_all(squares, AXES, 0, 0)  9.22 us
    ppermute x4, starting transfers between devices, trade(): return lax.ppermute(planes, 'slab', pairs)  8.57 us
    all_gather x1, blocking collectives, per_device(): lax.all_gather(lax.all_to_all(pieces, 'slab', 0, 0), 'pat', tiled=True)  6.31 us
    ppermute x4, waiting for transfers between devices, trade(): return lax.ppermute(planes, 'slab', pairs)  4 us
  transfers between devices with their start and end apart: 4, of which 2 were waited for; matrix products, arithmetic and copies ran while one was open for 0% of the time, Pallas kernels for 2%

profile of v5, /device:TPU:0, one launch (start us, length us, event | category | flops | bytes accessed | tf_op | source)
XLA Modules:
  0.0 103.1 jit_solution(12395623493929555983)
XLA Ops:
  0.6 0.0 copy-start
  0.6 1.0 copy-done
  1.6 0.0 copy-start.5
  1.6 1.0 copy-done.5
  2.6 3.1 %collective-permute-start.2 = (bf16[3,64,384]{2,1,0:T(8,128)(2,1)S(1)}, bf16[3,64,384]{2,1,0:T(8,128)(2,1)S(1)}, u32[]{:S(2)}, u32[]{:S(2)}) collective-permute-start(bf16[3,64,384]{2,1,0:T(8,128)(2,1)S(1)} %get-tuple-element.33), channel_id=1, source_target_pairs={{0,1},{1,0},{2,3},{3,2},{4,5},{5,4},{6,7},{7,6},{8,9},{9,8},{10,11... | collective-permute-start | bytes 442376 | tf_op jit(solution)/shard_map/ppermute | solution.py:494
  5.6 0.0 copy-start.2
  5.6 3.5 %collective-permute-start.3 = (bf16[3,64,384]{2,1,0:T(8,128)(2,1)S(1)}, bf16[3,64,384]{2,1,0:T(8,128)(2,1)S(1)}, u32[]{:S(2)}, u32[]{:S(2)}) collective-permute-start(bf16[3,64,384]{2,1,0:T(8,128)(2,1)S(1)} %get-tuple-element.34), channel_id=1, source_target_pairs={{0,7},{1,2},{2,1},{3,4},{4,3},{5,6},{6,5},{7,0},{8,15},{9,10},{10,... | collective-permute-start | bytes 442376 | tf_op jit(solution)/shard_map/ppermute | solution.py:494
  9.2 0.1 collective-permute-start
  9.3 1.9 %collective-permute-start.1 = (bf16[1,64,384]{2,1,0:T(8,128)(2,1)S(1)}, bf16[1,64,384]{2,1,0:T(8,128)(2,1)S(1)}, u32[]{:S(2)}, u32[]{:S(2)}) collective-permute-start(bf16[1,64,384]{2,1,0:T(8,128)(2,1)S(1)} %get-tuple-element.28), channel_id=1, source_target_pairs={{0,7},{1,2},{2,1},{3,4},{4,3},{5,6},{6,5},{7,0},{8,15},{9,10},{10,... | collective-permute-start | bytes 147464 | tf_op jit(solution)/shard_map/ppermute | solution.py:494
  11.2 0.0 copy-done.2
  11.2 0.9 shard_map.69
  12.1 3.1 %collective-permute-done.near_even = bf16[1,64,384]{2,1,0:T(8,128)(2,1)S(1)} collective-permute-done((bf16[1,64,384]{2,1,0:T(8,128)(2,1)S(1)}, bf16[1,64,384]{2,1,0:T(8,128)(2,1)S(1)}, u32[]{:S(2)}, u32[]{:S(2)}) %collective-permute-start) | collective-permute-done | bytes 49184 | tf_op jit(solution)/shard_map/ppermute | solution.py:494
  15.2 0.9 collective-permute-done.1.near_odd
  16.1 0.8 shard_map.70
  17.0 11.0 %all_to_all.54 = f32[8,1,128]{2,1,0:T(1,128)S(1)} all-to-all(f32[8,1,128]{2,1,0:T(1,128)S(1)} %bitcast.44), channel_id=1, replica_groups=mesh['pat'=4,'slab'=8] {'slab'}, dimensions={0} | all-to-all | bytes 8192 | tf_op jit(solution)/shard_map/all_to_all | solution.py:498
  27.9 0.0 collective-permute-done.2.far_even
  27.9 0.0 collective-permute-done.3.far_odd
  27.9 0.0 copy-start.1
  28.0 2.3 %shard_map.72 = (f32[8,64,384]{2,1,0:T(8,128)S(1)}, f32[8,128]{1,0:T(8,128)S(1)}, bf16[192,3840]{1,0:T(8,128)(2,1)S(1)}) custom-call(f32[8,128]{1,0:T(8,128)S(1)} %bitcast.36, f32[6,64,384]{2,1,0:T(8,128)S(1)} %get-tuple-element.32.first, bf16[3,64,384]{2,1,0:T(8,128)(2,1)S(1)} %collective-permute-done.2.far_even, ...), custom_call_target="tpu_custom_call" | custom-call | flops 849346560 | bytes 8409088 | tf_op jit(solution)/shard_map/pallas_call | solution.py:29
  30.2 8.9 %all_to_all.55 = f32[8,1,128]{2,1,0:T(1,128)S(1)} all-to-all(f32[8,1,128]{2,1,0:T(1,128)S(1)} %bitcast.43), channel_id=1, replica_groups=mesh['pat'=4,'slab'=8] {'slab'}, dimensions={0} | all-to-all | bytes 8192 | tf_op jit(solution)/shard_map/all_to_all | solution.py:498
  39.1 0.0 copy-done.1
  39.1 0.7 shard_map.73
  39.8 8.9 %all_to_all.56 = f32[8,1,128]{2,1,0:T(1,128)S(1)} all-to-all(f32[8,1,128]{2,1,0:T(1,128)S(1)} %bitcast.45), channel_id=1, replica_groups=mesh['pat'=4,'slab'=8] {'slab'}, dimensions={0} | all-to-all | bytes 8192 | tf_op jit(solution)/shard_map/all_to_all | solution.py:498
  48.6 1.4 %shard_map.74 = (bf16[6,64,384]{2,1,0:T(8,128)(2,1)S(1)}, f32[6,64,384]{2,1,0:T(8,128)S(1)}, f32[6,64,384]{2,1,0:T(8,128)S(1)}) custom-call(f32[8,128]{1,0:T(8,128)S(1)} %bitcast.37, f32[8,128]{1,0:T(8,128)S(1)} %bitcast.40, f32[8,128]{1,0:T(8,128)S(1)} %bitcast.42, f32[6,64,384]{2,1,0:T(8,128)S(1)} %get-tuple-element.32.first, ...), custom_call_target="tpu_custom_call" | custom-call | flops 679477248 | bytes 2396160 | tf_op jit(solution)/shard_map/pallas_call | solution.py:29
  50.1 3.3 %shard_map.75 = bf16[32,88,128]{2,1,0:T(8,128)(2,1)S(1)} custom-call(f32[8,128]{1,0:T(8,128)S(1)} %bitcast.38, f32[6,64,384]{2,1,0:T(8,128)S(1)} %get-tuple-element.42.normed_one, f32[6,64,384]{2,1,0:T(8,128)S(1)} %get-tuple-element.43.gradient_one, bf16[192,2304]{1,0:T(8,128)(2,1)S(1)} %get-tuple-element.44.own_stack, ...), custom_call_target="tpu_custom_call" | custom-call | flops 1528823808 | bytes 4132864 | tf_op jit(solution)/shard_map/pallas_call | solution.py:29
  53.3 0.0 copy-start.3
  53.3 0.0 copy-start.4
  53.3 22.3 %all_to_all.57.pieces = bf16[32,88,128]{2,1,0:T(8,128)(2,1)S(1)} all-to-all(bf16[32,88,128]{2,1,0:T(8,128)(2,1)S(1)} %shard_map.75), channel_id=1, replica_groups=mesh['pat'=4,'slab'=8] {'pat','slab'}, dimensions={0} | all-to-all | bytes 1441792 | tf_op jit(solution)/shard_map/all_to_all | solution.py:588
  75.6 0.8 shard_map.76
  76.4 9.2 %all_to_all.58 = f32[32,1,128]{2,1,0:T(1,128)S(1)} all-to-all(f32[32,1,128]{2,1,0:T(1,128)S(1)} %bitcast.41), channel_id=1, replica_groups=mesh['pat'=4,'slab'=8] {'pat','slab'}, dimensions={0} | all-to-all | bytes 32768 | tf_op jit(solution)/shard_map/all_to_all | solution.py:595
  85.6 0.1 shard_map.77
  85.7 9.6 %all_to_all.59 = bf16[8,56,128]{2,1,0:T(8,128)(2,1)S(1)} all-to-all(bf16[8,56,128]{2,1,0:T(8,128)(2,1)S(1)} %shard_map.77), channel_id=1, replica_groups=mesh['pat'=4,'slab'=8] {'slab'}, dimensions={0} | all-to-all | bytes 229376 | tf_op jit(solution)/shard_map/all_to_all | solution.py:597
  95.4 6.3 %all_gather.3.pieces = bf16[32,56,128]{2,1,0:T(8,128)(2,1)S(1)} all-gather(bf16[8,56,128]{2,1,0:T(8,128)(2,1)S(1)} %all_to_all.59), channel_id=1, replica_groups=mesh['pat'=4,'slab'=8] {'pat'}, dimensions={0}, use_global_device_ids=true | all-gather | bytes 573440 | tf_op jit(solution)/shard_map/all_gather | solution.py:597
  101.7 0.0 copy-done.3
  101.7 0.0 copy-done.4
  101.7 1.5 %shard_map.78 = (f32[128,1728]{1,0:T(8,128)}, f32[128,1728]{1,0:T(8,128)}) custom-call(bf16[32,56,128]{2,1,0:T(8,128)(2,1)S(1)} %all_gather.3.pieces, f32[128,1728]{1,0:T(8,128)S(1)} %bitcast.29, f32[128,1728]{1,0:T(8,128)S(1)} %bitcast.30, f32[128,1728]{1,0:T(8,128)S(1)} %bitcast.31), custom_call_target="tpu_custom_call" | custom-call | bytes 3112960 | tf_op jit(solution)/shard_map/pallas_call | solution.py:29
  (2 shorter events, 0.0 us)
Async XLA Ops:
  0.6 1.0 copy-start
  1.6 1.0 copy-start.5
  2.6 25.4 %collective-permute-start.2 = (bf16[3,64,384]{2,1,0:T(8,128)(2,1)S(1)}, bf16[3,64,384]{2,1,0:T(8,128)(2,1)S(1)}, u32[]{:S(2)}, u32[]{:S(2)}) collective-permute-start(bf16[3,64,384]{2,1,0:T(8,128)(2,1)S(1)} %get-tuple-element.33), channel_id=1, source_target_pairs={{0,1},{1,0},{2,3},{3,2},{4,5},{5,4},{6,7},{7,6},{8,9},{9,8},{10,11... | collective-permute-start | bytes 442376 | tf_op jit(solution)/shard_map/ppermute | solution.py:494
  5.6 5.5 %copy-start.2 = (f32[2,64,1728]{2,1,0:T(8,128)S(1)}, f32[2,64,1728]{2,1,0:T(8,128)}, u32[]{:S(2)}) copy-start(f32[2,64,1728]{2,1,0:T(8,128)} %weights.1) | copy-start | bytes 2654212
  5.6 22.3 %collective-permute-start.3 = (bf16[3,64,384]{2,1,0:T(8,128)(2,1)S(1)}, bf16[3,64,384]{2,1,0:T(8,128)(2,1)S(1)}, u32[]{:S(2)}, u32[]{:S(2)}) collective-permute-start(bf16[3,64,384]{2,1,0:T(8,128)(2,1)S(1)} %get-tuple-element.34), channel_id=1, source_target_pairs={{0,7},{1,2},{2,1},{3,4},{4,3},{5,6},{6,5},{7,0},{8,15},{9,10},{10,... | collective-permute-start | bytes 442376 | tf_op jit(solution)/shard_map/ppermute | solution.py:494
  9.2 6.0 %collective-permute-start = (bf16[1,64,384]{2,1,0:T(8,128)(2,1)S(1)}, bf16[1,64,384]{2,1,0:T(8,128)(2,1)S(1)}, u32[]{:S(2)}, u32[]{:S(2)}) collective-permute-start(bf16[1,64,384]{2,1,0:T(8,128)(2,1)S(1)} %get-tuple-element.27), channel_id=1, source_target_pairs={{0,1},{1,0},{2,3},{3,2},{4,5},{5,4},{6,7},{7,6},{8,9},{9,8},{10,11... | collective-permute-start | bytes 147464 | tf_op jit(solution)/shard_map/ppermute | solution.py:494
  9.3 6.9 %collective-permute-start.1 = (bf16[1,64,384]{2,1,0:T(8,128)(2,1)S(1)}, bf16[1,64,384]{2,1,0:T(8,128)(2,1)S(1)}, u32[]{:S(2)}, u32[]{:S(2)}) collective-permute-start(bf16[1,64,384]{2,1,0:T(8,128)(2,1)S(1)} %get-tuple-element.28), channel_id=1, source_target_pairs={{0,7},{1,2},{2,1},{3,4},{4,3},{5,6},{6,5},{7,0},{8,15},{9,10},{10,... | collective-permute-start | bytes 147464 | tf_op jit(solution)/shard_map/ppermute | solution.py:494
  27.9 11.1 %copy-start.1 = (bf16[1,64,6,384]{3,1,2,0:T(8,128)(2,1)S(1)}, bf16[1,64,6,384]{3,1,2,0:T(8,128)(2,1)}, u32[]{:S(2)}) copy-start(bf16[1,64,6,384]{3,1,2,0:T(8,128)(2,1)} %param.6) | copy-start | bytes 884740
  53.3 48.4 %copy-start.3 = (f32[2,64,1728]{2,1,0:T(8,128)S(1)}, f32[2,64,1728]{2,1,0:T(8,128)}, u32[]{:S(2)}) copy-start(f32[2,64,1728]{2,1,0:T(8,128)} %param.8) | copy-start | bytes 2654212
  53.3 48.4 %copy-start.4 = (f32[2,64,1728]{2,1,0:T(8,128)S(1)}, f32[2,64,1728]{2,1,0:T(8,128)}, u32[]{:S(2)}) copy-start(f32[2,64,1728]{2,1,0:T(8,128)} %param.9) | copy-start | bytes 2654212

commit v6 on v5

--- a/solution.py
+++ b/solution.py
@@ -472,7 +472,7 @@
         pieces[j] = rounded
 
 
-def update(pieces, weights, prev_state, tree_noise, state_next, weights_next, gathered):
+def update(pieces, weights, prev_state, tree_noise, state_next, weights_next, gathered, state, kernels, sems):
     count, length, lanes = pieces.shape
     width = 3 * (lanes // 2)
     for j in range(count):
@@ -482,12 +482,19 @@
         row = (at % 3 * 3 + at // 3) * width
         return gathered[row : row + width, :]
 
+    copies = []
     for at in range(0, 9, 2):
         group = range(at, min(at + 2, 9))
         span = slice(at * width, (group[-1] + 1) * width)
         combined = jnp.concatenate([block(i) for i in group], axis=0).T
-        state_next[:, span] = prev_state[:, span] + combined
-        weights_next[:, span] = weights[:, span] - step_rate * (combined + tree_noise[:, span])
+        state[:, span] = prev_state[:, span] + combined
+        kernels[:, span] = weights[:, span] - step_rate * (combined + tree_noise[:, span])
+        for source, target in ((state, state_next), (kernels, weights_next)):
+            copy = pltpu.make_async_copy(source.at[:, span], target.at[:, span], sems.at[len(copies)])
+            copy.start()
+            copies.append(copy)
+    for copy in copies:
+        copy.wait()
 
 
 def trade(planes, pairs):
@@ -596,12 +603,20 @@
     pieces = call(functools.partial(clipped, patients), pieces_shape, squares, sums)
     pieces = lax.all_gather(lax.all_to_all(pieces, "slab", 0, 0), "pat", tiled=True)
     flat = (2 * channels, columns)
-    state_next, weights_next = call(
+    vmem, hbm = pl.BlockSpec(memory_space=pltpu.VMEM), pl.BlockSpec(memory_space=pl.ANY)
+    state_next, weights_next = pl.pallas_call(
         update,
-        (sds(flat, f32), sds(flat, f32)),
-        pieces, weights.reshape(flat), prev_state.reshape(flat), tree_noise.reshape(flat),
-        scratch=[pltpu.VMEM((devices * length, 2 * channels), f32)],
-    )
+        out_shape=(sds(flat, f32), sds(flat, f32)),
+        in_specs=[vmem] * 4,
+        out_specs=(hbm, hbm),
+        scratch_shapes=[
+            pltpu.VMEM((devices * length, 2 * channels), f32),
+            pltpu.VMEM(flat, f32),
+            pltpu.VMEM(flat, f32),
+            pltpu.SemaphoreType.DMA((10,)),
+        ],
+        compiler_params=pltpu.CompilerParams(vmem_limit_bytes=18 * 2**20),
+    )(pieces, weights.reshape(flat), prev_state.reshape(flat), tree_noise.reshape(flat))
     return (state_next.reshape(weights.shape), weights_next.reshape(weights.shape))
 
 

time: 104 us -> 103 us (level)
    pallas_call x11 -> x10, Pallas kernels: 11.8 us -> 10.3 us  [call(): pl.pallas_call(kernel, out_shape=out_shape, in_specs=[vmem] * len(args),...]
    pallas_call x0 -> x1, Pallas kernels: none -> 1.42 us  [per_device(): pl.pallas_call(update, out_shape=(sds(flat, f32), sds(flat, f32)), in_spe...]
where the time goes in v6:
time: 103 us
  blocking collectives  76.1 us (74%)
  Pallas kernels  11.7 us (11%)
  starting transfers between devices  8.57 us (8%)
  waiting for transfers between devices  4 us (4%)
  local copies, waits for them, and re-layouts  1.94 us (2%)
    all_to_all x3, blocking collectives, exchange(): return lax.all_to_all(rows, 'slab', 0, 0)  28.7 us
    all_to_all x1, blocking collectives, per_device(): pieces = lax.all_to_all(pieces, AXES, 0, 0)  22.3 us
    pallas_call x10, Pallas kernels, call(): pl.pallas_call(kernel, out_shape=out_shape, in_specs=[vmem] * len(args),...  10.3 us
    all_to_all x1, blocking collectives, per_device(): lax.all_to_all(pieces, 'slab', 0, 0)  9.62 us
    all_to_all x1, blocking collectives, per_device(): squares = lax.all_to_all(squares, AXES, 0, 0)  9.22 us
    ppermute x4, starting transfers between devices, trade(): return lax.ppermute(planes, 'slab', pairs)  8.57 us
    all_gather x1, blocking collectives, per_device(): lax.all_gather(lax.all_to_all(pieces, 'slab', 0, 0), 'pat', tiled=True)  6.31 us
    ppermute x4, waiting for transfers between devices, trade(): return lax.ppermute(planes, 'slab', pairs)  4 us
  transfers between devices with their start and end apart: 4, of which 2 were waited for; matrix products, arithmetic and copies ran while one was open for 0% of the time, Pallas kernels for 2%

profile of v6, /device:TPU:0, one launch (start us, length us, event | category | flops | bytes accessed | tf_op | source)
XLA Modules:
  0.0 103.1 jit_solution(12464169124398985231)
XLA Ops:
  0.6 0.0 copy-start
  0.6 1.0 copy-done
  1.6 0.0 copy-start.5
  1.6 1.0 copy-done.5
  2.6 3.1 %collective-permute-start.2 = (bf16[3,64,384]{2,1,0:T(8,128)(2,1)S(1)}, bf16[3,64,384]{2,1,0:T(8,128)(2,1)S(1)}, u32[]{:S(2)}, u32[]{:S(2)}) collective-permute-start(bf16[3,64,384]{2,1,0:T(8,128)(2,1)S(1)} %get-tuple-element.33), channel_id=1, source_target_pairs={{0,1},{1,0},{2,3},{3,2},{4,5},{5,4},{6,7},{7,6},{8,9},{9,8},{10,11... | collective-permute-start | bytes 442376 | tf_op jit(solution)/shard_map/ppermute | solution.py:501
  5.6 0.0 copy-start.2
  5.6 3.5 %collective-permute-start.3 = (bf16[3,64,384]{2,1,0:T(8,128)(2,1)S(1)}, bf16[3,64,384]{2,1,0:T(8,128)(2,1)S(1)}, u32[]{:S(2)}, u32[]{:S(2)}) collective-permute-start(bf16[3,64,384]{2,1,0:T(8,128)(2,1)S(1)} %get-tuple-element.34), channel_id=1, source_target_pairs={{0,7},{1,2},{2,1},{3,4},{4,3},{5,6},{6,5},{7,0},{8,15},{9,10},{10,... | collective-permute-start | bytes 442376 | tf_op jit(solution)/shard_map/ppermute | solution.py:501
  9.2 0.1 collective-permute-start
  9.3 1.9 %collective-permute-start.1 = (bf16[1,64,384]{2,1,0:T(8,128)(2,1)S(1)}, bf16[1,64,384]{2,1,0:T(8,128)(2,1)S(1)}, u32[]{:S(2)}, u32[]{:S(2)}) collective-permute-start(bf16[1,64,384]{2,1,0:T(8,128)(2,1)S(1)} %get-tuple-element.28), channel_id=1, source_target_pairs={{0,7},{1,2},{2,1},{3,4},{4,3},{5,6},{6,5},{7,0},{8,15},{9,10},{10,... | collective-permute-start | bytes 147464 | tf_op jit(solution)/shard_map/ppermute | solution.py:501
  11.2 0.0 copy-done.2
  11.2 0.9 shard_map.69
  12.1 3.1 %collective-permute-done.near_even = bf16[1,64,384]{2,1,0:T(8,128)(2,1)S(1)} collective-permute-done((bf16[1,64,384]{2,1,0:T(8,128)(2,1)S(1)}, bf16[1,64,384]{2,1,0:T(8,128)(2,1)S(1)}, u32[]{:S(2)}, u32[]{:S(2)}) %collective-permute-start) | collective-permute-done | bytes 49184 | tf_op jit(solution)/shard_map/ppermute | solution.py:501
  15.2 0.9 collective-permute-done.1.near_odd
  16.1 0.8 shard_map.70
  17.0 11.0 %all_to_all.54 = f32[8,1,128]{2,1,0:T(1,128)S(1)} all-to-all(f32[8,1,128]{2,1,0:T(1,128)S(1)} %bitcast.44), channel_id=1, replica_groups=mesh['pat'=4,'slab'=8] {'slab'}, dimensions={0} | all-to-all | bytes 8192 | tf_op jit(solution)/shard_map/all_to_all | solution.py:505
  27.9 0.0 collective-permute-done.2.far_even
  27.9 0.0 collective-permute-done.3.far_odd
  27.9 0.0 copy-start.1
  28.0 2.3 %shard_map.72 = (f32[8,64,384]{2,1,0:T(8,128)S(1)}, f32[8,128]{1,0:T(8,128)S(1)}, bf16[192,3840]{1,0:T(8,128)(2,1)S(1)}) custom-call(f32[8,128]{1,0:T(8,128)S(1)} %bitcast.36, f32[6,64,384]{2,1,0:T(8,128)S(1)} %get-tuple-element.32.first, bf16[3,64,384]{2,1,0:T(8,128)(2,1)S(1)} %collective-permute-done.2.far_even, ...), custom_call_target="tpu_custom_call" | custom-call | flops 849346560 | bytes 8409088 | tf_op jit(solution)/shard_map/pallas_call | solution.py:29
  30.2 8.9 %all_to_all.55 = f32[8,1,128]{2,1,0:T(1,128)S(1)} all-to-all(f32[8,1,128]{2,1,0:T(1,128)S(1)} %bitcast.43), channel_id=1, replica_groups=mesh['pat'=4,'slab'=8] {'slab'}, dimensions={0} | all-to-all | bytes 8192 | tf_op jit(solution)/shard_map/all_to_all | solution.py:505
  39.1 0.0 copy-done.1
  39.1 0.7 shard_map.73
  39.8 8.9 %all_to_all.56 = f32[8,1,128]{2,1,0:T(1,128)S(1)} all-to-all(f32[8,1,128]{2,1,0:T(1,128)S(1)} %bitcast.45), channel_id=1, replica_groups=mesh['pat'=4,'slab'=8] {'slab'}, dimensions={0} | all-to-all | bytes 8192 | tf_op jit(solution)/shard_map/all_to_all | solution.py:505
  48.6 1.4 %shard_map.74 = (bf16[6,64,384]{2,1,0:T(8,128)(2,1)S(1)}, f32[6,64,384]{2,1,0:T(8,128)S(1)}, f32[6,64,384]{2,1,0:T(8,128)S(1)}) custom-call(f32[8,128]{1,0:T(8,128)S(1)} %bitcast.37, f32[8,128]{1,0:T(8,128)S(1)} %bitcast.40, f32[8,128]{1,0:T(8,128)S(1)} %bitcast.42, f32[6,64,384]{2,1,0:T(8,128)S(1)} %get-tuple-element.32.first, ...), custom_call_target="tpu_custom_call" | custom-call | flops 679477248 | bytes 2396160 | tf_op jit(solution)/shard_map/pallas_call | solution.py:29
  50.1 3.3 %shard_map.75 = bf16[32,88,128]{2,1,0:T(8,128)(2,1)S(1)} custom-call(f32[8,128]{1,0:T(8,128)S(1)} %bitcast.38, f32[6,64,384]{2,1,0:T(8,128)S(1)} %get-tuple-element.42.normed_one, f32[6,64,384]{2,1,0:T(8,128)S(1)} %get-tuple-element.43.gradient_one, bf16[192,2304]{1,0:T(8,128)(2,1)S(1)} %get-tuple-element.44.own_stack, ...), custom_call_target="tpu_custom_call" | custom-call | flops 1528823808 | bytes 4132864 | tf_op jit(solution)/shard_map/pallas_call | solution.py:29
  53.3 0.0 copy-start.3
  53.3 0.0 copy-start.4
  53.3 22.3 %all_to_all.57.pieces = bf16[32,88,128]{2,1,0:T(8,128)(2,1)S(1)} all-to-all(bf16[32,88,128]{2,1,0:T(8,128)(2,1)S(1)} %shard_map.75), channel_id=1, replica_groups=mesh['pat'=4,'slab'=8] {'pat','slab'}, dimensions={0} | all-to-all | bytes 1441792 | tf_op jit(solution)/shard_map/all_to_all | solution.py:595
  75.6 0.8 shard_map.76
  76.4 9.2 %all_to_all.58 = f32[32,1,128]{2,1,0:T(1,128)S(1)} all-to-all(f32[32,1,128]{2,1,0:T(1,128)S(1)} %bitcast.41), channel_id=1, replica_groups=mesh['pat'=4,'slab'=8] {'pat','slab'}, dimensions={0} | all-to-all | bytes 32768 | tf_op jit(solution)/shard_map/all_to_all | solution.py:602
  85.6 0.1 shard_map.77
  85.7 9.6 %all_to_all.59 = bf16[8,56,128]{2,1,0:T(8,128)(2,1)S(1)} all-to-all(bf16[8,56,128]{2,1,0:T(8,128)(2,1)S(1)} %shard_map.77), channel_id=1, replica_groups=mesh['pat'=4,'slab'=8] {'slab'}, dimensions={0} | all-to-all | bytes 229376 | tf_op jit(solution)/shard_map/all_to_all | solution.py:604
  95.4 6.3 %all_gather.3.pieces = bf16[32,56,128]{2,1,0:T(8,128)(2,1)S(1)} all-gather(bf16[8,56,128]{2,1,0:T(8,128)(2,1)S(1)} %all_to_all.59), channel_id=1, replica_groups=mesh['pat'=4,'slab'=8] {'pat'}, dimensions={0}, use_global_device_ids=true | all-gather | bytes 573440 | tf_op jit(solution)/shard_map/all_gather | solution.py:604
  101.7 0.0 copy-done.3
  101.7 0.0 copy-done.4
  101.7 1.4 %shard_map.78 = (f32[128,1728]{1,0:T(8,128)}, f32[128,1728]{1,0:T(8,128)}) custom-call(bf16[32,56,128]{2,1,0:T(8,128)(2,1)S(1)} %all_gather.3.pieces, f32[128,1728]{1,0:T(8,128)S(1)} %bitcast.29, f32[128,1728]{1,0:T(8,128)S(1)} %bitcast.30, f32[128,1728]{1,0:T(8,128)S(1)} %bitcast.31), custom_call_target="tpu_custom_call" | custom-call | tf_op jit(solution)/shard_map/pallas_call | solution.py:607
  (2 shorter events, 0.0 us)
Async XLA Ops:
  0.6 1.0 copy-start
  1.6 1.0 copy-start.5
  2.6 25.4 %collective-permute-start.2 = (bf16[3,64,384]{2,1,0:T(8,128)(2,1)S(1)}, bf16[3,64,384]{2,1,0:T(8,128)(2,1)S(1)}, u32[]{:S(2)}, u32[]{:S(2)}) collective-permute-start(bf16[3,64,384]{2,1,0:T(8,128)(2,1)S(1)} %get-tuple-element.33), channel_id=1, source_target_pairs={{0,1},{1,0},{2,3},{3,2},{4,5},{5,4},{6,7},{7,6},{8,9},{9,8},{10,11... | collective-permute-start | bytes 442376 | tf_op jit(solution)/shard_map/ppermute | solution.py:501
  5.6 5.5 %copy-start.2 = (f32[2,64,1728]{2,1,0:T(8,128)S(1)}, f32[2,64,1728]{2,1,0:T(8,128)}, u32[]{:S(2)}) copy-start(f32[2,64,1728]{2,1,0:T(8,128)} %weights.1) | copy-start | bytes 2654212
  5.6 22.3 %collective-permute-start.3 = (bf16[3,64,384]{2,1,0:T(8,128)(2,1)S(1)}, bf16[3,64,384]{2,1,0:T(8,128)(2,1)S(1)}, u32[]{:S(2)}, u32[]{:S(2)}) collective-permute-start(bf16[3,64,384]{2,1,0:T(8,128)(2,1)S(1)} %get-tuple-element.34), channel_id=1, source_target_pairs={{0,7},{1,2},{2,1},{3,4},{4,3},{5,6},{6,5},{7,0},{8,15},{9,10},{10,... | collective-permute-start | bytes 442376 | tf_op jit(solution)/shard_map/ppermute | solution.py:501
  9.2 6.0 %collective-permute-start = (bf16[1,64,384]{2,1,0:T(8,128)(2,1)S(1)}, bf16[1,64,384]{2,1,0:T(8,128)(2,1)S(1)}, u32[]{:S(2)}, u32[]{:S(2)}) collective-permute-start(bf16[1,64,384]{2,1,0:T(8,128)(2,1)S(1)} %get-tuple-element.27), channel_id=1, source_target_pairs={{0,1},{1,0},{2,3},{3,2},{4,5},{5,4},{6,7},{7,6},{8,9},{9,8},{10,11... | collective-permute-start | bytes 147464 | tf_op jit(solution)/shard_map/ppermute | solution.py:501
  9.3 6.9 %collective-permute-start.1 = (bf16[1,64,384]{2,1,0:T(8,128)(2,1)S(1)}, bf16[1,64,384]{2,1,0:T(8,128)(2,1)S(1)}, u32[]{:S(2)}, u32[]{:S(2)}) collective-permute-start(bf16[1,64,384]{2,1,0:T(8,128)(2,1)S(1)} %get-tuple-element.28), channel_id=1, source_target_pairs={{0,7},{1,2},{2,1},{3,4},{4,3},{5,6},{6,5},{7,0},{8,15},{9,10},{10,... | collective-permute-start | bytes 147464 | tf_op jit(solution)/shard_map/ppermute | solution.py:501
  27.9 11.1 %copy-start.1 = (bf16[1,64,6,384]{3,1,2,0:T(8,128)(2,1)S(1)}, bf16[1,64,6,384]{3,1,2,0:T(8,128)(2,1)}, u32[]{:S(2)}) copy-start(bf16[1,64,6,384]{3,1,2,0:T(8,128)(2,1)} %param.6) | copy-start | bytes 884740
  53.3 48.4 %copy-start.3 = (f32[2,64,1728]{2,1,0:T(8,128)S(1)}, f32[2,64,1728]{2,1,0:T(8,128)}, u32[]{:S(2)}) copy-start(f32[2,64,1728]{2,1,0:T(8,128)} %param.8) | copy-start | bytes 2654212
  53.3 48.4 %copy-start.4 = (f32[2,64,1728]{2,1,0:T(8,128)S(1)}, f32[2,64,1728]{2,1,0:T(8,128)}, u32[]{:S(2)}) copy-start(f32[2,64,1728]{2,1,0:T(8,128)} %param.9) | copy-start | bytes 2654212
